TPU v7x, 32 devices: a whole 2x2x4 slice. The times are simulated.
32 devices in a mesh: dp: 8 (over z, core), seq: 4 (over y, x).
Axes of the slice: x: 2, y: 2, z: 4, core: 2. Of those that a mesh axis runs over, the one named last changes fastest.
Arguments:
- latents: bfloat16 [16, 2048, 1152], P('dp', 'seq'), may hold values from -60 to 60, as said below
- cond: bfloat16 [16, 1152], P('dp'), may hold values from -6 to 6
- w_ada: bfloat16 [1152, 6912], P('dp'), may hold values from -0.1875 to 0.1875
- w_qkv: bfloat16 [1152, 3456], P('dp'), may hold values from -1 to 1
- w_proj: bfloat16 [1152, 1152], P('dp'), may hold values from -3 to 3
- w_fc1: bfloat16 [1152, 4608], P('dp'), may hold values from -0.1875 to 0.1875
- w_fc2: bfloat16 [4608, 1152], P('dp'), may hold values from -0.09375 to 0.09375
- cotangent: bfloat16 [16, 2048, 1152], P('dp', 'seq'), may hold values from -6 to 6
Outputs:
- mixed: float32 [16, 2048, 1152], P('dp', 'seq')
- grad_latents: float32 [16, 2048, 1152], P('dp', 'seq')
- grad_cond: float32 [16, 1152], P('dp')
- grad_ada: float32 [1152, 6912], P('dp')
- grad_qkv: float32 [1152, 3456], P('dp')
- grad_proj: float32 [1152, 1152], P('dp')
- grad_fc1: float32 [1152, 4608], P('dp')
- grad_fc2: float32 [4608, 1152], P('dp')
Inputs may be any that keep to these rules, and one draw needn't show every extreme that they name: latents of order one, with per-token and per-feature scales.
All inputs are finite; a program needn't handle non-finite values.
Results may differ from a plain program's by a relative error of at most 0.011.
The roundings to bfloat16 on the way count: a program that leaves them out, or rounds other values in their place, can miss the bound.
Values may be sent and summed in bfloat16 or wider, within the bound.
No kernel may reach another device: no remote copies, remote signals or barrier semaphores. Data moves between devices by JAX's collectives and lax.ppermute only.
A program may use at most 320 MiB of HBM per device.

v0:
```python
import math

import jax
import jax.numpy as jnp
from jax import lax
from jax.sharding import PartitionSpec as P

HEADS = 16


norm_eps = 1e-06
gelu_coeff = 0.044715


def normalize(values):
    centre = jnp.mean(values, axis=-1, keepdims=True)
    centred = values - centre
    variance = jnp.mean(centred * centred, axis=-1, keepdims=True)
    inv_std = lax.rsqrt(variance + norm_eps)
    return (centred * inv_std, inv_std)


def norm_back(grad_hat, scaled, inv_std):
    mean_grad = jnp.mean(grad_hat, axis=-1, keepdims=True)
    mean_cross = jnp.mean(grad_hat * scaled, axis=-1, keepdims=True)
    return (grad_hat - mean_grad - scaled * mean_cross) * inv_std


def over_rows(former, latter):
    return lax.dot_general(
        former, latter, (((0,), (0,)), ((), ())), preferred_element_type=jnp.float32
    )


def against(former, latter):
    return lax.dot_general(
        former, latter, (((1,), (1,)), ((), ())), preferred_element_type=jnp.float32
    )


def gelu_parts(hidden_pre):
    factor = math.sqrt(2.0 / math.pi)
    tangent = jnp.tanh(factor * (hidden_pre + gelu_coeff * hidden_pre**3))
    gelu_value = 0.5 * hidden_pre * (1.0 + tangent)
    gelu_slope = 0.5 * (1.0 + tangent) + 0.5 * hidden_pre * (1.0 - tangent * tangent) * factor * (
        1.0 + 3.0 * gelu_coeff * hidden_pre * hidden_pre
    )
    return (gelu_value, gelu_slope)


def attend(queries, keys_all, values_all, head_count):
    images_here, length_all, local_width = queries.shape
    head_size = local_width // head_count
    block_rows = min(512, length_all)
    block_count = length_all // block_rows
    score_scale = 1.0 / math.sqrt(head_size)
    query_blocks = queries.reshape(images_here, block_count, block_rows, head_count, head_size)
    keys_split = keys_all.reshape(images_here, length_all, head_count, head_size)
    values_split = values_all.reshape(images_here, length_all, head_count, head_size)

    def one_block(position):
        query_block = lax.dynamic_index_in_dim(query_blocks, position, 1, keepdims=False)
        scores = (
            jnp.einsum(
                "bqhd,bkhd->bhqk", query_block, keys_split, preferred_element_type=jnp.float32
            )
            * score_scale
        )
        top_score = jnp.max(scores, axis=-1, keepdims=True)
        exponent = jnp.exp(scores - top_score)
        row_total = jnp.sum(exponent, axis=-1, keepdims=True)
        weights = (exponent / row_total).astype(jnp.bfloat16)
        block_out = jnp.einsum(
            "bhqk,bkhd->bqhd", weights, values_split, preferred_element_type=jnp.float32
        )
        log_total = (top_score + jnp.log(row_total))[..., 0]
        return (block_out.astype(jnp.bfloat16), log_total)

    blocks_out, log_totals = lax.map(one_block, jnp.arange(block_count))
    attended = jnp.moveaxis(blocks_out, 0, 1).reshape(images_here, length_all, local_width)
    return (attended, log_totals)


def attend_back(queries, keys_all, values_all, log_totals, grad_attended, head_count):
    images_here, length_all, local_width = queries.shape
    head_size = local_width // head_count
    block_rows = min(512, length_all)
    block_count = length_all // block_rows
    score_scale = 1.0 / math.sqrt(head_size)
    query_blocks = queries.reshape(images_here, block_count, block_rows, head_count, head_size)
    grad_blocks = grad_attended.reshape(images_here, block_count, block_rows, head_count, head_size)
    keys_split = keys_all.reshape(images_here, length_all, head_count, head_size)
    values_split = values_all.reshape(images_here, length_all, head_count, head_size)

    def one_block(carry, position):
        grad_keys, grad_values = carry
        query_block = lax.dynamic_index_in_dim(query_blocks, position, 1, keepdims=False)
        grad_block = lax.dynamic_index_in_dim(grad_blocks, position, 1, keepdims=False)
        scores = (
            jnp.einsum(
                "bqhd,bkhd->bhqk", query_block, keys_split, preferred_element_type=jnp.float32
            )
            * score_scale
        )
        block_totals = lax.dynamic_index_in_dim(log_totals, position, 0, keepdims=False)
        weights_full = jnp.exp(scores - block_totals[..., None])
        grad_weights = jnp.einsum(
            "bqhd,bkhd->bhqk", grad_block, values_split, preferred_element_type=jnp.float32
        )
        centre = jnp.sum(weights_full * grad_weights, axis=-1, keepdims=True)
        grad_scores = (weights_full * (grad_weights - centre)).astype(jnp.bfloat16)
        grad_query = (
            jnp.einsum(
                "bhqk,bkhd->bqhd", grad_scores, keys_split, preferred_element_type=jnp.float32
            )
            * score_scale
        )
        grad_keys = (
            grad_keys
            + jnp.einsum(
                "bhqk,bqhd->bkhd", grad_scores, query_block, preferred_element_type=jnp.float32
            )
            * score_scale
        )
        grad_values = grad_values + jnp.einsum(
            "bhqk,bqhd->bkhd",
            weights_full.astype(jnp.bfloat16),
            grad_block,
            preferred_element_type=jnp.float32,
        )
        return ((grad_keys, grad_values), grad_query)

    zeros_both = jnp.zeros((images_here, length_all, head_count, head_size), jnp.float32)
    carried, grad_queries = lax.scan(one_block, (zeros_both, zeros_both), jnp.arange(block_count))
    grad_queries = jnp.moveaxis(grad_queries, 0, 1).reshape(images_here, length_all, local_width)
    grad_keys = carried[0].reshape(images_here, length_all, local_width)
    grad_values = carried[1].reshape(images_here, length_all, local_width)
    return jnp.stack([grad_queries, grad_keys, grad_values], axis=2).astype(jnp.bfloat16)


def per_device(latents, cond, w_ada, w_qkv, w_proj, w_fc1, w_fc2, cotangent):
    head_count = HEADS // lax.axis_size("seq")
    images_here, tokens_here, model_width = latents.shape
    flat_rows = images_here * tokens_here
    gathered = (
        lax.all_gather(w_ada, "dp", axis=0, tiled=True),
        lax.all_gather(w_qkv, "dp", axis=0, tiled=True),
        lax.all_gather(w_proj, "dp", axis=0, tiled=True),
        lax.all_gather(w_fc1, "dp", axis=0, tiled=True),
        lax.all_gather(w_fc2, "dp", axis=0, tiled=True),
    )
    ada_full, qkv_full, proj_full, fc1_full, fc2_full = gathered
    cond_full = cond.astype(jnp.float32)
    logistic = jax.nn.sigmoid(cond_full)
    shrunk = (cond_full * logistic).astype(jnp.bfloat16)
    modulation = jnp.dot(shrunk, ada_full, preferred_element_type=jnp.float32)
    mod_parts = jnp.split(modulation, 6, axis=1)
    shift_one, scale_one, gate_one, shift_two, scale_two, gate_two = [
        piece[:, None, :] for piece in mod_parts
    ]
    latent_full = latents.astype(jnp.float32)
    hat_one, inv_one = normalize(latent_full)
    normed_one = (
        (hat_one * (1.0 + scale_one) + shift_one)
        .astype(jnp.bfloat16)
        .reshape(flat_rows, model_width)
    )
    projected = jnp.dot(normed_one, qkv_full, preferred_element_type=jnp.float32).astype(
        jnp.bfloat16
    )
    projected = projected.reshape(images_here, tokens_here, 3, model_width)
    head_packed = lax.all_to_all(projected, "seq", split_axis=3, concat_axis=1, tiled=True)
    query_heads = head_packed[:, :, 0]
    key_heads = head_packed[:, :, 1]
    value_heads = head_packed[:, :, 2]
    attended_heads, log_totals = attend(query_heads, key_heads, value_heads, head_count)
    attended = lax.all_to_all(
        attended_heads, "seq", split_axis=1, concat_axis=2, tiled=True
    ).reshape(flat_rows, model_width)
    branch_one = jnp.dot(attended, proj_full, preferred_element_type=jnp.float32).reshape(
        images_here, tokens_here, model_width
    )
    residual = latent_full + gate_one * branch_one
    hat_two, inv_two = normalize(residual)
    normed_two = (
        (hat_two * (1.0 + scale_two) + shift_two)
        .astype(jnp.bfloat16)
        .reshape(flat_rows, model_width)
    )
    hidden_pre = jnp.dot(normed_two, fc1_full, preferred_element_type=jnp.float32)
    gelu_value, gelu_slope = gelu_parts(hidden_pre)
    hidden_act = gelu_value.astype(jnp.bfloat16)
    branch_two = jnp.dot(hidden_act, fc2_full, preferred_element_type=jnp.float32).reshape(
        images_here, tokens_here, model_width
    )
    mixed = residual + gate_two * branch_two
    again = (
        lax.all_gather(w_ada, "dp", axis=0, tiled=True),
        lax.all_gather(w_qkv, "dp", axis=0, tiled=True),
        lax.all_gather(w_proj, "dp", axis=0, tiled=True),
        lax.all_gather(w_fc1, "dp", axis=0, tiled=True),
        lax.all_gather(w_fc2, "dp", axis=0, tiled=True),
    )
    ada_back, qkv_back, proj_back, fc1_back, fc2_back = again
    grad_out = cotangent.astype(jnp.float32)
    grad_gate_two = jnp.sum(grad_out * branch_two, axis=1)
    grad_branch_two = (grad_out * gate_two).astype(jnp.bfloat16).reshape(flat_rows, model_width)
    grad_fc2 = over_rows(hidden_act, grad_branch_two)
    grad_act = against(grad_branch_two, fc2_back)
    grad_pre = (grad_act * gelu_slope).astype(jnp.bfloat16)
    grad_fc1 = over_rows(normed_two, grad_pre)
    grad_normed_two = against(grad_pre, fc1_back).reshape(images_here, tokens_here, model_width)
    grad_shift_two = jnp.sum(grad_normed_two, axis=1)
    grad_scale_two = jnp.sum(grad_normed_two * hat_two, axis=1)
    grad_residual = grad_out + norm_back(grad_normed_two * (1.0 + scale_two), hat_two, inv_two)
    grad_gate_one = jnp.sum(grad_residual * branch_one, axis=1)
    grad_branch_one = (
        (grad_residual * gate_one).astype(jnp.bfloat16).reshape(flat_rows, model_width)
    )
    grad_proj = over_rows(attended, grad_branch_one)
    grad_attended = (
        against(grad_branch_one, proj_back)
        .astype(jnp.bfloat16)
        .reshape(images_here, tokens_here, model_width)
    )
    grad_heads = lax.all_to_all(grad_attended, "seq", split_axis=2, concat_axis=1, tiled=True)
    grad_packed = attend_back(
        query_heads, key_heads, value_heads, log_totals, grad_heads, head_count
    )
    grad_projected = lax.all_to_all(
        grad_packed, "seq", split_axis=1, concat_axis=3, tiled=True
    ).reshape(flat_rows, 3 * model_width)
    grad_qkv = over_rows(normed_one, grad_projected)
    grad_normed_one = against(grad_projected, qkv_back).reshape(
        images_here, tokens_here, model_width
    )
    grad_shift_one = jnp.sum(grad_normed_one, axis=1)
    grad_scale_one = jnp.sum(grad_normed_one * hat_one, axis=1)
    grad_latents = grad_residual + norm_back(grad_normed_one * (1.0 + scale_one), hat_one, inv_one)
    grad_mod = jnp.concatenate(
        [
            grad_shift_one,
            grad_scale_one,
            grad_gate_one,
            grad_shift_two,
            grad_scale_two,
            grad_gate_two,
        ],
        axis=1,
    )
    grad_ada = lax.dot_general(
        shrunk.astype(jnp.float32),
        grad_mod,
        (((0,), (0,)), ((), ())),
        precision=lax.Precision.HIGHEST,
        preferred_element_type=jnp.float32,
    )
    mod_upper = grad_mod.astype(jnp.bfloat16)
    mod_lower = (grad_mod - mod_upper.astype(jnp.float32)).astype(jnp.bfloat16)
    grad_shrunk = against(mod_upper, ada_back) + against(mod_lower, ada_back)
    cond_term = grad_shrunk * logistic * (1.0 + cond_full * (1.0 - logistic))
    owned = (
        lax.psum_scatter(grad_ada, "dp", scatter_dimension=0, tiled=True),
        lax.psum_scatter(grad_qkv, "dp", scatter_dimension=0, tiled=True),
        lax.psum_scatter(grad_proj, "dp", scatter_dimension=0, tiled=True),
        lax.psum_scatter(grad_fc1, "dp", scatter_dimension=0, tiled=True),
        lax.psum_scatter(grad_fc2, "dp", scatter_dimension=0, tiled=True),
    )
    summed = lax.psum((owned[0], owned[1], owned[2], owned[3], owned[4], cond_term), "seq")
    final_grads = summed[:5]
    grad_cond = summed[5]
    return (
        mixed,
        grad_latents,
        grad_cond,
        final_grads[0],
        final_grads[1],
        final_grads[2],
        final_grads[3],
        final_grads[4],
    )


def solution(mesh):
    in_specs = (
        P("dp", "seq", None),
        P("dp", None),
        P("dp", None),
        P("dp", None),
        P("dp", None),
        P("dp", None),
        P("dp", None),
        P("dp", "seq", None),
    )
    out_specs = (
        P("dp", "seq", None),
        P("dp", "seq", None),
        P("dp", None),
        P("dp", None),
        P("dp", None),
        P("dp", None),
        P("dp", None),
        P("dp", None),
    )
    return jax.shard_map(
        per_device, mesh=mesh, in_specs=in_specs, out_specs=out_specs, check_vma=False
    )
```

profile of v0, /device:TPU:0, one launch (start us, length us, event | category | flops | bytes accessed | tf_op | source)
XLA Modules:
  0.0 2612.7 jit_solution(16569002691764786299)
XLA Ops:
  11.2 145.3 %all-gather.6.cloned.1.call-done = bf16[1152,6912]{1,0:T(8,128)(2,1)} async-done(((bf16[144,6912]{1,0:T(8,128)(2,1)}), bf16[1152,6912]{1,0:T(8,128)(2,1)}) %all-gather.6.cloned.1.call-update) | async-done | bytes 15925264 | tf_op jit(solution)/shard_map/all_gather | solution.py:146
  167.8 67.1 %all-gather.8.cloned.1.call-done = bf16[1152,3456]{1,0:T(8,128)(2,1)} async-done(((bf16[144,3456]{1,0:T(8,128)(2,1)}), bf16[1152,3456]{1,0:T(8,128)(2,1)}) %all-gather.8.cloned.1.call-update) | async-done | bytes 7962640 | tf_op jit(solution)/shard_map/all_gather | solution.py:147
  234.9 15.2 convolution_convert_fusion
  250.1 17.6 reshape.156
  267.7 24.8 copy.50
  298.5 78.4 %all-to-all-done = bf16[2,512,3,1152]{1,0,2,3:T(2,128)(2,1)} async-done(((bf16[2,512,3,1152]{1,0,2,3:T(2,128)(2,1)}), bf16[2,512,3,1152]{1,0,2,3:T(2,128)(2,1)}, u32[]{:S(2)}, u32[]{:S(2)}) %all-to-all-start) | async-done | bytes 7077920 | tf_op jit(solution)/shard_map/all_to_all | solution.py:172
  393.5 199.4 %while.27 = (s32[]{:T(128)}, bf16[4,2,512,4,72]{2,4,3,1,0:T(8,128)(2,1)S(1)}, f32[4,2,4,512]{3,2,1,0:T(4,128)}, s32[4]{0:T(128)S(1)}, bf16[2,4,512,4,72]{2,4,3,0...) while((s32[]{:T(128)}, ...), condition=%wide.region_5.6_spmd, body=%wide.region_2.5_spmd.sunk | while | flops 2491707392 | bytes 106692776 | solution.py:79
  396.0 17.9 multiply_reduce_fusion.8
  413.9 14.2 fusion.138
  428.1 15.2 fusion.139
  446.4 17.8 multiply_reduce_fusion.8
  464.2 14.0 fusion.138
  478.2 14.8 fusion.139
  496.2 17.6 multiply_reduce_fusion.8
  513.8 14.0 fusion.138
  527.8 14.8 fusion.139
  545.8 17.6 multiply_reduce_fusion.8
  563.3 14.0 fusion.138
  577.4 14.8 fusion.139
  597.6 10.7 reshape.157
  608.3 39.7 %all_to_all.63 = bf16[2,2048,288]{2,0,1:T(2,128)(2,1)} all-to-all(bf16[2,2048,288]{2,0,1:T(2,128)(2,1)S(1)} %reshape.157), channel_id=1, replica_groups=mesh['dp'=8,'seq'=4] {'seq'}, dimensions={1} | all-to-all | bytes 4718592 | tf_op jit(solution)/shard_map/all_to_all | solution.py:177
  674.9 19.6 fusion.86
  694.5 27.7 %fusion.42 = bf16[1024,4608]{1,0:T(8,128)(2,1)} fusion(f32[1024,4608]{1,0:T(8,128)} %fusion.86, bf16[1024,1152]{1,0:T(8,128)(2,1)} %bitcast.206, bf16[4608,1152]{1,0:T(8,128)(2,1)} %all-gather.14.cloned.1.call-done), kind=kOutput, calls=%fused_computation.52 | convolution fusion | flops 10961289216 | bytes 41287680 | tf_op jit(solution)/shard_map/dot_general | solution.py:36
  722.2 19.5 fusion.61
  749.0 24.0 fusion.82
  808.4 18.1 all-to-all-done.2
  829.9 438.2 %while.28 = (s32[]{:T(128)}, f32[2,2048,4,72]{1,3,2,0:T(8,128)}, f32[2,2048,4,72]{1,3,2,0:T(8,128)}, bf16[4,2,512,4,72]{2,4,3,1,0:T(8,128)(2,1)}, s32[4]{0:T(128...) while((s32[]{:T(128)}, f32[2,2048,4,72]{1,3,2,0:T(8,128)}, ...), condition=%wide.region_12.13_spmd.clone, body=%wide.region_10.12_spmd.clone.sunk | while | flops 6146650112 | bytes 348373216 | solution.py:134
  833.6 17.9 fusion.149
  851.4 16.5 bitcast_add_fusion.5
  868.0 24.2 multiply_reduce_fusion.9
  892.2 27.9 %multiply_convert_fusion.6 = bf16[2,4,512,2048]{3,2,1,0:T(8,128)(2,1)} fusion(f32[2,4,512,2048]{3,2,1,0:T(8,128)} %get-tuple-element.370, f32[2,4,512,2048]{3,2,1,0:T(8,128)} %fusion.149, f32[2,4,512]{2,1,0:T(4,128)S(1)} %get-tuple-element.371, f32[2,4,512]{2,1,0:T(4,128)S(1)} %dynamic-slice_bitcast_fusion.2), kind=kLoop, calls=%fused_computation.14.clone.1 | loop fusion | flops 41943040 | bytes 83918848 | tf_op jit(solution)/shard_map/while/body/eval_jaxpr/convert_element_type | solution.py:111
  920.1 10.4 fusion.150
  941.4 17.5 fusion.149
  958.8 17.6 bitcast_add_fusion.5
  976.5 24.2 multiply_reduce_fusion.9
  1000.7 27.9 %multiply_convert_fusion.6 = bf16[2,4,512,2048]{3,2,1,0:T(8,128)(2,1)} fusion(f32[2,4,512,2048]{3,2,1,0:T(8,128)} %get-tuple-element.370, f32[2,4,512,2048]{3,2,1,0:T(8,128)} %fusion.149, f32[2,4,512]{2,1,0:T(4,128)S(1)} %get-tuple-element.371, f32[2,4,512]{2,1,0:T(4,128)S(1)} %dynamic-slice_bitcast_fusion.2), kind=kLoop, calls=%fused_computation.14.clone.1 | loop fusion | flops 41943040 | bytes 83918848 | tf_op jit(solution)/shard_map/while/body/eval_jaxpr/convert_element_type | solution.py:111
  1028.6 10.4 fusion.150
  1051.3 17.5 fusion.149
  1068.8 17.6 bitcast_add_fusion.5
  1086.4 24.2 multiply_reduce_fusion.9
  1110.7 27.9 %multiply_convert_fusion.6 = bf16[2,4,512,2048]{3,2,1,0:T(8,128)(2,1)} fusion(f32[2,4,512,2048]{3,2,1,0:T(8,128)} %get-tuple-element.370, f32[2,4,512,2048]{3,2,1,0:T(8,128)} %fusion.149, f32[2,4,512]{2,1,0:T(4,128)S(1)} %get-tuple-element.371, f32[2,4,512]{2,1,0:T(4,128)S(1)} %dynamic-slice_bitcast_fusion.2), kind=kLoop, calls=%fused_computation.14.clone.1 | loop fusion | flops 41943040 | bytes 83918848 | tf_op jit(solution)/shard_map/while/body/eval_jaxpr/convert_element_type | solution.py:111
  1138.6 10.4 fusion.150
  1161.3 17.5 fusion.149
  1178.8 17.6 bitcast_add_fusion.5
  1196.4 24.2 multiply_reduce_fusion.9
  1220.6 27.9 %multiply_convert_fusion.6 = bf16[2,4,512,2048]{3,2,1,0:T(8,128)(2,1)} fusion(f32[2,4,512,2048]{3,2,1,0:T(8,128)} %get-tuple-element.370, f32[2,4,512,2048]{3,2,1,0:T(8,128)} %fusion.149, f32[2,4,512]{2,1,0:T(4,128)S(1)} %get-tuple-element.371, f32[2,4,512]{2,1,0:T(4,128)S(1)} %dynamic-slice_bitcast_fusion.2), kind=kLoop, calls=%fused_computation.14.clone.1 | loop fusion | flops 41943040 | bytes 83918848 | tf_op jit(solution)/shard_map/while/body/eval_jaxpr/convert_element_type | solution.py:111
  1248.5 10.3 fusion.150
  1285.4 23.5 copy.64
  1308.9 111.6 %all_to_all.64 = bf16[2,2048,3,288]{3,0,2,1:T(2,128)(2,1)} all-to-all(bf16[2,2048,3,288]{3,0,2,1:T(2,128)(2,1)} %copy.64), channel_id=1, replica_groups=mesh['dp'=8,'seq'=4] {'seq'}, dimensions={1} | all-to-all | bytes 14155776 | tf_op jit(solution)/shard_map/all_to_all | solution.py:230
  1420.5 24.8 copy.76
  1445.3 10.9 copy.68
  1458.5 13.9 fusion.87
  1474.0 23.5 fusion.81
  1499.2 18.1 fusion.89
  1522.3 16.2 fusion.57
  1538.6 17.1 fusion.75
  1556.0 73.9 %reduce-scatter.8.cloned.1.call-done = f32[144,3456]{1,0:T(8,128)} async-done(((f32[1152,3456]{1,0:T(8,128)}), f32[144,3456]{1,0:T(8,128)}) %reduce-scatter.8.cloned.1.call-update) | async-done | bytes 1990672 | tf_op jit(solution)/shard_map/reduce_scatter | solution.py:264
  1629.9 211.0 %reduce-scatter.14.cloned.1.call-done = f32[576,1152]{1,0:T(8,128)} async-done(((f32[4608,1152]{1,0:T(8,128)}), f32[576,1152]{1,0:T(8,128)}) %reduce-scatter.14.cloned.1.call-update) | async-done | bytes 2654224 | tf_op jit(solution)/shard_map/reduce_scatter | solution.py:267
  1840.9 211.0 %reduce-scatter.12.cloned.1.call-done = f32[144,4608]{1,0:T(8,128)} async-done(((f32[1152,4608]{1,0:T(8,128)}), f32[144,4608]{1,0:T(8,128)}) %reduce-scatter.12.cloned.1.call-update) | async-done | bytes 2654224 | tf_op jit(solution)/shard_map/reduce_scatter | solution.py:266
  2051.8 311.3 %reduce-scatter.6.cloned.1.call-done = f32[144,6912]{1,0:T(8,128)} async-done(((f32[1152,6912]{1,0:T(8,128)}), f32[144,6912]{1,0:T(8,128)}) %reduce-scatter.6.cloned.1.call-update) | async-done | bytes 3981328 | tf_op jit(solution)/shard_map/reduce_scatter | solution.py:263
  2363.1 9.7 fusion.68
  2372.8 9.8 fusion.66
  2382.6 11.9 psum.42
  2400.9 195.5 %all-reduce.3.cloned.1.call-done = (f32[144,6912]{1,0:T(8,128)}, f32[144,3456]{1,0:T(8,128)}, f32[144,1152]{1,0:T(8,128)}, f32[144,4608]{1,0:T(8,128)}, f32[576,1152]{1,0:T(8,128)}) async-done(((f32[144,6912]{1,0:T(8,128)}, f32[144,3456]{1,0:T(8,128)}, f32[144,1152]{1,0:T(8,128)}, f32[144,4608]{1,0:T(8,128)}, f32[576,1152]{1,0:T(8,128)}), (f32[144,6912]{1,0:T(8,128)}, f32[144,3456]{1,0:T(8,128)}, ...) | async-done | bytes 11943952 | tf_op jit(solution)/shard_map/psum | solution.py:269
  (207 shorter events, 204.5 us)
Async XLA Ops:
  7.2 2.8 copy-start.4
  7.2 149.3 %copy-start.27 = (bf16[2,1152]{1,0:T(2,128)(2,1)S(1)}, bf16[2,1152]{1,0:T(2,128)(2,1)}, u32[]{:S(2)}) copy-start(bf16[2,1152]{1,0:T(2,128)(2,1)} %param.13) | copy-start | bytes 13828
  7.2 149.3 %all-gather.6.cloned.1.call-start = ((), (), s32[]{:S(2)}) async-start(), calls=%async_computation.9 | async-start | bytes 17915904 | tf_op jit(solution)/shard_map/all_gather | solution.py:146
  7.9 227.0 %all-gather.8.cloned.1.call-start = ((), (), s32[]{:S(2)}) async-start(), calls=%async_computation.10 | async-start | bytes 8957952 | tf_op jit(solution)/shard_map/all_gather | solution.py:147
  8.7 652.0 %all-gather.10.cloned.1.call-start = ((), (), s32[]{:S(2)}) async-start(), calls=%async_computation.11 | async-start | bytes 2985984 | tf_op jit(solution)/shard_map/all_gather | solution.py:148
  9.4 665.5 %all-gather.12.cloned.1.call-start = ((), (), s32[]{:S(2)}) async-start(), calls=%async_computation.12 | async-start | bytes 11943936 | tf_op jit(solution)/shard_map/all_gather | solution.py:149
  10.4 154.4 %copy-start.25 = (f32[2,512]{1,0:T(2,128)}, f32[2,512]{1,0:T(2,128)S(1)}, u32[]{:S(2)}) copy-start(f32[2,512]{1,0:T(2,128)S(1)} %broadcast_multiply_fusion.5) | copy-start | bytes 12292
  11.2 153.7 %copy-start.36 = (f32[2,512]{1,0:T(2,128)}, f32[2,512]{1,0:T(2,128)S(1)}, u32[]{:S(2)}) copy-start(f32[2,512]{1,0:T(2,128)S(1)} %add_rsqrt_fusion.1) | copy-start | bytes 12292
  164.8 0.6 copy-start.23
  292.5 84.4 %all-to-all-start = ((bf16[2,512,3,1152]{1,0,2,3:T(2,128)(2,1)}), bf16[2,512,3,1152]{1,0,2,3:T(2,128)(2,1)}, u32[]{:S(2)}, u32[]{:S(2)}) async-start(bf16[2,512,3,1152]{1,0,2,3:T(2,128)(2,1)} %copy.50), calls=%async_computation | async-start | bytes 14155776 | tf_op jit(solution)/shard_map/all_to_all | solution.py:172
  297.9 396.7 %all-gather.14.cloned.1.call-start = ((), (), s32[]{:S(2)}) async-start(), calls=%async_computation.13 | async-start | bytes 11943936 | tf_op jit(solution)/shard_map/all_gather | solution.py:150
  389.7 3.8 copy-start.15
  648.0 12.7 copy-start.5
  648.0 12.7 copy-start.30
  669.2 2.4 copy-start.2
  669.2 3.4 copy-start.8
  669.2 3.4 copy-start.20
  669.2 3.4 copy-start.21
  669.2 3.4 copy-start.29
  674.9 19.6 copy-start.12
  741.7 31.3 %slice-start = ((s8[4718592]{0:T(1024)(128)(4,1)}), s8[4194304]{0:T(1024)(128)(4,1)S(1)}, s32[]{:S(2)}) async-start(s8[4718592]{0:T(1024)(128)(4,1)} %bitcast.183), calls=%async_computation.20 | async-start | bytes 8388608
  741.7 31.3 %slice-start.2 = ((s8[4718592]{0:T(1024)(128)(4,1)}), s8[4194304]{0:T(1024)(128)(4,1)S(1)}, s32[]{:S(2)}) async-start(s8[4718592]{0:T(1024)(128)(4,1)} %bitcast.188), calls=%async_computation.22 | async-start | bytes 8388608
  741.7 31.3 %slice-start.4 = ((s8[4718592]{0:T(1024)(128)(4,1)}), s8[4194304]{0:T(1024)(128)(4,1)S(1)}, s32[]{:S(2)}) async-start(s8[4718592]{0:T(1024)(128)(4,1)} %bitcast.202), calls=%async_computation.24 | async-start | bytes 8388608
  749.0 24.1 slice-start.1
  749.0 24.1 slice-start.3
  749.0 24.1 copy-start.9
  749.0 24.1 slice-start.5
  749.0 24.1 copy-start.22
  773.1 7.1 copy-start.31
  780.2 8.5 copy-start.3
  780.2 3.7 copy-start.38
  780.7 8.1 copy-start.16
  788.7 11.5 copy-start.7
  795.7 30.8 %all-to-all-start.2 = ((bf16[2,512,1152]{1,0,2:T(2,128)(2,1)}), bf16[2,512,1152]{1,0,2:T(2,128)(2,1)}, u32[]{:S(2)}, u32[]{:S(2)}) async-start(bf16[2,512,1152]{1,0,2:T(2,128)(2,1)} %copy.59), calls=%async_computation.2 | async-start | bytes 4718592 | tf_op jit(solution)/shard_map/all_to_all | solution.py:226
  800.2 755.8 %reduce-scatter.10.cloned.1.call-start = ((), (), s32[]{:S(2)}) async-start(), calls=%async_computation.16 | async-start | bytes 5971968 | tf_op jit(solution)/shard_map/reduce_scatter | solution.py:265
  800.3 3.1 copy-start.17
  808.3 821.6 %reduce-scatter.8.cloned.1.call-start = ((), (), s32[]{:S(2)}) async-start(), calls=%async_computation.15 | async-start | bytes 17915904 | tf_op jit(solution)/shard_map/reduce_scatter | solution.py:264
  920.1 11.4 copy-start
  1028.6 11.4 copy-start
  1138.6 11.4 copy-start
  1248.5 11.4 copy-start
  1277.8 3.8 copy-start.1
  1472.4 1.7 copy-start.14
  1472.4 368.5 %reduce-scatter.14.cloned.1.call-start = ((), (), s32[]{:S(2)}) async-start(), calls=%async_computation.18 | async-start | bytes 23887872 | tf_op jit(solution)/shard_map/reduce_scatter | solution.py:267
  1497.5 1.7 copy-start.13
  1497.5 554.3 %reduce-scatter.12.cloned.1.call-start = ((), (), s32[]{:S(2)}) async-start(), calls=%async_computation.17 | async-start | bytes 23887872 | tf_op jit(solution)/shard_map/reduce_scatter | solution.py:266
  1517.3 4.9 copy-start.6
  1517.3 4.9 copy-start.24
  1517.3 4.9 copy-start.26
  1517.3 4.9 copy-start.37
  1517.4 845.7 %reduce-scatter.6.cloned.1.call-start = ((), (), s32[]{:S(2)}) async-start(), calls=%async_computation.14 | async-start | bytes 35831808 | tf_op jit(solution)/shard_map/reduce_scatter | solution.py:263
  1522.2 16.3 copy-start.35
  1522.3 16.3 copy-start.33
  1522.3 16.3 copy-start.32
  1522.3 16.3 copy-start.34
  1522.3 16.3 copy-start.28
  1555.8 1040.6 %all-reduce.3.cloned.1.call-start = ((), (), s32[]{:S(2)}) async-start(), calls=%async_computation.19 | async-start | bytes 23887872 | tf_op jit(solution)/shard_map/psum | solution.py:269
  2596.4 4.5 copy-start.18
  2596.4 5.8 copy-start.19
  2596.4 6.6 copy-start.11
  2600.9 3.6 copy-start.10
Sparse Core Ops, SparseCore 0:
  9.6 146.8 all-gather.5
  158.1 76.6 all-gather.7
  236.5 32.4 all-gather.9
  270.6 99.5 all-gather.11
  371.7 98.7 all-gather.13
  808.4 59.0 reduce-scatter.9
  1472.5 157.3 reduce-scatter.7
  1632.3 208.5 reduce-scatter.13
  1843.2 208.5 reduce-scatter.11
  2054.0 308.9 reduce-scatter.5
  2367.5 228.8 all-reduce.2
where the time goes:
time: 2630 us; the launch traced here: 2610 us
  waiting for transfers between devices  1310 us (50%)
  matrix products  679 us (26%)
  local copies, waits for them, and re-layouts  209 us (8%)
  other arithmetic  205 us (8%)
  blocking collectives  163 us (6%)
    reduce_scatter x1, waiting for transfers between devices, per_device(): lax.psum_scatter(grad_ada, 'dp', scatter_dimension=0, tiled=True)  311 us
    reduce_scatter x1, waiting for transfers between devices, per_device(): lax.psum_scatter(grad_fc1, 'dp', scatter_dimension=0, tiled=True)  211 us
    reduce_scatter x1, waiting for transfers between devices, per_device(): lax.psum_scatter(grad_fc2, 'dp', scatter_dimension=0, tiled=True)  211 us
    psum x1, waiting for transfers between devices, per_device(): lax.psum((owned[0], owned[1], owned[2], owned[3], owned[4], cond_term), '...  195 us
    all_gather x1, waiting for transfers between devices, per_device(): lax.all_gather(w_ada, 'dp', axis=0, tiled=True)  145 us
    dot_general x8, matrix products, one_block(): jnp.einsum('bqhd,bkhd->bhqk', query_block, keys_split, preferred_element_...  141 us
    convert_element_type x4, other arithmetic, one_block(): grad_scores = (weights_full * (grad_weights - centre)).astype(jnp.bfloat16)  112 us
    all_to_all x1, blocking collectives, per_device(): lax.all_to_all(grad_packed, 'seq', split_axis=1, concat_axis=3, tiled=True)  112 us
  transfers between devices with their start and end apart: 13, of which 9 were waited for; matrix products, arithmetic and copies ran while one was open for 37% of the time, Pallas kernels for 0%

commit v1 on v0

v1 whole, which is shorter than its diff:
```python
import functools
import math

import jax
import jax.numpy as jnp
from jax import lax
from jax.experimental import pallas as pl
from jax.experimental.pallas import tpu as pltpu
from jax.sharding import PartitionSpec as P

HEADS = 16
IMAGE_GROUPS = 2

norm_eps = 1e-06
gelu_coeff = 0.044715
log2_e = math.log2(math.e)
half = jnp.bfloat16
full = jnp.float32


def normalize(values):
    centre = jnp.mean(values, axis=-1, keepdims=True)
    centred = values - centre
    variance = jnp.mean(centred * centred, axis=-1, keepdims=True)
    inv_std = lax.rsqrt(variance + norm_eps)
    return (centred * inv_std, inv_std)


def norm_back(grad_hat, scaled, inv_std):
    mean_grad = jnp.mean(grad_hat, axis=-1, keepdims=True)
    mean_cross = jnp.mean(grad_hat * scaled, axis=-1, keepdims=True)
    return (grad_hat - mean_grad - scaled * mean_cross) * inv_std


def dot(former, latter, former_dim, latter_dim):
    return lax.dot_general(
        former, latter, (((former_dim,), (latter_dim,)), ((), ())), preferred_element_type=full
    )


def gelu_parts(hidden_pre):
    factor = math.sqrt(2.0 / math.pi)
    tangent = jnp.tanh(factor * (hidden_pre + gelu_coeff * hidden_pre**3))
    gelu_value = 0.5 * hidden_pre * (1.0 + tangent)
    gelu_slope = 0.5 * (1.0 + tangent) + 0.5 * hidden_pre * (1.0 - tangent * tangent) * factor * (
        1.0 + 3.0 * gelu_coeff * hidden_pre * hidden_pre
    )
    return (gelu_value, gelu_slope)


def split_two(values):
    upper = values.astype(half)
    return upper, (values - upper.astype(full)).astype(half)


def forward_kernel(rows, chunk, q_ref, k_ref, v_ref, o_ref, l_ref, twice_ref, score_ref):
    features, length = k_ref.shape[1:]
    factor = log2_e / math.sqrt(features)
    keys = k_ref[0]
    twice_ref[...] = jnp.concatenate([keys, keys], axis=0).astype(full).T.astype(half)

    def step(at, carry):
        cols = pl.ds(pl.multiple_of(at * rows, rows), rows)
        queries = jnp.concatenate(split_two(q_ref[0, :, cols].astype(full) * factor), axis=0)
        top = None
        for low in range(0, length, chunk):
            scores = dot(twice_ref[low : low + chunk, :], queries, 1, 0)
            score_ref[low : low + chunk, :] = scores
            part = jnp.max(scores.reshape(chunk // 8, 8, rows), axis=0)
            top = part if top is None else jnp.maximum(top, part)
        top = jnp.max(top, axis=0, keepdims=True)
        total = None
        mix = None
        for low in range(0, length, chunk):
            exponent = jnp.exp2(score_ref[low : low + chunk, :] - top)
            part = jnp.sum(exponent.reshape(chunk // 8, 8, rows), axis=0)
            total = part if total is None else total + part
            term = dot(v_ref[0, :, low : low + chunk], exponent.astype(half), 1, 0)
            mix = term if mix is None else mix + term
        total = jnp.sum(total, axis=0, keepdims=True)
        o_ref[0, :, cols] = (mix / total).astype(o_ref.dtype)
        l_ref[0, :, cols] = top + jnp.log2(total)
        return carry

    lax.fori_loop(0, length // rows, step, 0)


def block_of(features, length, offset):
    return pl.BlockSpec((1, features, length), lambda head: (head + offset, 0, 0))


def attend(packed):
    triple, features, length = packed.shape
    heads = triple // 3
    rows, chunk = min(1024, length), min(512, length)
    block = functools.partial(block_of, features, length)
    return pl.pallas_call(
        functools.partial(forward_kernel, rows, chunk),
        grid=(heads,),
        out_shape=(
            jax.ShapeDtypeStruct((heads, features, length), half),
            jax.ShapeDtypeStruct((heads, 1, length), full),
        ),
        in_specs=[block(0), block(heads), block(2 * heads)],
        out_specs=(block(0), block_of(1, length, 0)),
        scratch_shapes=[
            pltpu.VMEM((length, 2 * features), half),
            pltpu.VMEM((length, rows), full),
        ],
        compiler_params=pltpu.CompilerParams(vmem_limit_bytes=40 * 2**20),
        cost_estimate=pl.CostEstimate(
            flops=14 * heads * length * length * features,
            bytes_accessed=8 * heads * length * features,
            transcendentals=heads * length * length,
        ),
        name="attend",
    )(packed, packed, packed)


def backward_kernel(
    rows, chunk, q_ref, k_ref, v_ref, g_ref, l_ref, out_ref, k_s, twice_s, dk_s, dv_s, p_s, t_s
):
    features, length = k_ref.shape[1:]
    scale = 1.0 / math.sqrt(features)
    factor = log2_e * scale
    keys = k_ref[0]
    row_id = lax.broadcasted_iota(jnp.int32, (8, length), 0)
    ones = jnp.where(row_id < 3, 1.0, 0.0).astype(half)
    twice_s[...] = jnp.concatenate([keys, keys, ones], axis=0)
    lanes = k_s.shape[1]
    wide = jnp.concatenate([keys.astype(full), jnp.zeros((lanes - features, length), full)], axis=0)
    k_s[...] = wide.T.astype(half)
    dk_s[...] = jnp.zeros_like(dk_s)
    dv_s[...] = jnp.zeros_like(dv_s)

    def step(at, carry):
        cols = pl.ds(pl.multiple_of(at * rows, rows), rows)
        queries = q_ref[0, :, cols]
        grads = g_ref[0, :, cols]
        upper, lower = split_two(queries.astype(full) * factor)
        rest = -l_ref[0, :, cols]
        first = rest.astype(half).astype(full)
        second = (rest - first).astype(half).astype(full)
        third = rest - first - second
        which = lax.broadcasted_iota(jnp.int32, (8, rows), 0)
        extra = jnp.where(
            which == 0, first, jnp.where(which == 1, second, jnp.where(which == 2, third, 0.0))
        ).astype(half)
        wide_queries = jnp.concatenate([upper, lower, extra], axis=0)
        centre = None
        for low in range(0, length, chunk):
            span = slice(low, low + chunk)
            prob = jnp.exp2(dot(wide_queries, twice_s[:, span], 0, 0))
            p_s[:, span] = prob
            both = prob * dot(grads, v_ref[0, :, span], 0, 0)
            t_s[:, span] = both
            for lane in range(0, chunk, 128):
                part = both[:, lane : lane + 128]
                centre = part if centre is None else centre + part
        centre = jnp.sum(centre, axis=1, keepdims=True)
        dq = None
        for low in range(0, length, chunk):
            span = slice(low, low + chunk)
            prob = p_s[:, span]
            dv_s[:, span] += dot(grads, prob.astype(half), 1, 0)
            grad_scores = (t_s[:, span] - prob * centre).astype(half)
            dk_s[:, span] += dot(queries, grad_scores, 1, 0)
            term = dot(grad_scores, k_s[span, :], 1, 0)
            dq = term if dq is None else dq + term
        out_ref[0, 0, :, cols] = (dq * scale).T[:features].astype(half)
        return carry

    lax.fori_loop(0, length // rows, step, 0)
    out_ref[1, 0] = (dk_s[...] * scale).astype(half)
    out_ref[2, 0] = dv_s[...].astype(half)


def attend_back(packed, grads, log_totals):
    triple, features, length = packed.shape
    heads = triple // 3
    rows, chunk = min(512, length), min(256, length)
    lanes = -(-features // 128) * 128
    block = functools.partial(block_of, features, length)
    return pl.pallas_call(
        functools.partial(backward_kernel, rows, chunk),
        grid=(heads,),
        out_shape=jax.ShapeDtypeStruct((3, heads, features, length), half),
        in_specs=[block(0), block(heads), block(2 * heads), block(0), block_of(1, length, 0)],
        out_specs=pl.BlockSpec((3, 1, features, length), lambda head: (0, head, 0, 0)),
        scratch_shapes=[
            pltpu.VMEM((length, lanes), half),
            pltpu.VMEM((2 * features + 8, length), half),
            pltpu.VMEM((features, length), full),
            pltpu.VMEM((features, length), full),
            pltpu.VMEM((rows, length), full),
            pltpu.VMEM((rows, length), full),
        ],
        compiler_params=pltpu.CompilerParams(vmem_limit_bytes=40 * 2**20),
        cost_estimate=pl.CostEstimate(
            flops=28 * heads * length * length * features,
            bytes_accessed=16 * heads * length * features,
            transcendentals=heads * length * length,
        ),
        name="attend_back",
    )(packed, packed, packed, grads, log_totals)


class Exchange:
    def __init__(self):
        self.size = lax.axis_size("seq")
        self.groups = self.size // IMAGE_GROUPS
        index = lax.axis_index("seq")
        self.side = index % IMAGE_GROUPS
        self.group = index // IMAGE_GROUPS

    def across(self, value):
        return lax.ppermute(value, "seq", [(at, at ^ 1) for at in range(self.size)])

    def shift(self, value, by):
        pairs = [
            (2 * group + side, 2 * ((group + by) % self.groups) + side)
            for group in range(self.groups)
            for side in range(2)
        ]
        return lax.ppermute(value, "seq", pairs)

    def total(self, value):
        value = value + self.across(value)
        return value + sum(self.shift(value, by) for by in range(1, self.groups))

    def mine(self, first, second):
        return jnp.where(self.side == 0, first, second)

    def other(self, first, second):
        return jnp.where(self.side == 0, second, first)


def gather_rows(shard):
    return lax.all_gather(shard, "dp", axis=0, tiled=True)


def scatter_rows(term):
    return lax.psum_scatter(term, "dp", scatter_dimension=0, tiled=True)


def per_device(latents, cond, w_ada, w_qkv, w_proj, w_fc1, w_fc2, cotangent):
    ex = Exchange()
    groups = ex.groups
    dp_size = lax.axis_size("dp")
    dp_index = lax.axis_index("dp")
    images_here, tokens_here, width = latents.shape
    flat_rows = images_here * tokens_here
    length = ex.size * tokens_here
    features = width // HEADS
    span = width // groups
    own_heads = HEADS // groups
    ada_rows = w_ada.shape[0]

    cond_all = gather_rows(cond).astype(full)
    logistic_all = jax.nn.sigmoid(cond_all)
    shrunk_all = (cond_all * logistic_all).astype(half)
    shrunk_rows = lax.dynamic_slice_in_dim(shrunk_all, dp_index * ada_rows, ada_rows, 1)
    mod_terms = dot(shrunk_rows, w_ada, 1, 0)
    mod_terms = lax.all_to_all(mod_terms, "dp", split_axis=0, concat_axis=0, tiled=True)
    modulation = jnp.sum(mod_terms.reshape(dp_size, images_here, 6 * width), axis=0)
    shift_one, scale_one, gate_one, shift_two, scale_two, gate_two = [
        piece[:, None, :] for piece in jnp.split(modulation, 6, axis=1)
    ]

    received = ex.across(ex.other(latents[0], latents[1]))
    pair = jnp.concatenate([ex.mine(latents[0], latents[1]), received], axis=0)
    tokens_image = jnp.concatenate([pair] + [ex.shift(pair, by) for by in range(1, groups)], axis=0)

    qkv_cols = lax.dynamic_slice_in_dim(
        w_qkv.reshape(w_qkv.shape[0], 3, width), ex.group * span, span, 2
    ).reshape(w_qkv.shape[0], 3 * span)
    qkv_full = gather_rows(qkv_cols)
    proj_full = gather_rows(w_proj)
    fc1_full = gather_rows(w_fc1)
    fc2_full = gather_rows(w_fc2)

    hat_image, _ = normalize(tokens_image.astype(full))
    normed_image = (
        hat_image * (1.0 + ex.mine(scale_one[0], scale_one[1]))
        + ex.mine(shift_one[0], shift_one[1])
    ).astype(half)
    packed = dot(qkv_full, normed_image, 0, 1).astype(half)
    packed = packed.reshape(3 * own_heads, features, length)
    attended_own, log_totals = attend(packed)
    attended_own = attended_own.reshape(span, groups, 2 * tokens_here)

    attended_pair = jnp.zeros((width, 2 * tokens_here), half)
    for by in range(groups):
        block = attended_own[:, by]
        block = ex.shift(block, -by) if by else block
        start = ((ex.group + by) % groups) * span
        attended_pair = lax.dynamic_update_slice_in_dim(attended_pair, block, start, 0)
    kept, sent = attended_pair[:, :tokens_here], attended_pair[:, tokens_here:]
    received = ex.across(sent)
    attended = jnp.concatenate([ex.mine(kept, received), ex.other(kept, received)], axis=1)

    latent_full = latents.astype(full)
    branch_one = dot(attended, proj_full, 0, 0).reshape(images_here, tokens_here, width)
    residual = latent_full + gate_one * branch_one
    hat_two, inv_two = normalize(residual)
    normed_two = (hat_two * (1.0 + scale_two) + shift_two).astype(half).reshape(flat_rows, width)
    hidden_pre = dot(normed_two, fc1_full, 1, 0)
    gelu_value, gelu_slope = gelu_parts(hidden_pre)
    hidden_act = gelu_value.astype(half)
    branch_two = dot(hidden_act, fc2_full, 1, 0).reshape(images_here, tokens_here, width)
    mixed = residual + gate_two * branch_two

    grad_out = cotangent.astype(full)
    grad_gate_two = jnp.sum(grad_out * branch_two, axis=1)
    grad_branch_two = (grad_out * gate_two).astype(half).reshape(flat_rows, width)
    grad_act = dot(grad_branch_two, fc2_full, 1, 1)
    grad_pre = (grad_act * gelu_slope).astype(half)
    grad_normed_two = dot(grad_pre, fc1_full, 1, 1).reshape(images_here, tokens_here, width)
    grad_shift_two = jnp.sum(grad_normed_two, axis=1)
    grad_scale_two = jnp.sum(grad_normed_two * hat_two, axis=1)
    grad_residual = grad_out + norm_back(grad_normed_two * (1.0 + scale_two), hat_two, inv_two)
    grad_gate_one = jnp.sum(grad_residual * branch_one, axis=1)
    grad_branch_one = (grad_residual * gate_one).astype(half).reshape(flat_rows, width)
    grad_attended = dot(proj_full, grad_branch_one, 1, 1).astype(half)

    first, second = grad_attended[:, :tokens_here], grad_attended[:, tokens_here:]
    received = ex.across(ex.other(first, second))
    grad_pair = jnp.concatenate([ex.mine(first, second), received], axis=1)
    blocks = []
    for by in range(groups):
        start = ((ex.group + by) % groups) * span
        block = lax.dynamic_slice_in_dim(grad_pair, start, span, 0)
        blocks.append(ex.shift(block, by) if by else block)
    grad_heads = jnp.concatenate(blocks, axis=1).reshape(own_heads, features, length)

    grad_fc2 = scatter_rows(dot(hidden_act, grad_branch_two, 0, 0).astype(half))
    grad_fc1 = scatter_rows(dot(normed_two, grad_pre, 0, 0).astype(half))
    grad_proj = scatter_rows(dot(attended, grad_branch_one, 1, 0).astype(half))
    grad_fc2 = lax.psum(grad_fc2.astype(full), "seq")
    grad_fc1 = lax.psum(grad_fc1.astype(full), "seq")
    grad_proj = lax.psum(grad_proj.astype(full), "seq")

    grad_packed = attend_back(packed, grad_heads, log_totals).reshape(3 * span, length)

    grad_qkv = scatter_rows(dot(normed_image, grad_packed, 0, 1).astype(half))
    grad_qkv = lax.all_gather(grad_qkv, "seq", axis=0).astype(full)
    qkv_rows = w_qkv.shape[0]
    grad_qkv = jnp.sum(grad_qkv.reshape(groups, 2, qkv_rows, 3, span), axis=1)
    grad_qkv = jnp.transpose(grad_qkv, (1, 2, 0, 3)).reshape(qkv_rows, 3 * width)

    terms = dot(grad_packed, qkv_full, 0, 1)
    terms = terms.reshape(groups, 2 * tokens_here, width)
    grad_pair_normed = terms[0]
    for by in range(1, groups):
        grad_pair_normed = grad_pair_normed + ex.shift(terms[by].astype(half), -by).astype(full)
    kept = grad_pair_normed[:tokens_here]
    received = ex.across(grad_pair_normed[tokens_here:].astype(half)).astype(full)
    grad_normed_one = jnp.stack([ex.mine(kept, received), ex.other(kept, received)])

    hat_one, inv_one = normalize(latent_full)
    grad_shift_one = jnp.sum(grad_normed_one, axis=1)
    grad_scale_one = jnp.sum(grad_normed_one * hat_one, axis=1)
    grad_latents = grad_residual + norm_back(grad_normed_one * (1.0 + scale_one), hat_one, inv_one)

    late = ex.total(jnp.concatenate([grad_shift_one, grad_scale_one], axis=1))
    early = ex.total(
        jnp.concatenate([grad_gate_one, grad_shift_two, grad_scale_two, grad_gate_two], axis=1)
    )
    shrunk_own = shrunk_rows.astype(full)
    grad_ada = []
    grad_shrunk = 0.0
    for piece, low in ((late, 0), (early, 2 * width)):
        piece = gather_rows(piece)
        grad_ada.append(
            lax.dot_general(
                shrunk_own,
                piece,
                (((0,), (0,)), ((), ())),
                precision=lax.Precision.HIGHEST,
                preferred_element_type=full,
            )
        )
        upper, lower = split_two(piece)
        ada_cols = w_ada[:, low : low + piece.shape[1]]
        grad_shrunk = grad_shrunk + dot(upper, ada_cols, 1, 1) + dot(lower, ada_cols, 1, 1)
    grad_ada = jnp.concatenate(grad_ada, axis=1)
    grad_shrunk = lax.all_to_all(grad_shrunk, "dp", split_axis=0, concat_axis=0, tiled=True)
    grad_shrunk = grad_shrunk.reshape(dp_size, images_here, ada_rows)
    grad_shrunk = jnp.transpose(grad_shrunk, (1, 0, 2)).reshape(images_here, width)
    cond_full = cond.astype(full)
    logistic = jax.nn.sigmoid(cond_full)
    grad_cond = grad_shrunk * logistic * (1.0 + cond_full * (1.0 - logistic))
    return (
        mixed,
        grad_latents,
        grad_cond,
        grad_ada,
        grad_qkv,
        grad_proj,
        grad_fc1,
        grad_fc2,
    )


def solution(mesh):
    tokens = P("dp", "seq", None)
    rows = P("dp", None)
    return jax.shard_map(
        per_device,
        mesh=mesh,
        in_specs=(tokens, rows, rows, rows, rows, rows, rows, tokens),
        out_specs=(tokens, tokens, rows, rows, rows, rows, rows, rows),
        check_vma=False,
    )
```

time: 2630 us -> 1170 us (0.44)
  waiting for transfers between devices: 1310 us -> 344 us
  matrix products: 679 us -> 200 us
  Pallas kernels: 0 us -> 157 us
  other arithmetic: 205 us -> 55.2 us
  local copies, waits for them, and re-layouts: 209 us -> 90.5 us
  blocking collectives: 163 us -> 278 us
    reduce_scatter x5 -> x4, waiting for transfers between devices: 807 us -> 143 us  [scatter_rows(): return lax.psum_scatter(term, 'dp', scatter_dimension=0, tiled=True)]
    dot_general x44 -> x19, matrix products: 679 us -> 200 us  [the longest x17 195 us: dot(): lax.dot_general(former, latter, (((former_dim,), (latter_dim,)), ((), ())...]
    psum x1 -> x0, waiting for transfers between devices: 195 us -> none  [per_device(): lax.psum((owned[0], owned[1], owned[2], owned[3], owned[4], cond_term), '...]
    all_gather x5, waiting for transfers between devices: 212 us -> 17.9 us  [the longest x4 17.9 us: gather_rows(): return lax.all_gather(shard, 'dp', axis=0, tiled=True)]
    psum x1, blocking collectives: 11.9 us -> 200 us  [per_device(): grad_proj = lax.psum(grad_proj.astype(full), 'seq')]
    ppermute x0 -> x12, waiting for transfers between devices: none -> 180 us  [the longest x6 93.7 us: shift(): return lax.ppermute(value, 'seq', pairs)]
    pallas_call x0 -> x2, Pallas kernels: none -> 157 us  [the longest x1 106 us: attend_back(): pl.pallas_call(functools.partial(backward_kernel, rows, chunk), grid=(hea...]
    all_to_all x2 -> x1, blocking collectives: 151 us -> 30.5 us  [per_device(): lax.all_to_all(mod_terms, 'dp', split_axis=0, concat_axis=0, tiled=True)]
  transfers between devices with their start and end apart: 13 -> 22, of which waited for: 9 -> 14; matrix products, arithmetic and copies ran while one was open for 37% -> 18% of each run, Pallas kernels for 0% -> 4%
where the time goes in v1:
time: 1170 us; the launch traced here: 1160 us
  waiting for transfers between devices  344 us (29%)
  blocking collectives  278 us (24%)
  matrix products  200 us (17%)
  Pallas kernels  157 us (13%)
  local copies, waits for them, and re-layouts  90.5 us (8%)
  other arithmetic  55.2 us (5%)
  starting transfers between devices  22.4 us (2%)
  between operations  15 us (1%)
    psum x1, blocking collectives, per_device(): grad_proj = lax.psum(grad_proj.astype(full), 'seq')  200 us
    dot_general x17, matrix products, dot(): lax.dot_general(former, latter, (((former_dim,), (latter_dim,)), ((), ())...  195 us
    reduce_scatter x4, waiting for transfers between devices, scatter_rows(): return lax.psum_scatter(term, 'dp', scatter_dimension=0, tiled=True)  143 us
    pallas_call x1, Pallas kernels, attend_back(): pl.pallas_call(functools.partial(backward_kernel, rows, chunk), grid=(hea...  106 us
    ppermute x6, waiting for transfers between devices, shift(): return lax.ppermute(value, 'seq', pairs)  93.7 us
    ppermute x6, waiting for transfers between devices, across(): return lax.ppermute(value, 'seq', [(at, at ^ 1) for at in range(self.size)])  86.4 us
    pallas_call x1, Pallas kernels, attend(): pl.pallas_call(functools.partial(forward_kernel, rows, chunk), grid=(head...  51.2 us
    all_gather x3, blocking collectives, gather_rows(): return lax.all_gather(shard, 'dp', axis=0, tiled=True)  47 us
  transfers between devices with their start and end apart: 22, of which 14 were waited for; matrix products, arithmetic and copies ran while one was open for 18% of the time, Pallas kernels for 4%

profile of v1, /device:TPU:0, one launch (start us, length us, event | category | flops | bytes accessed | tf_op | source)
XLA Modules:
  0.0 1162.1 jit_solution(2260280883143971921)
XLA Ops:
  7.2 3.3 reshape.162
  10.5 1.9 constant_dynamic-slice_fusion
  16.5 3.0 collective-permute-start
  19.6 26.2 %collective-permute-done = bf16[512,1152]{1,0:T(8,128)(2,1)} collective-permute-done((bf16[512,1152]{1,0:T(8,128)(2,1)}, bf16[512,1152]{1,0:T(8,128)(2,1)}, u32[]{:S(2)}, u32[]{:S(2)}) %collective-permute-start) | collective-permute-done | bytes 1179680 | tf_op jit(solution)/shard_map/ppermute | solution.py:217
  45.8 2.9 pad_maximum_fusion.4
  50.4 14.6 %all-gather.1 = bf16[8,2,1152]{2,1,0:T(2,128)(2,1)S(1)} all-gather(bf16[1,2,1152]{2,1,0:T(2,128)(2,1)S(1)} %bitcast.90), channel_id=1, replica_groups=mesh['dp'=8,'seq'=4] {'dp'}, dimensions={0}, use_global_device_ids=true | all-gather | bytes 41472 | tf_op jit(solution)/shard_map/all_gather | solution.py:239
  67.5 30.5 %all_to_all.18 = f32[8,2,6912]{2,1,0:T(2,128)S(1)} all-to-all(f32[8,2,6912]{2,1,0:T(2,128)S(1)} %all_to_all.12), channel_id=1, replica_groups=mesh['dp'=8,'seq'=4] {'dp'}, dimensions={0} | all-to-all | bytes 884736 | tf_op jit(solution)/shard_map/all_to_all | solution.py:264
  98.2 3.2 collective-permute-done.1
  101.4 2.7 convert_reduce_fusion
  104.1 4.1 fusion.11
  108.3 14.1 %convolution_convert_fusion.3 = bf16[1728,2048]{1,0:T(8,128)(2,1)S(1)} fusion(bf16[1152,1728]{1,0:T(8,128)(2,1)} %all-gather.10.cloned.1.call-done, f32[1152]{0:T(1024)S(1)} %get-tuple-element.20, f32[1152]{0:T(1024)S(1)} %get-tuple-element.19, f32[2048]{0:T(1024)S(1)} %add_rsqrt_fusion, f32[2048]{0:T(1024)S(1)} %broadcast_multiply_fusion, ...), kind=kOutput, calls=%fused_computation.23 | convolution fusion | flops 8183218176 | bytes 15803392 | tf_op jit(solution)/shard_map/dot_general | solution.py:36
  122.5 51.2 %attend.1 = (bf16[8,72,2048]{2,1,0:T(8,128)(2,1)S(1)}, f32[8,1,2048]{2,1,0:T(1,128)S(1)}) custom-call(bf16[24,72,2048]{2,1,0:T(8,128)(2,1)S(1)} %bitcast.65, bf16[24,72,2048]{2,1,0:T(8,128)(2,1)S(1)} %bitcast.66, bf16[24,72,2048]{2,1,0:T(8,128)(2,1)S(1)} %bitcast.67), custom_call_target="tpu_custom_call" | custom-call | flops 33822867456 | bytes 9437184 | tf_op jit(solution)/shard_map/attend/pallas_call | solution.py:97
  173.7 3.1 reshape.165
  176.8 6.4 fusion.72
  186.1 4.5 copy.39
  192.2 12.8 %dynamic_update_slice.6 = bf16[1152,1024]{0,1:T(8,128)(2,1)} dynamic-update-slice(bf16[1152,1024]{0,1:T(8,128)(2,1)} %broadcast_in_dim.2, bf16[576,1024]{0,1:T(8,128)(2,1)} %bitcast.82, s32[]{:T(128)S(6)} %select_n.117, s32[]{:T(128)} %constant.69.clone.1) | dynamic-update-slice | bytes 2359300 | tf_op jit(solution)/shard_map/dynamic_update_slice | solution.py:297
  205.1 6.2 collective-permute-done.2
  211.3 2.4 copy.33
  213.7 13.8 %dynamic_update_slice.7 = bf16[1152,1024]{0,1:T(8,128)(2,1)} dynamic-update-slice(bf16[1152,1024]{0,1:T(8,128)(2,1)} %dynamic_update_slice.6, bf16[576,1024]{0,1:T(8,128)(2,1)} %copy.33, s32[]{:T(128)S(6)} %select_n.119, s32[]{:T(128)} %constant.69.clone.1) | dynamic-update-slice | bytes 2359300 | tf_op jit(solution)/shard_map/dynamic_update_slice | solution.py:297
  231.2 23.3 %collective-permute-done.3 = bf16[1152,512]{0,1:T(8,128)(2,1)S(1)} collective-permute-done((bf16[1152,512]{0,1:T(8,128)(2,1)S(1)}, bf16[1152,512]{0,1:T(8,128)(2,1)S(1)}, u32[]{:S(2)}, u32[]{:S(2)}) %collective-permute-start.3) | collective-permute-done | bytes 1179680 | tf_op jit(solution)/shard_map/ppermute | solution.py:217
  256.2 6.0 fusion.33
  262.2 2.2 fusion.71
  267.8 2.6 fusion.26
  270.3 20.4 %fusion.73 = f32[1024,4608]{1,0:T(8,128)} fusion(bf16[1024,1152]{1,0:T(8,128)(2,1)} %bitcast.85, bf16[1152,4608]{1,0:T(8,128)(2,1)} %all-gather.14.cloned.1.call-done), kind=kOutput, calls=%fused_computation.142 | convolution fusion | flops 10871635968 | bytes 31850496 | tf_op jit(solution)/shard_map/dot_general | solution.py:36
  290.8 17.8 %all-gather.16.cloned.1.call-done = bf16[4608,1152]{1,0:T(8,128)(2,1)} async-done(((bf16[576,1152]{1,0:T(8,128)(2,1)}), bf16[4608,1152]{1,0:T(8,128)(2,1)}) %all-gather.16.cloned.1.call-update) | async-done | bytes 10616848 | tf_op jit(solution)/shard_map/all_gather | solution.py:239
  308.6 25.6 %fusion.8 = bf16[1024,4608]{1,0:T(8,128)(2,1)} fusion(f32[1024,4608]{1,0:T(8,128)} %fusion.73, bf16[1024,1152]{1,0:T(8,128)(2,1)S(1)} %bitcast.83, bf16[4608,1152]{1,0:T(8,128)(2,1)} %all-gather.16.cloned.1.call-done), kind=kOutput, calls=%fused_computation.12 | convolution fusion | flops 10961289216 | bytes 41287680 | tf_op jit(solution)/shard_map/dot_general | solution.py:36
  334.2 19.7 %fusion.28 = (f32[1024]{0:T(1024)S(1)}, f32[1024,1152]{1,0:T(8,128)}) fusion(f32[2,1152]{1,0:T(2,128)S(1)} %get-tuple-element.45, bf16[1024,4608]{1,0:T(8,128)(2,1)} %fusion.8, bf16[1152,4608]{1,0:T(8,128)(2,1)} %all-gather.14.cloned.1.call-done), kind=kOutput, calls=%fused_computation.49 | convolution fusion | flops 10873994240 | bytes 24785920 | tf_op jit(solution)/shard_map/dot_general | solution.py:36
  353.9 7.0 fusion.29
  360.9 24.0 %fusion.70 = f32[1024,1152]{1,0:T(8,128)} fusion(bf16[4608,1152]{1,0:T(8,128)(2,1)} %all-gather.16.cloned.1.call-done, f32[1024,4608]{1,0:T(8,128)} %fusion.73), kind=kOutput, calls=%fused_computation.139 | convolution fusion | flops 10914103296 | bytes 34209792 | tf_op jit(solution)/shard_map/dot_general | solution.py:36
  385.0 7.1 multiply_reduce_fusion
  392.5 3.3 copy-done.48
  395.8 4.0 fusion.30
  401.6 26.7 %collective-permute-done.4 = bf16[1152,512]{0,1:T(8,128)(2,1)S(1)} collective-permute-done((bf16[1152,512]{0,1:T(8,128)(2,1)S(1)}, bf16[1152,512]{0,1:T(8,128)(2,1)S(1)}, u32[]{:S(2)}, u32[]{:S(2)}) %collective-permute-start.4) | collective-permute-done | bytes 1179680 | tf_op jit(solution)/shard_map/ppermute | solution.py:217
  428.2 2.1 fusion.36
  433.2 26.2 %collective-permute-done.5 = bf16[576,1024]{1,0:T(8,128)(2,1)} collective-permute-done((bf16[576,1024]{1,0:T(8,128)(2,1)}, bf16[576,1024]{1,0:T(8,128)(2,1)}, u32[]{:S(2)}, u32[]{:S(2)}) %collective-permute-start.5) | collective-permute-done | bytes 1179680 | tf_op jit(solution)/shard_map/ppermute | solution.py:225
  462.7 2.9 copy.36
  465.7 105.6 %attend_back.1 = bf16[3,8,72,2048]{3,2,1,0:T(8,128)(2,1)S(1)} custom-call(bf16[24,72,2048]{2,1,0:T(8,128)(2,1)} %bitcast.68, bf16[24,72,2048]{2,1,0:T(8,128)(2,1)} %bitcast.69, bf16[24,72,2048]{2,1,0:T(8,128)(2,1)} %bitcast.70, bf16[8,72,2048]{2,1,0:T(8,128)(2,1)S(1)} %bitcast.64, f32[8,1,2048]{2,1,0:T(1,128)S(1)} %get-tuple-element.11.l_ref), custom_call_target="tpu_custom_call" | custom-call | flops 67645734912 | bytes 18874368 | tf_op jit(solution)/shard_map/attend_back/pallas_call | solution.py:184
  571.4 2.8 copy-done.1
  574.3 16.0 %convolution_convert_fusion.4 = bf16[1152,1728]{1,0:T(8,128)(2,1)} fusion(bf16[1728,2048]{1,0:T(8,128)(2,1)} %bitcast.71, f32[1152]{0:T(1024)S(1)} %copy-done.45, f32[1152]{0:T(1024)S(1)} %copy-done.43, f32[2048]{0:T(1024)S(1)} %copy-done.47, f32[2048]{0:T(1024)S(1)} %copy-done.38, bf16[1024,1152]{1,0:T(8,128)(2,1)} %collective-permute-done.1, ...), kind=kOutput, calls=%fused_computation.24 | convolution fusion | flops 8181669888 | bytes 15803392 | tf_op jit(solution)/shard_map/dot_general | solution.py:36
  590.8 7.0 convolution_convert_fusion.2
  597.9 40.2 %reduce-scatter.5.cloned.1.call-done = bf16[144,1728]{1,0:T(8,128)(2,1)} async-done(((bf16[1152,1728]{1,0:T(8,128)(2,1)}), bf16[144,1728]{1,0:T(8,128)(2,1)}) %reduce-scatter.5.cloned.1.call-update) | async-done | bytes 497680 | tf_op jit(solution)/shard_map/reduce_scatter | solution.py:243
  638.2 17.2 %convolution_convert_fusion.1 = bf16[1152,4608]{1,0:T(8,128)(2,1)} fusion(bf16[1024,1152]{1,0:T(8,128)(2,1)S(1)} %bitcast.86, bf16[1024,4608]{1,0:T(8,128)(2,1)} %fusion.8), kind=kOutput, calls=%fused_computation.3 | convolution fusion | flops 10876944384 | bytes 22413312 | tf_op jit(solution)/shard_map/dot_general | solution.py:36
  657.1 21.1 %convolution_convert_fusion = bf16[4608,1152]{1,0:T(8,128)(2,1)} fusion(bf16[1024,1152]{1,0:T(8,128)(2,1)S(1)} %bitcast.84, f32[1024,4608]{1,0:T(8,128)} %fusion.73), kind=kOutput, calls=%fused_computation.2 | convolution fusion | flops 10919411712 | bytes 31850496 | tf_op jit(solution)/shard_map/dot_general | solution.py:36
  678.2 13.5 %fusion.74 = f32[2048,1152]{1,0:T(8,128)S(1)} fusion(bf16[1728,2048]{1,0:T(8,128)(2,1)} %bitcast.72, bf16[1152,1728]{1,0:T(8,128)(2,1)} %all-gather.10.cloned.1.call-done), kind=kOutput, calls=%fused_computation.143 | convolution fusion | flops 8153726976 | bytes 20496384 | tf_op jit(solution)/shard_map/dot_general | solution.py:36
  695.2 2.5 collective-permute-done.10
  698.3 58.1 %collective-permute-done.6 = bf16[1024,1152]{1,0:T(8,128)(2,1)S(1)} collective-permute-done((bf16[1024,1152]{1,0:T(8,128)(2,1)S(1)}, bf16[1024,1152]{1,0:T(8,128)(2,1)S(1)}, u32[]{:S(2)}, u32[]{:S(2)}) %collective-permute-start.6) | collective-permute-done | bytes 2359328 | tf_op jit(solution)/shard_map/ppermute | solution.py:225
  756.9 2.1 copy-done.12
  761.6 15.6 %all-gather.3 = f32[8,2,4608]{2,1,0:T(2,128)S(1)} all-gather(f32[1,2,4608]{2,1,0:T(2,128)S(1)} %add_bitcast_fusion), channel_id=1, replica_groups=mesh['dp'=8,'seq'=4] {'dp'}, dimensions={0}, use_global_device_ids=true | all-gather | bytes 331776 | tf_op jit(solution)/shard_map/all_gather | solution.py:239
  777.9 3.6 fusion.67
  781.5 5.4 collective-permute-done.7
  786.9 2.4 fusion.31
  789.3 2.0 fusion.24
  792.9 2.3 collective-permute-done.8
  795.3 4.9 fusion.23
  800.2 16.8 %all-gather.2 = f32[8,2,2304]{2,1,0:T(2,128)S(1)} all-gather(f32[1,2,2304]{2,1,0:T(2,128)S(1)} %add_bitcast_fusion.1), channel_id=1, replica_groups=mesh['dp'=8,'seq'=4] {'dp'}, dimensions={0}, use_global_device_ids=true | all-gather | bytes 165888 | tf_op jit(solution)/shard_map/all_gather | solution.py:239
  822.2 4.5 all-to-all-start.1
  828.4 2.2 pad_maximum_fusion.2
  830.6 2.1 all-to-all-done.1
  833.4 7.1 reshape.179
  840.5 4.9 reduce_sum.179
  845.5 3.1 copy.38
  848.6 3.7 reshape.177
  852.2 102.6 %reduce-scatter.11.cloned.1.call-done = bf16[576,1152]{1,0:T(8,128)(2,1)} async-done(((bf16[4608,1152]{1,0:T(8,128)(2,1)}), bf16[576,1152]{1,0:T(8,128)(2,1)}) %reduce-scatter.11.cloned.1.call-update) | async-done | bytes 1327120 | tf_op jit(solution)/shard_map/reduce_scatter | solution.py:243
  954.9 200.4 %all-reduce.2 = (f32[144,1152]{1,0:T(8,128)}, f32[144,4608]{1,0:T(8,128)}, f32[576,1152]{1,0:T(8,128)}) all-reduce(bf16[144,1152]{1,0:T(8,128)(2,1)S(1)} %copy-done.22, bf16[144,4608]{1,0:T(8,128)(2,1)} %reduce-scatter.9.cloned.1.call-done, ...), channel_id=1, replica_groups=mesh['dp'=8,'seq'=4] {'seq'}, use_global_device_ids=true, to_apply=%region_20.21 | all-reduce | flops 1492992 | bytes 8957952 | tf_op jit(solution)/shard_map/psum | solution.py:341
  (197 shorter events, 49.6 us)
Async XLA Ops:
  7.2 8.1 copy-start.3
  7.2 101.1 %all-gather.10.cloned.1.call-start = ((), (), s32[]{:S(2)}) async-start(), calls=%async_computation.6 | async-start | bytes 4644864 | tf_op jit(solution)/shard_map/all_gather | solution.py:239
  13.7 242.4 %all-gather.12.cloned.1.call-start = ((), (), s32[]{:S(2)}) async-start(), calls=%async_computation.7 | async-start | bytes 2985984 | tf_op jit(solution)/shard_map/all_gather | solution.py:239
  14.5 255.9 %all-gather.14.cloned.1.call-start = ((), (), s32[]{:S(2)}) async-start(), calls=%async_computation.8 | async-start | bytes 11943936 | tf_op jit(solution)/shard_map/all_gather | solution.py:239
  15.2 293.4 %all-gather.16.cloned.1.call-start = ((), (), s32[]{:S(2)}) async-start(), calls=%async_computation.9 | async-start | bytes 11943936 | tf_op jit(solution)/shard_map/all_gather | solution.py:239
  15.3 35.1 %copy-start.39 = (bf16[2,1152]{1,0:T(2,128)(2,1)S(1)}, bf16[2,1152]{1,0:T(2,128)(2,1)}, u32[]{:S(2)}) copy-start(bf16[2,1152]{1,0:T(2,128)(2,1)} %param.9) | copy-start | bytes 13828
  16.5 91.8 %copy-start.7 = (bf16[512,1152]{1,0:T(8,128)(2,1)}, bf16[512,1152]{1,0:T(8,128)(2,1)S(1)}, u32[]{:S(2)}) copy-start(bf16[512,1152]{1,0:T(8,128)(2,1)S(1)} %get-tuple-element.41) | copy-start | bytes 3538948
  16.5 48.4 %copy-start.10 = (bf16[144,6912]{1,0:T(8,128)(2,1)S(1)}, bf16[144,6912]{1,0:T(8,128)(2,1)}, u32[]{:S(2)}) copy-start(bf16[144,6912]{1,0:T(8,128)(2,1)} %param.10) | copy-start | bytes 5971972
  16.5 29.2 %collective-permute-start = (bf16[512,1152]{1,0:T(8,128)(2,1)}, bf16[512,1152]{1,0:T(8,128)(2,1)}, u32[]{:S(2)}, u32[]{:S(2)}) collective-permute-start(bf16[512,1152]{1,0:T(8,128)(2,1)} %get-tuple-element.42), channel_id=1, source_target_pairs={{0,1},{1,0},{2,3},{3,2},{4,5},{5,4},{6,7},{7,6},{8,9},{9,8},{10,11... | collective-permute-start | bytes 3538952 | tf_op jit(solution)/shard_map/ppermute | solution.py:217
  19.5 618.6 %reduce-scatter.5.cloned.1.call-start = ((), (), s32[]{:S(2)}) async-start(), calls=%async_computation.10 | async-start | bytes 4644864 | tf_op jit(solution)/shard_map/reduce_scatter | solution.py:243
  48.6 52.7 %collective-permute-start.1 = (bf16[1024,1152]{1,0:T(8,128)(2,1)}, bf16[1024,1152]{1,0:T(8,128)(2,1)}, u32[]{:S(2)}, u32[]{:S(2)}) collective-permute-start(bf16[1024,1152]{1,0:T(8,128)(2,1)} %pad_maximum_fusion.4), channel_id=1, source_target_pairs={{0,2},{1,3},{2,0},{3,1},{4,6},{5,7},{6,4},{7,5},{8,10},{9,11},{10,... | collective-permute-start | bytes 7077896 | tf_op jit(solution)/shard_map/ppermute | solution.py:225
  64.9 39.1 %copy-start.25 = (f32[16,1152]{1,0:T(8,128)}, f32[16,1152]{1,0:T(8,128)S(1)}, u32[]{:S(2)}) copy-start(f32[16,1152]{1,0:T(8,128)S(1)} %reshape.190) | copy-start | bytes 221188
  98.1 10.1 copy-start.23
  98.2 10.1 copy-start.42
  98.2 10.1 copy-start.44
  104.1 18.4 %copy-start.37 = (f32[2048]{0:T(1024)}, f32[2048]{0:T(1024)S(1)}, u32[]{:S(2)}) copy-start(f32[2048]{0:T(1024)S(1)} %broadcast_multiply_fusion) | copy-start | bytes 24580
  108.3 14.2 %copy-start.46 = (f32[2048]{0:T(1024)}, f32[2048]{0:T(1024)S(1)}, u32[]{:S(2)}) copy-start(f32[2048]{0:T(1024)S(1)} %add_rsqrt_fusion) | copy-start | bytes 24580
  122.5 51.2 %copy-start = (bf16[1728,2048]{1,0:T(8,128)(2,1)}, bf16[1728,2048]{1,0:T(8,128)(2,1)S(1)}, u32[]{:S(2)}) copy-start(bf16[1728,2048]{1,0:T(8,128)(2,1)S(1)} %convolution_convert_fusion.3) | copy-start | bytes 21233668
  184.7 26.6 %collective-permute-start.2 = (bf16[576,1024]{1,0:T(8,128)(2,1)}, bf16[576,1024]{1,0:T(8,128)(2,1)}, u32[]{:S(2)}, u32[]{:S(2)}) collective-permute-start(bf16[576,1024]{1,0:T(8,128)(2,1)} %bitcast.63), channel_id=1, source_target_pairs={{0,2},{1,3},{2,0},{3,1},{4,6},{5,7},{6,4},{7,5},{8,10},{9,11},{10,... | collective-permute-start | bytes 3538952 | tf_op jit(solution)/shard_map/ppermute | solution.py:225
  192.2 37.9 %copy-start.4 = (bf16[2,512,1152]{2,1,0:T(8,128)(2,1)S(1)}, bf16[2,512,1152]{2,1,0:T(8,128)(2,1)}, u32[]{:S(2)}) copy-start(bf16[2,512,1152]{2,1,0:T(8,128)(2,1)} %param.8) | copy-start | bytes 7077892
  205.1 25.5 %copy-start.24 = (f32[2,6912]{1,0:T(2,128)S(1)}, f32[2,6912]{1,0:T(2,128)}, u32[]{:S(2)}) copy-start(f32[2,6912]{1,0:T(2,128)} %copy-done.23) | copy-start | bytes 165892
  227.5 27.0 %copy-start.16 = (bf16[1152,1024]{0,1:T(8,128)(2,1)S(1)}, bf16[1152,1024]{0,1:T(8,128)(2,1)}, u32[]{:S(2)}) copy-start(bf16[1152,1024]{0,1:T(8,128)(2,1)} %dynamic_update_slice.7) | copy-start | bytes 7077892
  229.0 25.5 %collective-permute-start.3 = (bf16[1152,512]{0,1:T(8,128)(2,1)S(1)}, bf16[1152,512]{0,1:T(8,128)(2,1)S(1)}, u32[]{:S(2)}, u32[]{:S(2)}) collective-permute-start(bf16[1152,512]{0,1:T(8,128)(2,1)S(1)} %slice.93), channel_id=1, source_target_pairs={{0,1},{1,0},{2,3},{3,2},{4,5},{5,4},{6,7},{7,6},{8,9},{9,8},{10,11... | collective-permute-start | bytes 3538952 | tf_op jit(solution)/shard_map/ppermute | solution.py:217
  230.5 31.6 %copy-start.35 = (f32[2,512]{1,0:T(2,128)}, f32[2,512]{1,0:T(2,128)S(1)}, u32[]{:S(2)}) copy-start(f32[2,512]{1,0:T(2,128)S(1)} %broadcast_multiply_fusion.3) | copy-start | bytes 12292
  231.2 31.0 %copy-start.29 = (f32[2,1152]{1,0:T(2,128)}, f32[2,1152]{1,0:T(2,128)S(1)}, u32[]{:S(2)}) copy-start(f32[2,1152]{1,0:T(2,128)S(1)} %get-tuple-element.47) | copy-start | bytes 27652
  231.2 33.8 %copy-start.27 = (f32[2,1152]{1,0:T(2,128)}, f32[2,1152]{1,0:T(2,128)S(1)}, u32[]{:S(2)}) copy-start(f32[2,1152]{1,0:T(2,128)S(1)} %get-tuple-element.44) | copy-start | bytes 27652
  270.3 38.3 %copy-start.17 = (bf16[2,512,1152]{2,1,0:T(8,128)(2,1)}, bf16[2,512,1152]{2,1,0:T(8,128)(2,1)S(1)}, u32[]{:S(2)}) copy-start(bf16[2,512,1152]{2,1,0:T(8,128)(2,1)S(1)} %get-tuple-element.50) | copy-start | bytes 7077892
  353.8 31.1 %slice-start = ((s8[4718592]{0:T(1024)(128)(4,1)}), s8[4194304]{0:T(1024)(128)(4,1)S(1)}, s32[]{:S(2)}) async-start(s8[4718592]{0:T(1024)(128)(4,1)} %bitcast.73), calls=%async_computation.15 | async-start | bytes 8388608
  353.8 31.1 %slice-start.2 = ((s8[4718592]{0:T(1024)(128)(4,1)}), s8[4194304]{0:T(1024)(128)(4,1)S(1)}, s32[]{:S(2)}) async-start(s8[4718592]{0:T(1024)(128)(4,1)} %bitcast.76), calls=%async_computation.17 | async-start | bytes 8388608
  353.8 31.1 %slice-start.4 = ((s8[4718592]{0:T(1024)(128)(4,1)}), s8[4194304]{0:T(1024)(128)(4,1)S(1)}, s32[]{:S(2)}) async-start(s8[4718592]{0:T(1024)(128)(4,1)} %bitcast.79), calls=%async_computation.19 | async-start | bytes 8388608
  360.9 24.0 %slice-start.1 = ((s8[4718592]{0:T(1024)(128)(4,1)}), s8[524288]{0:T(1024)(128)(4,1)S(1)}, s32[]{:S(2)}) async-start(s8[4718592]{0:T(1024)(128)(4,1)} %bitcast.73), calls=%async_computation.16 | async-start | bytes 1048576
  360.9 24.0 %slice-start.3 = ((s8[4718592]{0:T(1024)(128)(4,1)}), s8[524288]{0:T(1024)(128)(4,1)S(1)}, s32[]{:S(2)}) async-start(s8[4718592]{0:T(1024)(128)(4,1)} %bitcast.76), calls=%async_computation.18 | async-start | bytes 1048576
  360.9 24.1 %slice-start.5 = ((s8[4718592]{0:T(1024)(128)(4,1)}), s8[524288]{0:T(1024)(128)(4,1)S(1)}, s32[]{:S(2)}) async-start(s8[4718592]{0:T(1024)(128)(4,1)} %bitcast.79), calls=%async_computation.20 | async-start | bytes 1048576
  360.9 24.1 %copy-start.15 = (bf16[2,512,1152]{2,1,0:T(8,128)(2,1)S(1)}, bf16[2,512,1152]{2,1,0:T(8,128)(2,1)}, u32[]{:S(2)}) copy-start(bf16[2,512,1152]{2,1,0:T(8,128)(2,1)} %param.15) | copy-start | bytes 7077892
  360.9 24.1 %copy-start.28 = (f32[2,1152]{1,0:T(2,128)S(1)}, f32[2,1152]{1,0:T(2,128)}, u32[]{:S(2)}) copy-start(f32[2,1152]{1,0:T(2,128)} %copy-done.27) | copy-start | bytes 27652
  385.0 7.1 copy-start.30
  392.1 7.7 copy-start.6
  392.5 7.3 copy-start.20
  400.0 28.2 %collective-permute-start.4 = (bf16[1152,512]{0,1:T(8,128)(2,1)S(1)}, bf16[1152,512]{0,1:T(8,128)(2,1)S(1)}, u32[]{:S(2)}, u32[]{:S(2)}) collective-permute-start(bf16[1152,512]{0,1:T(8,128)(2,1)S(1)} %get-tuple-element.36), channel_id=1, source_target_pairs={{0,1},{1,0},{2,3},{3,2},{4,5},{5,4},{6,7},{7,6},{8,9},{9,8},{10,11... | collective-permute-start | bytes 3538952 | tf_op jit(solution)/shard_map/ppermute | solution.py:217
  431.7 27.6 %collective-permute-start.5 = (bf16[576,1024]{1,0:T(8,128)(2,1)}, bf16[576,1024]{1,0:T(8,128)(2,1)}, u32[]{:S(2)}, u32[]{:S(2)}) collective-permute-start(bf16[576,1024]{1,0:T(8,128)(2,1)} %copy.34), channel_id=1, source_target_pairs={{0,2},{1,3},{2,0},{3,1},{4,6},{5,7},{6,4},{7,5},{8,10},{9,11},{10,... | collective-permute-start | bytes 3538952 | tf_op jit(solution)/shard_map/ppermute | solution.py:225
  465.7 108.5 %copy-start.8 = (bf16[512,1152]{1,0:T(8,128)(2,1)S(1)}, bf16[512,1152]{1,0:T(8,128)(2,1)}, u32[]{:S(2)}) copy-start(bf16[512,1152]{1,0:T(8,128)(2,1)} %copy-done.7) | copy-start | bytes 3538948
  465.7 108.5 %copy-start.38 = (f32[2048]{0:T(1024)S(1)}, f32[2048]{0:T(1024)}, u32[]{:S(2)}) copy-start(f32[2048]{0:T(1024)} %copy-done.37) | copy-start | bytes 24580
  465.7 108.5 %copy-start.43 = (f32[1152]{0:T(1024)S(1)}, f32[1152]{0:T(1024)}, u32[]{:S(2)}) copy-start(f32[1152]{0:T(1024)} %copy-done.42) | copy-start | bytes 13828
  465.7 108.5 %copy-start.45 = (f32[1152]{0:T(1024)S(1)}, f32[1152]{0:T(1024)}, u32[]{:S(2)}) copy-start(f32[1152]{0:T(1024)} %copy-done.44) | copy-start | bytes 13828
  465.7 108.5 %copy-start.47 = (f32[2048]{0:T(1024)S(1)}, f32[2048]{0:T(1024)}, u32[]{:S(2)}) copy-start(f32[2048]{0:T(1024)} %copy-done.46) | copy-start | bytes 24580
  574.2 16.6 %copy-start.21 = (bf16[1152,512]{0,1:T(8,128)(2,1)S(1)}, bf16[1152,512]{0,1:T(8,128)(2,1)}, u32[]{:S(2)}) copy-start(bf16[1152,512]{0,1:T(8,128)(2,1)} %get-tuple-element.31) | copy-start | bytes 3538948
  590.3 47.8 %copy-start.19 = (bf16[2,512,1152]{2,1,0:T(8,128)(2,1)S(1)}, bf16[2,512,1152]{2,1,0:T(8,128)(2,1)}, u32[]{:S(2)}) copy-start(bf16[2,512,1152]{2,1,0:T(8,128)(2,1)} %get-tuple-element.51) | copy-start | bytes 7077892
  590.3 191.2 %reduce-scatter.7.cloned.1.call-start = ((), (), s32[]{:S(2)}) async-start(), calls=%async_computation.11 | async-start | bytes 2985984 | tf_op jit(solution)/shard_map/reduce_scatter | solution.py:243
  597.8 235.6 %all-gather.18.cloned.1.call-start = ((), (), s32[]{:S(2)}) async-start(), calls=%async_computation.14 | async-start | bytes 2580480 | tf_op jit(solution)/shard_map/all_gather | solution.py:346
  638.1 214.1 %reduce-scatter.9.cloned.1.call-start = ((), (), s32[]{:S(2)}) async-start(), calls=%async_computation.12 | async-start | bytes 11943936 | tf_op jit(solution)/shard_map/reduce_scatter | solution.py:243
  655.4 299.5 %reduce-scatter.11.cloned.1.call-start = ((), (), s32[]{:S(2)}) async-start(), calls=%async_computation.13 | async-start | bytes 11943936 | tf_op jit(solution)/shard_map/reduce_scatter | solution.py:243
  692.0 64.4 %collective-permute-start.6 = (bf16[1024,1152]{1,0:T(8,128)(2,1)S(1)}, bf16[1024,1152]{1,0:T(8,128)(2,1)S(1)}, u32[]{:S(2)}, u32[]{:S(2)}) collective-permute-start(bf16[1024,1152]{1,0:T(8,128)(2,1)S(1)} %slice.131), channel_id=1, source_target_pairs={{0,2},{1,3},{2,0},{3,1},{4,6},{5,7},{6,4},{7,5},{8,10},{9,11},{10,... | collective-permute-start | bytes 7077896 | tf_op jit(solution)/shard_map/ppermute | solution.py:225
  693.6 4.0 collective-permute-start.10
  697.7 79.7 %copy-start.11 = (bf16[144,6912]{1,0:T(8,128)(2,1)S(1)}, bf16[144,6912]{1,0:T(8,128)(2,1)}, u32[]{:S(2)}) copy-start(bf16[144,6912]{1,0:T(8,128)(2,1)} %param.10) | copy-start | bytes 5971972
  697.7 63.9 %collective-permute-start.11 = (f32[2,4608]{1,0:T(2,128)S(1)}, f32[2,4608]{1,0:T(2,128)S(1)}, u32[]{:S(2)}, u32[]{:S(2)}) collective-permute-start(f32[2,4608]{1,0:T(2,128)S(1)} %fusion.96), channel_id=1, source_target_pairs={{0,2},{1,3},{2,0},{3,1},{4,6},{5,7},{6,4},{7,5},{8,10},{9,11},{10,... | collective-permute-start | bytes 110600 | tf_op jit(solution)/shard_map/ppermute | solution.py:225
  760.1 26.8 %collective-permute-start.7 = (bf16[512,1152]{1,0:T(8,128)(2,1)}, bf16[512,1152]{1,0:T(8,128)(2,1)}, u32[]{:S(2)}, u32[]{:S(2)}) collective-permute-start(bf16[512,1152]{1,0:T(8,128)(2,1)} %slice.132), channel_id=1, source_target_pairs={{0,1},{1,0},{2,3},{3,2},{4,5},{5,4},{6,7},{7,6},{8,9},{9,8},{10,11... | collective-permute-start | bytes 3538952 | tf_op jit(solution)/shard_map/ppermute | solution.py:217
  781.5 7.8 copy-start.5
  781.5 7.8 copy-start.26
  781.5 7.8 copy-start.36
  791.3 3.8 collective-permute-start.8
  795.2 5.0 collective-permute-start.9
  800.1 28.2 %copy-start.13 = (f32[144,4608]{1,0:T(8,128)S(1)}, f32[144,4608]{1,0:T(8,128)}, u32[]{:S(2)}) copy-start(f32[144,4608]{1,0:T(8,128)} %fusion.67) | copy-start | bytes 7962628
  822.2 10.5 all-to-all-start.1
  845.5 109.4 %copy-start.22 = (bf16[144,1152]{1,0:T(8,128)(2,1)S(1)}, bf16[144,1152]{1,0:T(8,128)(2,1)}, u32[]{:S(2)}) copy-start(bf16[144,1152]{1,0:T(8,128)(2,1)} %reduce-scatter.7.cloned.1.call-done) | copy-start | bytes 995332
  (13 other events, 35.1 us)
Sparse Core Ops, SparseCore 0:
  13.8 49.1 all-gather.9
  64.7 42.5 all-gather.11
  108.9 99.2 all-gather.13
  209.8 98.7 all-gather.15
  590.4 47.6 reduce-scatter.4
  640.8 36.5 reduce-scatter.6
  679.3 47.4 all-gather.17
  729.1 114.3 reduce-scatter.8
  845.8 109.0 reduce-scatter.10

commit v2 on v1

--- a/solution.py
+++ b/solution.py
@@ -54,6 +54,7 @@
 
 
 def forward_kernel(rows, chunk, q_ref, k_ref, v_ref, o_ref, l_ref, twice_ref, score_ref):
+    steps_each = o_ref.shape[3] // rows
     features, length = k_ref.shape[1:]
     factor = log2_e / math.sqrt(features)
     keys = k_ref[0]
@@ -78,7 +79,8 @@
             term = dot(v_ref[0, :, low : low + chunk], exponent.astype(half), 1, 0)
             mix = term if mix is None else mix + term
         total = jnp.sum(total, axis=0, keepdims=True)
-        o_ref[0, :, cols] = (mix / total).astype(o_ref.dtype)
+        within = pl.ds(pl.multiple_of((at % steps_each) * rows, rows), rows)
+        o_ref[at // steps_each, 0, :, within] = (mix / total).astype(o_ref.dtype)
         l_ref[0, :, cols] = top + jnp.log2(total)
         return carry
 
@@ -89,20 +91,24 @@
     return pl.BlockSpec((1, features, length), lambda head: (head + offset, 0, 0))
 
 
-def attend(packed):
-    triple, features, length = packed.shape
-    heads = triple // 3
-    rows, chunk = min(1024, length), min(512, length)
+def attend(packed, heads, which, groups):
+    features, length = packed.shape[1:]
+    each = length // groups
+    rows, chunk = min(1024, each), min(512, length)
     block = functools.partial(block_of, features, length)
+    base = 3 * heads * which
     return pl.pallas_call(
         functools.partial(forward_kernel, rows, chunk),
         grid=(heads,),
         out_shape=(
-            jax.ShapeDtypeStruct((heads, features, length), half),
+            jax.ShapeDtypeStruct((groups, heads, features, each), half),
             jax.ShapeDtypeStruct((heads, 1, length), full),
         ),
-        in_specs=[block(0), block(heads), block(2 * heads)],
-        out_specs=(block(0), block_of(1, length, 0)),
+        in_specs=[block(base), block(base + heads), block(base + 2 * heads)],
+        out_specs=(
+            pl.BlockSpec((groups, 1, features, each), lambda head: (0, head, 0, 0)),
+            block_of(1, length, 0),
+        ),
         scratch_shapes=[
             pltpu.VMEM((length, 2 * features), half),
             pltpu.VMEM((length, rows), full),
@@ -118,8 +124,9 @@
 
 
 def backward_kernel(
-    rows, chunk, q_ref, k_ref, v_ref, g_ref, l_ref, out_ref, k_s, twice_s, dk_s, dv_s, p_s, t_s
+    rows, chunk, q_ref, k_ref, v_ref, g_ref, l_ref, *refs
 ):
+    out_ref, k_s, twice_s, dk_s, dv_s, p_s, t_s = refs[-7:]
     features, length = k_ref.shape[1:]
     scale = 1.0 / math.sqrt(features)
     factor = log2_e * scale
@@ -175,18 +182,27 @@
     out_ref[2, 0] = dv_s[...].astype(half)
 
 
-def attend_back(packed, grads, log_totals):
-    triple, features, length = packed.shape
-    heads = triple // 3
+def attend_back(packed, grads, log_totals, heads, which, earlier):
+    features, length = packed.shape[1:]
     rows, chunk = min(512, length), min(256, length)
     lanes = -(-features // 128) * 128
     block = functools.partial(block_of, features, length)
+    base = 3 * heads * which
+    operands = [packed, packed, packed, grads, log_totals]
+    in_specs = [block(base), block(base + heads), block(base + 2 * heads), block(heads * which)]
+    in_specs.append(block_of(1, length, 0))
+    aliases = {}
+    if earlier is not None:
+        aliases = {len(operands): 0}
+        operands.append(earlier)
+        in_specs.append(pl.BlockSpec(memory_space=pl.ANY))
     return pl.pallas_call(
         functools.partial(backward_kernel, rows, chunk),
         grid=(heads,),
-        out_shape=jax.ShapeDtypeStruct((3, heads, features, length), half),
-        in_specs=[block(0), block(heads), block(2 * heads), block(0), block_of(1, length, 0)],
-        out_specs=pl.BlockSpec((3, 1, features, length), lambda head: (0, head, 0, 0)),
+        out_shape=jax.ShapeDtypeStruct((packed.shape[0] // heads, heads, features, length), half),
+        in_specs=in_specs,
+        out_specs=pl.BlockSpec((3, 1, features, length), lambda head: (which, head, 0, 0)),
+        input_output_aliases=aliases,
         scratch_shapes=[
             pltpu.VMEM((length, lanes), half),
             pltpu.VMEM((2 * features + 8, length), half),
@@ -202,7 +218,7 @@
             transcendentals=heads * length * length,
         ),
         name="attend_back",
-    )(packed, packed, packed, grads, log_totals)
+    )(*operands)
 
 
 class Exchange:
@@ -224,9 +240,23 @@
         ]
         return lax.ppermute(value, "seq", pairs)
 
+    def over_groups(self, value):
+        sent = value.astype(self.kind(value))
+        for by in range(1, self.groups):
+            value = value + self.shift(sent, by).astype(full)
+        return value
+
+    def over_sides(self, value):
+        return value + self.across(value.astype(self.kind(value))).astype(full)
+
+    def kind(self, value):
+        return half if value.size > 65536 else full
+
     def total(self, value):
-        value = value + self.across(value)
-        return value + sum(self.shift(value, by) for by in range(1, self.groups))
+        return self.over_groups(self.over_sides(value.astype(full)))
+
+    def place(self, values, at):
+        return jnp.concatenate([lax.dynamic_index_in_dim(values, spot, 0) for spot in at], axis=0)
 
     def mine(self, first, second):
         return jnp.where(self.side == 0, first, second)
@@ -254,12 +284,16 @@
     features = width // HEADS
     span = width // groups
     own_heads = HEADS // groups
+    chunks = 2
+    chunk_heads = own_heads // chunks
+    piece = span // chunks
     ada_rows = w_ada.shape[0]
 
-    cond_all = gather_rows(cond).astype(full)
-    logistic_all = jax.nn.sigmoid(cond_all)
-    shrunk_all = (cond_all * logistic_all).astype(half)
-    shrunk_rows = lax.dynamic_slice_in_dim(shrunk_all, dp_index * ada_rows, ada_rows, 1)
+    cond_full = cond.astype(full)
+    logistic = jax.nn.sigmoid(cond_full)
+    shrunk = (cond_full * logistic).astype(half).reshape(images_here, dp_size, ada_rows)
+    shrunk_rows = lax.all_to_all(jnp.swapaxes(shrunk, 0, 1), "dp", 0, 0)
+    shrunk_rows = shrunk_rows.reshape(dp_size * images_here, ada_rows)
     mod_terms = dot(shrunk_rows, w_ada, 1, 0)
     mod_terms = lax.all_to_all(mod_terms, "dp", split_axis=0, concat_axis=0, tiled=True)
     modulation = jnp.sum(mod_terms.reshape(dp_size, images_here, 6 * width), axis=0)
@@ -267,17 +301,28 @@
         piece[:, None, :] for piece in jnp.split(modulation, 6, axis=1)
     ]
 
+    own = ex.mine(latents[0], latents[1])
     received = ex.across(ex.other(latents[0], latents[1]))
-    pair = jnp.concatenate([ex.mine(latents[0], latents[1]), received], axis=0)
-    tokens_image = jnp.concatenate([pair] + [ex.shift(pair, by) for by in range(1, groups)], axis=0)
-
-    qkv_cols = lax.dynamic_slice_in_dim(
-        w_qkv.reshape(w_qkv.shape[0], 3, width), ex.group * span, span, 2
-    ).reshape(w_qkv.shape[0], 3 * span)
+    blocks = [own, received]
+    for by in range(1, groups):
+        blocks += [ex.shift(own, by), ex.shift(received, by)]
+    tokens_image = jnp.concatenate(blocks, axis=0)
+
+    starts = [
+        part * width + ex.group * span + which * piece
+        for which in range(chunks)
+        for part in range(3)
+    ]
+    qkv_cols = jnp.concatenate(
+        [lax.dynamic_slice_in_dim(w_qkv, start, piece, 1) for start in starts], axis=1
+    )
     qkv_full = gather_rows(qkv_cols)
     proj_full = gather_rows(w_proj)
     fc1_full = gather_rows(w_fc1)
     fc2_full = gather_rows(w_fc2)
+    proj_full = ex.place(
+        proj_full.reshape(groups, span, width), [(ex.group + by) % groups for by in range(groups)]
+    ).reshape(width, width)
 
     hat_image, _ = normalize(tokens_image.astype(full))
     normed_image = (
@@ -286,18 +331,23 @@
     ).astype(half)
     packed = dot(qkv_full, normed_image, 0, 1).astype(half)
     packed = packed.reshape(3 * own_heads, features, length)
-    attended_own, log_totals = attend(packed)
-    attended_own = attended_own.reshape(span, groups, 2 * tokens_here)
-
-    attended_pair = jnp.zeros((width, 2 * tokens_here), half)
-    for by in range(groups):
-        block = attended_own[:, by]
-        block = ex.shift(block, -by) if by else block
-        start = ((ex.group + by) % groups) * span
-        attended_pair = lax.dynamic_update_slice_in_dim(attended_pair, block, start, 0)
-    kept, sent = attended_pair[:, :tokens_here], attended_pair[:, tokens_here:]
-    received = ex.across(sent)
-    attended = jnp.concatenate([ex.mine(kept, received), ex.other(kept, received)], axis=1)
+
+    log_totals = []
+    pieces = {}
+    for which in range(chunks):
+        attended_own, log_total = attend(packed, chunk_heads, which, groups)
+        log_totals.append(log_total)
+        attended_own = attended_own.reshape(groups, piece, 2 * tokens_here)
+        for by in range(groups):
+            block = ex.shift(attended_own[by], -by) if by else attended_own[0]
+            received = ex.across(block[:, tokens_here:])
+            kept = block[:, :tokens_here]
+            pieces[by, which] = jnp.concatenate(
+                [ex.mine(kept, received), ex.other(kept, received)], axis=1
+            )
+    attended = jnp.concatenate(
+        [pieces[by, which] for by in range(groups) for which in range(chunks)], axis=0
+    )
 
     latent_full = latents.astype(full)
     branch_one = dot(attended, proj_full, 0, 0).reshape(images_here, tokens_here, width)
@@ -325,70 +375,95 @@
 
     first, second = grad_attended[:, :tokens_here], grad_attended[:, tokens_here:]
     received = ex.across(ex.other(first, second))
-    grad_pair = jnp.concatenate([ex.mine(first, second), received], axis=1)
-    blocks = []
-    for by in range(groups):
-        start = ((ex.group + by) % groups) * span
-        block = lax.dynamic_slice_in_dim(grad_pair, start, span, 0)
-        blocks.append(ex.shift(block, by) if by else block)
+    own = ex.mine(first, second)
+    term_fc2 = dot(hidden_act, grad_branch_two, 0, 0).astype(half)
+    early = ex.total(
+        jnp.concatenate([grad_gate_one, grad_shift_two, grad_scale_two, grad_gate_two], axis=1)
+    )
+    own_moved = [ex.shift(own[by * span : (by + 1) * span], by) for by in range(1, groups)]
+    received, term_fc2 = lax.optimization_barrier((received, term_fc2))
+    grad_fc2 = scatter_rows(term_fc2)
+    received_moved = [ex.shift(received[by * span : (by + 1) * span], by) for by in range(1, groups)]
+    term_fc1 = dot(normed_two, grad_pre, 0, 0).astype(half)
+    term_proj = dot(attended, grad_branch_one, 1, 0).astype(half)
+    term_proj = ex.place(
+        term_proj.reshape(groups, span, width), [(by - ex.group) % groups for by in range(groups)]
+    ).reshape(width, width)
+    early = gather_rows(early)
+    received_moved, own_moved, term_fc1, term_proj, early = lax.optimization_barrier(
+        (received_moved, own_moved, term_fc1, term_proj, early)
+    )
+    grad_fc1 = scatter_rows(term_fc1)
+    blocks = [own[:span], received[:span]]
+    for by in range(1, groups):
+        blocks += [own_moved[by - 1], received_moved[by - 1]]
     grad_heads = jnp.concatenate(blocks, axis=1).reshape(own_heads, features, length)
 
-    grad_fc2 = scatter_rows(dot(hidden_act, grad_branch_two, 0, 0).astype(half))
-    grad_fc1 = scatter_rows(dot(normed_two, grad_pre, 0, 0).astype(half))
-    grad_proj = scatter_rows(dot(attended, grad_branch_one, 1, 0).astype(half))
-    grad_fc2 = lax.psum(grad_fc2.astype(full), "seq")
-    grad_fc1 = lax.psum(grad_fc1.astype(full), "seq")
-    grad_proj = lax.psum(grad_proj.astype(full), "seq")
-
-    grad_packed = attend_back(packed, grad_heads, log_totals).reshape(3 * span, length)
+    grad_packed = None
+    for which in range(chunks):
+        grad_packed = attend_back(
+            packed, grad_heads, log_totals[which], chunk_heads, which, grad_packed
+        )
+    grad_packed = grad_packed.reshape(3 * span, length)
+    grad_packed, grad_fc2 = lax.optimization_barrier((grad_packed, grad_fc2))
+    grad_fc2 = ex.total(grad_fc2)
+
+    def term_of(at):
+        return dot(grad_packed[:, at * tokens_here : (at + 1) * tokens_here], qkv_full, 0, 1)
+
+    partner_term, own_term = 0.0, 0.0
+    for by in range(1, groups):
+        partner_term += ex.shift(term_of(2 * by + 1).astype(half), -by).astype(full)
+    for by in range(1, groups):
+        own_term += ex.shift(term_of(2 * by).astype(half), -by).astype(full)
+    received = ex.across((partner_term + term_of(1)).astype(half)).astype(full)
+    kept = own_term + term_of(0)
+    grad_normed_one = jnp.stack([ex.mine(kept, received), ex.other(kept, received)])
 
     grad_qkv = scatter_rows(dot(normed_image, grad_packed, 0, 1).astype(half))
-    grad_qkv = lax.all_gather(grad_qkv, "seq", axis=0).astype(full)
+    grad_proj = ex.total(scatter_rows(term_proj))
+    grad_fc1 = ex.total(grad_fc1)
+    grad_qkv = ex.over_sides(grad_qkv.astype(full)).astype(half)
+    grad_qkv = jnp.stack([grad_qkv] + [ex.shift(grad_qkv, by) for by in range(1, groups)])
+    grad_qkv = ex.place(grad_qkv, [(ex.group - at) % groups for at in range(groups)])
     qkv_rows = w_qkv.shape[0]
-    grad_qkv = jnp.sum(grad_qkv.reshape(groups, 2, qkv_rows, 3, span), axis=1)
-    grad_qkv = jnp.transpose(grad_qkv, (1, 2, 0, 3)).reshape(qkv_rows, 3 * width)
-
-    terms = dot(grad_packed, qkv_full, 0, 1)
-    terms = terms.reshape(groups, 2 * tokens_here, width)
-    grad_pair_normed = terms[0]
-    for by in range(1, groups):
-        grad_pair_normed = grad_pair_normed + ex.shift(terms[by].astype(half), -by).astype(full)
-    kept = grad_pair_normed[:tokens_here]
-    received = ex.across(grad_pair_normed[tokens_here:].astype(half)).astype(full)
-    grad_normed_one = jnp.stack([ex.mine(kept, received), ex.other(kept, received)])
+    grad_qkv = grad_qkv.reshape(groups, qkv_rows, chunks, 3, piece)
+    grad_qkv = jnp.concatenate(
+        [
+            grad_qkv[at, :, which, part]
+            for part in range(3)
+            for at in range(groups)
+            for which in range(chunks)
+        ],
+        axis=1,
+    ).astype(full)
 
     hat_one, inv_one = normalize(latent_full)
     grad_shift_one = jnp.sum(grad_normed_one, axis=1)
     grad_scale_one = jnp.sum(grad_normed_one * hat_one, axis=1)
     grad_latents = grad_residual + norm_back(grad_normed_one * (1.0 + scale_one), hat_one, inv_one)
 
-    late = ex.total(jnp.concatenate([grad_shift_one, grad_scale_one], axis=1))
-    early = ex.total(
-        jnp.concatenate([grad_gate_one, grad_shift_two, grad_scale_two, grad_gate_two], axis=1)
-    )
+    late = gather_rows(ex.total(jnp.concatenate([grad_shift_one, grad_scale_one], axis=1)))
     shrunk_own = shrunk_rows.astype(full)
     grad_ada = []
     grad_shrunk = 0.0
-    for piece, low in ((late, 0), (early, 2 * width)):
-        piece = gather_rows(piece)
+    for sums, low in ((late, 0), (early, 2 * width)):
         grad_ada.append(
             lax.dot_general(
                 shrunk_own,
-                piece,
+                sums,
                 (((0,), (0,)), ((), ())),
                 precision=lax.Precision.HIGHEST,
                 preferred_element_type=full,
             )
         )
-        upper, lower = split_two(piece)
-        ada_cols = w_ada[:, low : low + piece.shape[1]]
+        upper, lower = split_two(sums)
+        ada_cols = w_ada[:, low : low + sums.shape[1]]
         grad_shrunk = grad_shrunk + dot(upper, ada_cols, 1, 1) + dot(lower, ada_cols, 1, 1)
     grad_ada = jnp.concatenate(grad_ada, axis=1)
     grad_shrunk = lax.all_to_all(grad_shrunk, "dp", split_axis=0, concat_axis=0, tiled=True)
     grad_shrunk = grad_shrunk.reshape(dp_size, images_here, ada_rows)
     grad_shrunk = jnp.transpose(grad_shrunk, (1, 0, 2)).reshape(images_here, width)
-    cond_full = cond.astype(full)
-    logistic = jax.nn.sigmoid(cond_full)
     grad_cond = grad_shrunk * logistic * (1.0 + cond_full * (1.0 - logistic))
     return (
         mixed,

time: 1170 us -> 899 us (0.77)
  blocking collectives: 278 us -> 40.2 us
  local copies, waits for them, and re-layouts: 90.5 us -> 39.4 us
  waiting for transfers between devices: 344 us -> 307 us
  starting transfers between devices: 22.4 us -> 44.6 us
  other arithmetic: 55.2 us -> 76.2 us
  matrix products: 200 us -> 214 us
    psum x1 -> x0, blocking collectives: 200 us -> none  [per_device(): grad_proj = lax.psum(grad_proj.astype(full), 'seq')]
    reduce_scatter x4, waiting for transfers between devices: 143 us -> 102 us  [scatter_rows(): return lax.psum_scatter(term, 'dp', scatter_dimension=0, tiled=True)]
    dynamic_update_slice x2 -> x0, local copies, waits for them, and re-layouts: 26.6 us -> none  [per_device(): lax.dynamic_update_slice_in_dim(attended_pair, block, start, 0)]
    ppermute x6 -> x14, waiting for transfers between devices: 93.7 us -> 72.1 us  [shift(): return lax.ppermute(value, 'seq', pairs)]
    all_to_all x1, blocking collectives: 30.5 us -> 10.4 us  [per_device(): shrunk_rows = lax.all_to_all(jnp.swapaxes(shrunk, 0, 1), 'dp', 0, 0)]
    all_gather x4, waiting for transfers between devices: 17.9 us -> 37.3 us  [gather_rows(): return lax.all_gather(shard, 'dp', axis=0, tiled=True)]
    all_gather x3 -> x2, blocking collectives: 47 us -> 29.8 us  [gather_rows(): return lax.all_gather(shard, 'dp', axis=0, tiled=True)]
    reshape x5 -> x3, local copies, waits for them, and re-layouts: 18.5 us -> 1.91 us  [the longest x1 1.79 us: per_device(): grad_qkv = grad_qkv.reshape(groups, qkv_rows, chunks, 3, piece)]
  transfers between devices with their start and end apart: 22 -> 37, of which waited for: 14 -> 20; matrix products, arithmetic and copies ran while one was open for 18% -> 23% of each run, Pallas kernels for 4% -> 18%
where the time goes in v2:
time: 899 us; the launch traced here: 895 us
  waiting for transfers between devices  307 us (34%)
  matrix products  214 us (24%)
  Pallas kernels  159 us (18%)
  other arithmetic  76.2 us (8%)
  starting transfers between devices  44.6 us (5%)
  blocking collectives  40.2 us (4%)
  local copies, waits for them, and re-layouts  39.4 us (4%)
  between operations  15.7 us (2%)
    dot_general x20, matrix products, dot(): lax.dot_general(former, latter, (((former_dim,), (latter_dim,)), ((), ())...  210 us
    pallas_call x2, Pallas kernels, attend_back(): pl.pallas_call(functools.partial(backward_kernel, rows, chunk), grid=(hea...  107 us
    reduce_scatter x4, waiting for transfers between devices, scatter_rows(): return lax.psum_scatter(term, 'dp', scatter_dimension=0, tiled=True)  102 us
    ppermute x13, waiting for transfers between devices, across(): return lax.ppermute(value, 'seq', [(at, at ^ 1) for at in range(self.size)])  81.9 us
    ppermute x14, waiting for transfers between devices, shift(): return lax.ppermute(value, 'seq', pairs)  72.1 us
    pallas_call x2, Pallas kernels, attend(): pl.pallas_call(functools.partial(forward_kernel, rows, chunk), grid=(head...  51.5 us
    all_gather x4, waiting for transfers between devices, gather_rows(): return lax.all_gather(shard, 'dp', axis=0, tiled=True)  37.3 us
    all_gather x2, blocking collectives, gather_rows(): return lax.all_gather(shard, 'dp', axis=0, tiled=True)  29.8 us
  transfers between devices with their start and end apart: 37, of which 20 were waited for; matrix products, arithmetic and copies ran while one was open for 23% of the time, Pallas kernels for 18%

profile of v2, /device:TPU:0, one launch (start us, length us, event | category | flops | bytes accessed | tf_op | source)
XLA Modules:
  0.0 895.3 jit_solution(16268835807070051198)
XLA Ops:
  12.7 3.0 collective-permute-start
  15.9 10.4 %all_to_all.20 = bf16[8,2,144]{2,1,0:T(2,128)(2,1)S(1)} all-to-all(bf16[8,2,144]{2,1,0:T(2,128)(2,1)S(1)} %copy.140), channel_id=1, replica_groups=mesh['dp'=8,'seq'=4] {'dp'}, dimensions={0} | all-to-all | bytes 9216 | tf_op jit(solution)/shard_map/all_to_all | solution.py:295
  26.9 1.9 fusion.34
  29.8 4.1 all-to-all-start.1
  35.5 6.5 collective-permute-done
  44.8 10.0 %all-to-all-done.1 = f32[8,2,6912]{2,1,0:T(2,128)} async-done(((f32[8,2,6912]{2,1,0:T(2,128)}), f32[8,2,6912]{2,1,0:T(2,128)}, u32[]{:S(2)}, u32[]{:S(2)}) %all-to-all-start.1) | async-done | bytes 442400 | tf_op jit(solution)/shard_map/all_to_all | solution.py:298
  59.4 3.6 collective-permute-done.1
  63.0 24.6 %collective-permute-done.2 = bf16[512,1152]{1,0:T(8,128)(2,1)} collective-permute-done((bf16[512,1152]{1,0:T(8,128)(2,1)}, bf16[512,1152]{1,0:T(8,128)(2,1)}, u32[]{:S(2)}, u32[]{:S(2)}) %collective-permute-start.2) | collective-permute-done | bytes 1179680 | tf_op jit(solution)/shard_map/ppermute | solution.py:241
  87.6 3.2 convert_reduce_fusion
  91.4 4.1 fusion.11
  96.1 3.4 constant_dynamic-slice_fusion.3
  99.6 3.6 all-gather.7.cloned.1.call-done
  103.1 14.4 %convolution_convert_fusion.3 = bf16[1728,2048]{1,0:T(8,128)(2,1)S(1)} fusion(bf16[1152,1728]{1,0:T(8,128)(2,1)} %all-gather.7.cloned.1.call-done, f32[1152]{0:T(1024)} %get-tuple-element.42, f32[1152]{0:T(1024)} %get-tuple-element.41, f32[2048]{0:T(1024)} %add_rsqrt_fusion, f32[2048]{0:T(1024)} %copy-done.58, ...), kind=kOutput, calls=%fused_computation.23 | convolution fusion | flops 8187936768 | bytes 15803392 | tf_op jit(solution)/shard_map/dot_general | solution.py:36
  117.6 25.7 %attend.3 = (bf16[2,4,72,1024]{3,2,1,0:T(8,128)(2,1)S(1)}, f32[4,1,2048]{2,1,0:T(1,128)S(1)}) custom-call(bf16[24,72,2048]{2,1,0:T(8,128)(2,1)S(1)} %bitcast.115, bf16[24,72,2048]{2,1,0:T(8,128)(2,1)S(1)} %bitcast.116, bf16[24,72,2048]{2,1,0:T(8,128)(2,1)S(1)} %bitcast.117), custom_call_target="tpu_custom_call" | custom-call | flops 16911433728 | bytes 4718592 | tf_op jit(solution)/shard_map/attend/pallas_call | solution.py:100
  146.4 25.8 %attend.2 = (bf16[2,4,72,1024]{3,2,1,0:T(8,128)(2,1)S(1)}, f32[4,1,2048]{2,1,0:T(1,128)S(1)}) custom-call(bf16[24,72,2048]{2,1,0:T(8,128)(2,1)S(1)} %bitcast.118, bf16[24,72,2048]{2,1,0:T(8,128)(2,1)S(1)} %bitcast.119, bf16[24,72,2048]{2,1,0:T(8,128)(2,1)S(1)} %bitcast.120), custom_call_target="tpu_custom_call" | custom-call | flops 16911433728 | bytes 4718592 | tf_op jit(solution)/shard_map/attend/pallas_call | solution.py:100
  176.9 10.7 %collective-permute-done.5 = bf16[288,1024]{1,0:T(8,128)(2,1)S(1)} collective-permute-done((bf16[288,1024]{1,0:T(8,128)(2,1)S(1)}, bf16[288,1024]{1,0:T(8,128)(2,1)S(1)}, u32[]{:S(2)}, u32[]{:S(2)}) %collective-permute-start.5) | collective-permute-done | bytes 589856 | tf_op jit(solution)/shard_map/ppermute | solution.py:241
  189.3 5.9 collective-permute-done.6
  196.1 14.8 %fusion.78 = bf16[1024,1152]{0,1:T(8,128)(2,1)} fusion(bf16[288,512]{1,0:T(8,128)(2,1)S(1)} %get-tuple-element.95, bf16[288,512]{1,0:T(8,128)(2,1)S(1)} %get-tuple-element.94, bf16[288,512]{1,0:T(8,128)(2,1)S(1)} %get-tuple-element.93, bf16[288,512]{1,0:T(8,128)(2,1)S(1)} %get-tuple-element.92, bf16[288,512]{1,0:T(8,128)(2,1)S(1)} %get-tuple-element.91, ...), kind=kLoop, calls=%fused_computation.181 | loop fusion | flops 18874368 | bytes 4718592 | tf_op jit(solution)/shard_map/dot_general | solution.py:36
  210.9 4.6 copy.143
  215.6 9.2 %fusion.82 = (f32[2,512]{1,0:T(2,128)S(1)}, f32[2,512,1152]{2,1,0:T(8,128)S(1)}, f32[2,512]{1,0:T(2,128)}, f32[2,512,1152]{2,1,0:T(8,128)}) fusion(f32[2,1152]{1,0:T(2,128)S(1)} %copy-done.56, bf16[2,512,1152]{2,1,0:T(8,128)(2,1)S(1)} %copy-done.6, f32[2,512]{1,0:T(2,128)S(1)} %broadcast_multiply_fusion.3, bf16[2,512,1152]{2,1,0:T(8,128)(2,1)} %bitcast.152, ...), kind=kOutput, calls=%fused_computation.183 | convolution fusion | flops 2726164480 | bytes 16831488 | tf_op jit(solution)/shard_map/dot_general | solution.py:36
  228.1 2.4 fusion.26
  230.5 18.9 %fusion.90 = f32[1024,4608]{1,0:T(8,128)} fusion(bf16[1024,1152]{1,0:T(8,128)(2,1)S(1)} %bitcast.146, bf16[1152,4608]{1,0:T(8,128)(2,1)} %all-gather.11.cloned.1.call-done), kind=kOutput, calls=%fused_computation.189 | convolution fusion | flops 10871635968 | bytes 31850496 | tf_op jit(solution)/shard_map/dot_general | solution.py:36
  249.4 21.3 %convolution_convert_fusion.1 = bf16[4608,1152]{1,0:T(8,128)(2,1)} fusion(bf16[1024,1152]{1,0:T(8,128)(2,1)S(1)} %bitcast.149, f32[1024,4608]{1,0:T(8,128)} %fusion.90), kind=kOutput, calls=%fused_computation.3 | convolution fusion | flops 10919411712 | bytes 31850496 | tf_op jit(solution)/shard_map/dot_general | solution.py:36
  270.7 33.7 %all-gather.13.cloned.1.call-done = bf16[4608,1152]{1,0:T(8,128)(2,1)} async-done(((bf16[576,1152]{1,0:T(8,128)(2,1)}), bf16[4608,1152]{1,0:T(8,128)(2,1)}) %all-gather.13.cloned.1.call-update) | async-done | bytes 10616848 | tf_op jit(solution)/shard_map/all_gather | solution.py:269
  304.4 25.6 %fusion.8 = bf16[1024,4608]{1,0:T(8,128)(2,1)S(1)} fusion(f32[1024,4608]{1,0:T(8,128)} %fusion.90, bf16[1024,1152]{1,0:T(8,128)(2,1)} %bitcast.148, bf16[4608,1152]{1,0:T(8,128)(2,1)} %all-gather.13.cloned.1.call-done), kind=kOutput, calls=%fused_computation.12 | convolution fusion | flops 10961289216 | bytes 41287680 | tf_op jit(solution)/shard_map/dot_general | solution.py:36
  330.0 3.6 copy-done.67
  333.6 13.5 %convolution_convert_fusion = bf16[1152,4608]{1,0:T(8,128)(2,1)} fusion(bf16[1024,1152]{1,0:T(8,128)(2,1)S(1)} %bitcast.147, bf16[1024,4608]{1,0:T(8,128)(2,1)S(1)} %fusion.8), kind=kOutput, calls=%fused_computation.2 | convolution fusion | flops 10876944384 | bytes 22413312 | tf_op jit(solution)/shard_map/dot_general | solution.py:36
  347.1 19.9 %fusion.28 = (f32[1024]{0:T(1024)S(1)}, f32[1024,1152]{1,0:T(8,128)}) fusion(f32[2,1152]{1,0:T(2,128)S(1)} %get-tuple-element.98, bf16[1024,4608]{1,0:T(8,128)(2,1)} %copy-done.67, bf16[1152,4608]{1,0:T(8,128)(2,1)} %all-gather.11.cloned.1.call-done), kind=kOutput, calls=%fused_computation.47 | convolution fusion | flops 10873994240 | bytes 24785920 | tf_op jit(solution)/shard_map/dot_general | solution.py:36
  367.0 6.7 fusion.29
  373.8 24.1 %fusion.81 = f32[1024,1152]{1,0:T(8,128)} fusion(bf16[4608,1152]{1,0:T(8,128)(2,1)} %all-gather.13.cloned.1.call-done, f32[1024,4608]{1,0:T(8,128)} %fusion.90), kind=kOutput, calls=%fused_computation.182 | convolution fusion | flops 10914103296 | bytes 34209792 | tf_op jit(solution)/shard_map/dot_general | solution.py:36
  398.0 6.5 multiply_reduce_fusion
  407.8 19.2 %convolution_convert_fusion.2 = bf16[1152,1152]{1,0:T(8,128)(2,1)S(1)} fusion(bf16[1024,1152]{1,0:T(8,128)(2,1)S(1)} %bitcast.150, bf16[288,512]{1,0:T(8,128)(2,1)S(1)} %copy-done.36, bf16[288,512]{1,0:T(8,128)(2,1)S(1)} %copy-done.34, bf16[288,512]{1,0:T(8,128)(2,1)S(1)} %copy-done.40, bf16[288,512]{1,0:T(8,128)(2,1)S(1)} %copy-done.38, ...), kind=kOutput, calls=%fused_computation.22 | convolution fusion | flops 2738110464 | bytes 7372800 | tf_op jit(solution)/shard_map/dot_general | solution.py:36
  427.0 3.5 convolution_convert_fusion.5
  436.4 23.7 %collective-permute-done.9 = bf16[1152,512]{1,0:T(8,128)(2,1)S(1)} collective-permute-done((bf16[1152,512]{1,0:T(8,128)(2,1)S(1)}, bf16[1152,512]{1,0:T(8,128)(2,1)S(1)}, u32[]{:S(2)}, u32[]{:S(2)}) %collective-permute-start.9) | collective-permute-done | bytes 1179680 | tf_op jit(solution)/shard_map/ppermute | solution.py:233
  461.8 14.3 %all-gather = f32[8,2,4608]{2,1,0:T(2,128)S(1)} all-gather(f32[1,2,4608]{2,1,0:T(2,128)S(1)} %add_bitcast_fusion), channel_id=1, replica_groups=mesh['dp'=8,'seq'=4] {'dp'}, dimensions={0}, use_global_device_ids=true | all-gather | bytes 331776 | tf_op jit(solution)/shard_map/all_gather | solution.py:269
  479.9 53.4 %attend_back.2.refs_0_ = bf16[6,4,72,2048]{3,2,1,0:T(8,128)(2,1)S(1)} custom-call(bf16[24,72,2048]{2,1,0:T(8,128)(2,1)} %bitcast.121, bf16[24,72,2048]{2,1,0:T(8,128)(2,1)} %bitcast.122, bf16[24,72,2048]{2,1,0:T(8,128)(2,1)} %bitcast.123, bf16[8,72,2048]{2,1,0:T(8,128)(2,1)S(1)} %bitcast.113, f32[4,1,2048]{2,1,0:T(1,128)S(1)} %get-tuple-element.27.l_ref), custom_call_target="tpu_custom_call" | custom-call | flops 33822867456 | bytes 9437184 | tf_op jit(solution)/shard_map/attend_back/pallas_call | solution.py:199
  533.3 3.0 copy-done.1
  537.6 3.1 copy-done.2
  540.7 53.7 %attend_back.3 = bf16[6,4,72,2048]{3,2,1,0:T(8,128)(2,1)S(1)} custom-call(bf16[24,72,2048]{2,1,0:T(8,128)(2,1)} %bitcast.124, bf16[24,72,2048]{2,1,0:T(8,128)(2,1)} %bitcast.125, bf16[24,72,2048]{2,1,0:T(8,128)(2,1)} %bitcast.126, bf16[8,72,2048]{2,1,0:T(8,128)(2,1)S(1)} %bitcast.114, ...), custom_call_target="tpu_custom_call", output_to_operand_aliasing={{}: (5, {})} | custom-call | flops 33822867456 | bytes 9437184 | tf_op jit(solution)/shard_map/attend_back/pallas_call | solution.py:199
  594.5 3.0 copy-done.3
  599.5 2.8 fusion.92
  602.3 5.2 collective-permute-done.22
  608.4 16.3 %reduce-scatter.5.cloned.1.call-done = bf16[576,1152]{1,0:T(8,128)(2,1)} async-done(((bf16[4608,1152]{1,0:T(8,128)(2,1)}), bf16[576,1152]{1,0:T(8,128)(2,1)}) %reduce-scatter.5.cloned.1.call-update) | async-done | bytes 1327120 | tf_op jit(solution)/shard_map/reduce_scatter | solution.py:273
  624.7 6.5 convolution_convert_fusion.6
  634.2 16.2 %convolution_convert_fusion.4 = bf16[1152,1728]{1,0:T(8,128)(2,1)} fusion(bf16[1728,2048]{1,0:T(8,128)(2,1)} %bitcast.128, f32[1152]{0:T(1024)S(1)} %copy-done.63, f32[1152]{0:T(1024)S(1)} %copy-done.62, f32[2048]{0:T(1024)S(1)} %copy-done.64, f32[2048]{0:T(1024)S(1)} %copy-done.59, bf16[512,1152]{1,0:T(8,128)(2,1)} %collective-permute-done.2, ...), kind=kOutput, calls=%fused_computation.24 | convolution fusion | flops 8186388480 | bytes 15803392 | tf_op jit(solution)/shard_map/dot_general | solution.py:36
  650.4 85.7 %reduce-scatter.11.cloned.1.call-done = bf16[144,4608]{1,0:T(8,128)(2,1)} async-done(((bf16[1152,4608]{1,0:T(8,128)(2,1)}), bf16[144,4608]{1,0:T(8,128)(2,1)}) %reduce-scatter.11.cloned.1.call-update) | async-done | bytes 1327120 | tf_op jit(solution)/shard_map/reduce_scatter | solution.py:273
  737.6 5.3 convolution_convert_fusion.7
  744.4 4.1 add_convert_fusion.1
  749.5 2.9 fusion.31
  753.0 15.3 %collective-permute-done.23 = bf16[144,4608]{1,0:T(8,128)(2,1)S(1)} collective-permute-done((bf16[144,4608]{1,0:T(8,128)(2,1)}, bf16[144,4608]{1,0:T(8,128)(2,1)S(1)}, u32[]{:S(2)}, u32[]{:S(2)}) %collective-permute-start.23) | collective-permute-done | bytes 1327136 | tf_op jit(solution)/shard_map/ppermute | solution.py:233
  771.8 18.8 %collective-permute-done.16 = bf16[512,1152]{1,0:T(8,128)(2,1)S(1)} collective-permute-done((bf16[512,1152]{1,0:T(8,128)(2,1)S(1)}, bf16[512,1152]{1,0:T(8,128)(2,1)S(1)}, u32[]{:S(2)}, u32[]{:S(2)}) %collective-permute-start.16) | collective-permute-done | bytes 1179680 | tf_op jit(solution)/shard_map/ppermute | solution.py:233
  790.6 4.2 fusion.32
  794.8 2.5 fusion.24
  798.9 2.3 collective-permute-done.17
  802.7 3.2 fusion.23
  805.9 20.0 %collective-permute-done.18 = f32[2,2304]{1,0:T(2,128)S(1)} collective-permute-done((f32[2,2304]{1,0:T(2,128)S(1)}, f32[2,2304]{1,0:T(2,128)S(1)}, u32[]{:S(2)}, u32[]{:S(2)}) %collective-permute-start.18) | collective-permute-done | bytes 18464 | tf_op jit(solution)/shard_map/ppermute | solution.py:241
  825.9 15.5 %all-gather.1 = f32[8,2,2304]{2,1,0:T(2,128)} all-gather(f32[1,2,2304]{2,1,0:T(2,128)S(1)} %add_bitcast_fusion.1), channel_id=1, replica_groups=mesh['dp'=8,'seq'=4] {'dp'}, dimensions={0}, use_global_device_ids=true | all-gather | bytes 165888 | tf_op jit(solution)/shard_map/all_gather | solution.py:269
  845.0 3.6 all-to-all-start.2
  849.3 3.9 pad_maximum_fusion.2
  855.4 3.8 convert_add_fusion.2
  859.2 9.4 %collective-permute-done.19 = bf16[144,1728]{1,0:T(8,128)(2,1)S(1)} collective-permute-done((bf16[144,1728]{1,0:T(8,128)(2,1)}, bf16[144,1728]{1,0:T(8,128)(2,1)S(1)}, u32[]{:S(2)}, u32[]{:S(2)}) %collective-permute-start.19) | collective-permute-done | bytes 497696 | tf_op jit(solution)/shard_map/ppermute | solution.py:233
  870.4 3.3 convert_add_fusion.4
  873.7 7.7 collective-permute-done.20
  883.7 1.9 fusion.83
  (293 shorter events, 77.0 us)
Async XLA Ops:
  7.2 89.0 %all-gather.9.cloned.1.call-start = ((), (), s32[]{:S(2)}) async-start(), calls=%async_computation.8 | async-start | bytes 2985984 | tf_op jit(solution)/shard_map/all_gather | solution.py:269
  7.9 95.2 %all-gather.7.cloned.1.call-start = ((), (), s32[]{:S(2)}) async-start(), calls=%async_computation.7 | async-start | bytes 4644864 | tf_op jit(solution)/shard_map/all_gather | solution.py:269
  10.8 219.8 %all-gather.11.cloned.1.call-start = ((), (), s32[]{:S(2)}) async-start(), calls=%async_computation.9 | async-start | bytes 11943936 | tf_op jit(solution)/shard_map/all_gather | solution.py:269
  12.7 90.4 %copy-start.10 = (bf16[512,1152]{1,0:T(8,128)(2,1)}, bf16[512,1152]{1,0:T(8,128)(2,1)S(1)}, u32[]{:S(2)}) copy-start(bf16[512,1152]{1,0:T(8,128)(2,1)S(1)} %get-tuple-element.58) | copy-start | bytes 3538948
  12.7 29.2 %collective-permute-start = (bf16[512,1152]{1,0:T(8,128)(2,1)}, bf16[512,1152]{1,0:T(8,128)(2,1)}, u32[]{:S(2)}, u32[]{:S(2)}) collective-permute-start(bf16[512,1152]{1,0:T(8,128)(2,1)} %get-tuple-element.59), channel_id=1, source_target_pairs={{0,1},{1,0},{2,3},{3,2},{4,5},{5,4},{6,7},{7,6},{8,9},{9,8},{10,11... | collective-permute-start | bytes 3538952 | tf_op jit(solution)/shard_map/ppermute | solution.py:233
  29.8 25.0 %all-to-all-start.1 = ((f32[8,2,6912]{2,1,0:T(2,128)}), f32[8,2,6912]{2,1,0:T(2,128)}, u32[]{:S(2)}, u32[]{:S(2)}) async-start(f32[8,2,6912]{2,1,0:T(2,128)} %copy.142), calls=%async_computation.1 | async-start | bytes 884736 | tf_op jit(solution)/shard_map/all_to_all | solution.py:298
  33.9 270.5 %all-gather.13.cloned.1.call-start = ((), (), s32[]{:S(2)}) async-start(), calls=%async_computation.10 | async-start | bytes 11943936 | tf_op jit(solution)/shard_map/all_gather | solution.py:269
  34.0 29.0 %collective-permute-start.1 = (bf16[512,1152]{1,0:T(8,128)(2,1)S(1)}, bf16[512,1152]{1,0:T(8,128)(2,1)}, u32[]{:S(2)}, u32[]{:S(2)}) collective-permute-start(bf16[512,1152]{1,0:T(8,128)(2,1)S(1)} %get-tuple-element.58), channel_id=1, source_target_pairs={{0,2},{1,3},{2,0},{3,1},{4,6},{5,7},{6,4},{7,5},{8,10},{9,11},{10,... | collective-permute-start | bytes 3538952 | tf_op jit(solution)/shard_map/ppermute | solution.py:241
  42.0 45.6 %collective-permute-start.2 = (bf16[512,1152]{1,0:T(8,128)(2,1)}, bf16[512,1152]{1,0:T(8,128)(2,1)}, u32[]{:S(2)}, u32[]{:S(2)}) collective-permute-start(bf16[512,1152]{1,0:T(8,128)(2,1)} %collective-permute-done), channel_id=1, source_target_pairs={{0,2},{1,3},{2,0},{3,1},{4,6},{5,7},{6,4},{7,5},{8,10},{9,11},{10,... | collective-permute-start | bytes 3538952 | tf_op jit(solution)/shard_map/ppermute | solution.py:241
  43.8 492.5 %reduce-scatter.9.cloned.1.call-start = ((), (), s32[]{:S(2)}) async-start(), calls=%async_computation.13 | async-start | bytes 2985984 | tf_op jit(solution)/shard_map/reduce_scatter | solution.py:273
  44.8 170.7 %copy-start.53 = (f32[2,512]{1,0:T(2,128)}, f32[2,512]{1,0:T(2,128)S(1)}, u32[]{:S(2)}) copy-start(f32[2,512]{1,0:T(2,128)S(1)} %broadcast_multiply_fusion.3) | copy-start | bytes 12292
  117.6 28.8 %copy-start = (bf16[1728,2048]{1,0:T(8,128)(2,1)}, bf16[1728,2048]{1,0:T(8,128)(2,1)S(1)}, u32[]{:S(2)}) copy-start(bf16[1728,2048]{1,0:T(8,128)(2,1)S(1)} %convolution_convert_fusion.3) | copy-start | bytes 21233668
  143.4 33.5 %collective-permute-start.4 = (bf16[288,512]{1,0:T(8,128)(2,1)S(1)}, bf16[288,512]{1,0:T(8,128)(2,1)S(1)}, u32[]{:S(2)}, u32[]{:S(2)}) collective-permute-start(bf16[288,512]{1,0:T(8,128)(2,1)S(1)} %slice.189), channel_id=1, source_target_pairs={{0,1},{1,0},{2,3},{3,2},{4,5},{5,4},{6,7},{7,6},{8,9},{9,8},{10,11... | collective-permute-start | bytes 884744 | tf_op jit(solution)/shard_map/ppermute | solution.py:233
  144.9 28.6 %copy-start.19 = (bf16[1,576,1152]{2,1,0:T(8,128)(2,1)S(1)}, bf16[1,576,1152]{2,1,0:T(8,128)(2,1)}, u32[]{:S(2)}) copy-start(bf16[1,576,1152]{2,1,0:T(8,128)(2,1)} %get-tuple-element.52) | copy-start | bytes 3981316
  144.9 28.6 %copy-start.20 = (bf16[1,576,1152]{2,1,0:T(8,128)(2,1)S(1)}, bf16[1,576,1152]{2,1,0:T(8,128)(2,1)}, u32[]{:S(2)}) copy-start(bf16[1,576,1152]{2,1,0:T(8,128)(2,1)} %get-tuple-element.53) | copy-start | bytes 3981316
  144.9 30.4 %collective-permute-start.7 = (bf16[288,1024]{1,0:T(8,128)(2,1)S(1)}, bf16[288,1024]{1,0:T(8,128)(2,1)S(1)}, u32[]{:S(2)}, u32[]{:S(2)}) collective-permute-start(bf16[288,1024]{1,0:T(8,128)(2,1)S(1)} %bitcast.159), channel_id=1, source_target_pairs={{0,2},{1,3},{2,0},{3,1},{4,6},{5,7},{6,4},{7,5},{8,10},{9,11},{10,... | collective-permute-start | bytes 1769480 | tf_op jit(solution)/shard_map/ppermute | solution.py:241
  172.3 16.8 %collective-permute-start.3 = (bf16[288,512]{1,0:T(8,128)(2,1)S(1)}, bf16[288,512]{1,0:T(8,128)(2,1)S(1)}, u32[]{:S(2)}, u32[]{:S(2)}) collective-permute-start(bf16[288,512]{1,0:T(8,128)(2,1)S(1)} %slice.187), channel_id=1, source_target_pairs={{0,1},{1,0},{2,3},{3,2},{4,5},{5,4},{6,7},{7,6},{8,9},{9,8},{10,11... | collective-permute-start | bytes 884744 | tf_op jit(solution)/shard_map/ppermute | solution.py:233
  172.9 14.6 %collective-permute-start.5 = (bf16[288,1024]{1,0:T(8,128)(2,1)S(1)}, bf16[288,1024]{1,0:T(8,128)(2,1)S(1)}, u32[]{:S(2)}, u32[]{:S(2)}) collective-permute-start(bf16[288,1024]{1,0:T(8,128)(2,1)S(1)} %bitcast.158), channel_id=1, source_target_pairs={{0,2},{1,3},{2,0},{3,1},{4,6},{5,7},{6,4},{7,5},{8,10},{9,11},{10,... | collective-permute-start | bytes 1769480 | tf_op jit(solution)/shard_map/ppermute | solution.py:241
  175.3 13.9 %collective-permute-start.8 = (bf16[288,512]{1,0:T(8,128)(2,1)S(1)}, bf16[288,512]{1,0:T(8,128)(2,1)S(1)}, u32[]{:S(2)}, u32[]{:S(2)}) collective-permute-start(bf16[288,512]{1,0:T(8,128)(2,1)S(1)} %slice.193), channel_id=1, source_target_pairs={{0,1},{1,0},{2,3},{3,2},{4,5},{5,4},{6,7},{7,6},{8,9},{9,8},{10,11... | collective-permute-start | bytes 884744 | tf_op jit(solution)/shard_map/ppermute | solution.py:233
  187.6 7.6 collective-permute-start.6
  196.1 19.5 %copy-start.56 = (f32[2,1152]{1,0:T(2,128)S(1)}, f32[2,1152]{1,0:T(2,128)}, u32[]{:S(2)}) copy-start(f32[2,1152]{1,0:T(2,128)} %get-tuple-element.100) | copy-start | bytes 27652
  347.1 19.9 %copy-start.45 = (f32[2,512]{1,0:T(2,128)S(1)}, f32[2,512]{1,0:T(2,128)}, u32[]{:S(2)}) copy-start(f32[2,512]{1,0:T(2,128)} %copy-done.44) | copy-start | bytes 12292
  347.1 19.9 %copy-start.52 = (f32[2,512]{1,0:T(2,128)S(1)}, f32[2,512]{1,0:T(2,128)}, u32[]{:S(2)}) copy-start(f32[2,512]{1,0:T(2,128)} %copy-done.51) | copy-start | bytes 12292
  367.0 30.9 %slice-start = ((s8[4718592]{0:T(1024)(128)(4,1)}), s8[4194304]{0:T(1024)(128)(4,1)S(1)}, s32[]{:S(2)}) async-start(s8[4718592]{0:T(1024)(128)(4,1)} %bitcast.132), calls=%async_computation.15 | async-start | bytes 8388608
  367.0 30.9 %slice-start.4 = ((s8[4718592]{0:T(1024)(128)(4,1)}), s8[4194304]{0:T(1024)(128)(4,1)S(1)}, s32[]{:S(2)}) async-start(s8[4718592]{0:T(1024)(128)(4,1)} %bitcast.137), calls=%async_computation.19 | async-start | bytes 8388608
  367.0 30.9 %slice-start.6 = ((s8[4718592]{0:T(1024)(128)(4,1)}), s8[4194304]{0:T(1024)(128)(4,1)S(1)}, s32[]{:S(2)}) async-start(s8[4718592]{0:T(1024)(128)(4,1)} %bitcast.140), calls=%async_computation.21 | async-start | bytes 8388608
  373.8 24.2 %slice-start.1 = ((s8[4718592]{0:T(1024)(128)(4,1)}), s8[524288]{0:T(1024)(128)(4,1)S(1)}, s32[]{:S(2)}) async-start(s8[4718592]{0:T(1024)(128)(4,1)} %bitcast.132), calls=%async_computation.16 | async-start | bytes 1048576
  373.8 24.2 %slice-start.5 = ((s8[4718592]{0:T(1024)(128)(4,1)}), s8[524288]{0:T(1024)(128)(4,1)S(1)}, s32[]{:S(2)}) async-start(s8[4718592]{0:T(1024)(128)(4,1)} %bitcast.137), calls=%async_computation.20 | async-start | bytes 1048576
  373.8 24.2 %copy-start.13 = (bf16[2,512,1152]{2,1,0:T(8,128)(2,1)S(1)}, bf16[2,512,1152]{2,1,0:T(8,128)(2,1)}, u32[]{:S(2)}) copy-start(bf16[2,512,1152]{2,1,0:T(8,128)(2,1)} %param.15) | copy-start | bytes 7077892
  373.8 24.2 %slice-start.7 = ((s8[4718592]{0:T(1024)(128)(4,1)}), s8[524288]{0:T(1024)(128)(4,1)S(1)}, s32[]{:S(2)}) async-start(s8[4718592]{0:T(1024)(128)(4,1)} %bitcast.140), calls=%async_computation.22 | async-start | bytes 1048576
  373.8 24.2 %copy-start.48 = (f32[2,1152]{1,0:T(2,128)S(1)}, f32[2,1152]{1,0:T(2,128)}, u32[]{:S(2)}) copy-start(f32[2,1152]{1,0:T(2,128)} %get-tuple-element.97) | copy-start | bytes 27652
  404.5 22.5 %copy-start.5 = (f32[2,512,1152]{2,1,0:T(8,128)}, f32[2,512,1152]{2,1,0:T(8,128)S(1)}, u32[]{:S(2)}) copy-start(f32[2,512,1152]{2,1,0:T(8,128)S(1)} %get-tuple-element.44) | copy-start | bytes 14155780
  404.6 31.1 %collective-permute-start.12 = (f32[2,4608]{1,0:T(2,128)S(1)}, f32[2,4608]{1,0:T(2,128)S(1)}, u32[]{:S(2)}, u32[]{:S(2)}) collective-permute-start(f32[2,4608]{1,0:T(2,128)S(1)} %pad_maximum_fusion.7), channel_id=1, source_target_pairs={{0,1},{1,0},{2,3},{3,2},{4,5},{5,4},{6,7},{7,6},{8,9},{9,8},{10,11... | collective-permute-start | bytes 110600 | tf_op jit(solution)/shard_map/ppermute | solution.py:233
  430.8 45.5 %collective-permute-start.11 = (bf16[576,512]{1,0:T(8,128)(2,1)S(1)}, bf16[576,512]{1,0:T(8,128)(2,1)S(1)}, u32[]{:S(2)}, u32[]{:S(2)}) collective-permute-start(bf16[576,512]{1,0:T(8,128)(2,1)S(1)} %get-tuple-element.73), channel_id=1, source_target_pairs={{0,2},{1,3},{2,0},{3,1},{4,6},{5,7},{6,4},{7,5},{8,10},{9,11},{10,... | collective-permute-start | bytes 1769480 | tf_op jit(solution)/shard_map/ppermute | solution.py:241
  432.3 27.8 %collective-permute-start.9 = (bf16[1152,512]{1,0:T(8,128)(2,1)S(1)}, bf16[1152,512]{1,0:T(8,128)(2,1)S(1)}, u32[]{:S(2)}, u32[]{:S(2)}) collective-permute-start(bf16[1152,512]{1,0:T(8,128)(2,1)S(1)} %get-tuple-element.56), channel_id=1, source_target_pairs={{0,1},{1,0},{2,3},{3,2},{4,5},{5,4},{6,7},{7,6},{8,9},{9,8},{10,11... | collective-permute-start | bytes 3538952 | tf_op jit(solution)/shard_map/ppermute | solution.py:233
  435.8 26.0 %collective-permute-start.13 = (f32[2,4608]{1,0:T(2,128)S(1)}, f32[2,4608]{1,0:T(2,128)S(1)}, u32[]{:S(2)}, u32[]{:S(2)}) collective-permute-start(f32[2,4608]{1,0:T(2,128)S(1)} %fusion.118), channel_id=1, source_target_pairs={{0,2},{1,3},{2,0},{3,1},{4,6},{5,7},{6,4},{7,5},{8,10},{9,11},{10,... | collective-permute-start | bytes 110600 | tf_op jit(solution)/shard_map/ppermute | solution.py:241
  461.2 15.1 %collective-permute-start.10 = (bf16[576,512]{1,0:T(8,128)(2,1)}, bf16[576,512]{1,0:T(8,128)(2,1)S(1)}, u32[]{:S(2)}, u32[]{:S(2)}) collective-permute-start(bf16[576,512]{1,0:T(8,128)(2,1)} %get-tuple-element.75), channel_id=1, source_target_pairs={{0,2},{1,3},{2,0},{3,1},{4,6},{5,7},{6,4},{7,5},{8,10},{9,11},{10,... | collective-permute-start | bytes 1769480 | tf_op jit(solution)/shard_map/ppermute | solution.py:241
  476.3 123.2 %copy-start.21 = (f32[16,4608]{1,0:T(8,128)}, f32[16,4608]{1,0:T(8,128)S(1)}, u32[]{:S(2)}) copy-start(f32[16,4608]{1,0:T(8,128)S(1)} %reshape.188) | copy-start | bytes 884740
  476.4 148.4 %reduce-scatter.5.cloned.1.call-start = ((), (), s32[]{:S(2)}) async-start(), calls=%async_computation.11 | async-start | bytes 11943936 | tf_op jit(solution)/shard_map/reduce_scatter | solution.py:273
  477.4 258.8 %reduce-scatter.11.cloned.1.call-start = ((), (), s32[]{:S(2)}) async-start(), calls=%async_computation.14 | async-start | bytes 11943936 | tf_op jit(solution)/shard_map/reduce_scatter | solution.py:273
  478.1 376.9 %reduce-scatter.7.cloned.1.call-start = ((), (), s32[]{:S(2)}) async-start(), calls=%async_computation.12 | async-start | bytes 4644864 | tf_op jit(solution)/shard_map/reduce_scatter | solution.py:273
  536.3 61.2 %collective-permute-start.21 = (bf16[144,1152]{1,0:T(8,128)(2,1)}, bf16[144,1152]{1,0:T(8,128)(2,1)S(1)}, u32[]{:S(2)}, u32[]{:S(2)}) collective-permute-start(bf16[144,1152]{1,0:T(8,128)(2,1)} %reduce-scatter.9.cloned.1.call-done), channel_id=1, source_target_pairs={{0,1},{1,0},{2,3},{3,2},{4,5},{5,4},{6,7},{7,6},{8,9},{9,8},{10,11... | collective-permute-start | bytes 995336 | tf_op jit(solution)/shard_map/ppermute | solution.py:233
  540.7 56.7 %copy-start.24 = (bf16[144,1152]{1,0:T(8,128)(2,1)S(1)}, bf16[144,1152]{1,0:T(8,128)(2,1)}, u32[]{:S(2)}) copy-start(bf16[144,1152]{1,0:T(8,128)(2,1)} %reduce-scatter.9.cloned.1.call-done) | copy-start | bytes 995332
  540.7 58.4 %copy-start.8 = (bf16[144,6912]{1,0:T(8,128)(2,1)S(1)}, bf16[144,6912]{1,0:T(8,128)(2,1)}, u32[]{:S(2)}) copy-start(bf16[144,6912]{1,0:T(8,128)(2,1)} %param.10) | copy-start | bytes 5971972
  597.5 9.9 %collective-permute-start.22 = (bf16[144,1152]{1,0:T(8,128)(2,1)S(1)}, bf16[144,1152]{1,0:T(8,128)(2,1)S(1)}, u32[]{:S(2)}, u32[]{:S(2)}) collective-permute-start(bf16[144,1152]{1,0:T(8,128)(2,1)S(1)} %fusion.57), channel_id=1, source_target_pairs={{0,2},{1,3},{2,0},{3,1},{4,6},{5,7},{6,4},{7,5},{8,10},{9,11},{10,... | collective-permute-start | bytes 995336 | tf_op jit(solution)/shard_map/ppermute | solution.py:241
  631.2 113.2 %collective-permute-start.15 = (bf16[512,1152]{1,0:T(8,128)(2,1)}, bf16[512,1152]{1,0:T(8,128)(2,1)S(1)}, u32[]{:S(2)}, u32[]{:S(2)}) collective-permute-start(bf16[512,1152]{1,0:T(8,128)(2,1)} %convolution_convert_fusion.6), channel_id=1, source_target_pairs={{0,2},{1,3},{2,0},{3,1},{4,6},{5,7},{6,4},{7,5},{8,10},{9,11},{10,... | collective-permute-start | bytes 3538952 | tf_op jit(solution)/shard_map/ppermute | solution.py:241
  632.7 116.8 %collective-permute-start.25 = (bf16[576,1152]{1,0:T(8,128)(2,1)S(1)}, bf16[576,1152]{1,0:T(8,128)(2,1)}, u32[]{:S(2)}, u32[]{:S(2)}) collective-permute-start(bf16[576,1152]{1,0:T(8,128)(2,1)S(1)} %copy-done.15), channel_id=1, source_target_pairs={{0,1},{1,0},{2,3},{3,2},{4,5},{5,4},{6,7},{7,6},{8,9},{9,8},{10,11... | collective-permute-start | bytes 3981320 | tf_op jit(solution)/shard_map/ppermute | solution.py:233
  736.1 32.2 %collective-permute-start.23 = (bf16[144,4608]{1,0:T(8,128)(2,1)}, bf16[144,4608]{1,0:T(8,128)(2,1)S(1)}, u32[]{:S(2)}, u32[]{:S(2)}) collective-permute-start(bf16[144,4608]{1,0:T(8,128)(2,1)} %reduce-scatter.11.cloned.1.call-done), channel_id=1, source_target_pairs={{0,1},{1,0},{2,3},{3,2},{4,5},{5,4},{6,7},{7,6},{8,9},{9,8},{10,11... | collective-permute-start | bytes 3981320 | tf_op jit(solution)/shard_map/ppermute | solution.py:233
  742.9 28.9 %collective-permute-start.14 = (bf16[512,1152]{1,0:T(8,128)(2,1)S(1)}, bf16[512,1152]{1,0:T(8,128)(2,1)S(1)}, u32[]{:S(2)}, u32[]{:S(2)}) collective-permute-start(bf16[512,1152]{1,0:T(8,128)(2,1)S(1)} %convolution_convert_fusion.7), channel_id=1, source_target_pairs={{0,2},{1,3},{2,0},{3,1},{4,6},{5,7},{6,4},{7,5},{8,10},{9,11},{10,... | collective-permute-start | bytes 3538952 | tf_op jit(solution)/shard_map/ppermute | solution.py:241
  748.5 19.8 %copy-start.14 = (bf16[144,4608]{1,0:T(8,128)(2,1)S(1)}, bf16[144,4608]{1,0:T(8,128)(2,1)}, u32[]{:S(2)}) copy-start(bf16[144,4608]{1,0:T(8,128)(2,1)} %reduce-scatter.11.cloned.1.call-done) | copy-start | bytes 3981316
  748.6 42.1 %collective-permute-start.16 = (bf16[512,1152]{1,0:T(8,128)(2,1)S(1)}, bf16[512,1152]{1,0:T(8,128)(2,1)S(1)}, u32[]{:S(2)}, u32[]{:S(2)}) collective-permute-start(bf16[512,1152]{1,0:T(8,128)(2,1)S(1)} %add_convert_fusion.1), channel_id=1, source_target_pairs={{0,1},{1,0},{2,3},{3,2},{4,5},{5,4},{6,7},{7,6},{8,9},{9,8},{10,11... | collective-permute-start | bytes 3538952 | tf_op jit(solution)/shard_map/ppermute | solution.py:233
  749.5 53.2 %slice-start.2 = ((s8[4718592]{0:T(1024)(128)(4,1)}), s8[4194304]{0:T(1024)(128)(4,1)S(1)}, s32[]{:S(2)}) async-start(s8[4718592]{0:T(1024)(128)(4,1)} %bitcast.134), calls=%async_computation.17 | async-start | bytes 8388608
  752.4 103.0 %collective-permute-start.26 = (bf16[576,1152]{1,0:T(8,128)(2,1)}, bf16[576,1152]{1,0:T(8,128)(2,1)}, u32[]{:S(2)}, u32[]{:S(2)}) collective-permute-start(bf16[576,1152]{1,0:T(8,128)(2,1)} %fusion.31), channel_id=1, source_target_pairs={{0,2},{1,3},{2,0},{3,1},{4,6},{5,7},{6,4},{7,5},{8,10},{9,11},{10,... | collective-permute-start | bytes 3981320 | tf_op jit(solution)/shard_map/ppermute | solution.py:241
  769.8 25.0 %copy-start.7 = (bf16[2,512,1152]{2,1,0:T(8,128)(2,1)S(1)}, bf16[2,512,1152]{2,1,0:T(8,128)(2,1)}, u32[]{:S(2)}) copy-start(bf16[2,512,1152]{2,1,0:T(8,128)(2,1)} %param.8) | copy-start | bytes 7077892
  769.8 25.0 %copy-start.46 = (f32[2,1152]{1,0:T(2,128)S(1)}, f32[2,1152]{1,0:T(2,128)}, u32[]{:S(2)}) copy-start(f32[2,1152]{1,0:T(2,128)} %get-tuple-element.96) | copy-start | bytes 27652
  769.8 25.0 %copy-start.54 = (f32[2,512]{1,0:T(2,128)S(1)}, f32[2,512]{1,0:T(2,128)}, u32[]{:S(2)}) copy-start(f32[2,512]{1,0:T(2,128)} %copy-done.53) | copy-start | bytes 12292
  769.8 32.9 %slice-start.3 = ((s8[4718592]{0:T(1024)(128)(4,1)}), s8[524288]{0:T(1024)(128)(4,1)S(1)}, s32[]{:S(2)}) async-start(s8[4718592]{0:T(1024)(128)(4,1)} %bitcast.134), calls=%async_computation.18 | async-start | bytes 1048576
  769.8 100.5 %collective-permute-start.24 = (bf16[144,4608]{1,0:T(8,128)(2,1)}, bf16[144,4608]{1,0:T(8,128)(2,1)}, u32[]{:S(2)}, u32[]{:S(2)}) collective-permute-start(bf16[144,4608]{1,0:T(8,128)(2,1)} %fusion.30), channel_id=1, source_target_pairs={{0,2},{1,3},{2,0},{3,1},{4,6},{5,7},{6,4},{7,5},{8,10},{9,11},{10,... | collective-permute-start | bytes 3981320 | tf_op jit(solution)/shard_map/ppermute | solution.py:241
  797.3 3.8 collective-permute-start.17
  801.2 41.2 %copy-start.9 = (bf16[144,6912]{1,0:T(8,128)(2,1)S(1)}, bf16[144,6912]{1,0:T(8,128)(2,1)}, u32[]{:S(2)}) copy-start(bf16[144,6912]{1,0:T(8,128)(2,1)} %param.10) | copy-start | bytes 5971972
  801.2 24.7 %collective-permute-start.18 = (f32[2,2304]{1,0:T(2,128)S(1)}, f32[2,2304]{1,0:T(2,128)S(1)}, u32[]{:S(2)}, u32[]{:S(2)}) collective-permute-start(f32[2,2304]{1,0:T(2,128)S(1)} %fusion.77), channel_id=1, source_target_pairs={{0,2},{1,3},{2,0},{3,1},{4,6},{5,7},{6,4},{7,5},{8,10},{9,11},{10,... | collective-permute-start | bytes 55304 | tf_op jit(solution)/shard_map/ppermute | solution.py:241
  845.0 9.2 %all-to-all-start.2 = ((f32[8,2,144]{2,1,0:T(2,128)}), f32[8,2,144]{2,1,0:T(2,128)S(1)}, u32[]{:S(2)}, u32[]{:S(2)}) async-start(f32[8,2,144]{2,1,0:T(2,128)} %all_to_all.15), calls=%async_computation.3 | async-start | bytes 32768 | tf_op jit(solution)/shard_map/all_to_all | solution.py:464
  855.0 13.6 %collective-permute-start.19 = (bf16[144,1728]{1,0:T(8,128)(2,1)}, bf16[144,1728]{1,0:T(8,128)(2,1)S(1)}, u32[]{:S(2)}, u32[]{:S(2)}) collective-permute-start(bf16[144,1728]{1,0:T(8,128)(2,1)} %reduce-scatter.7.cloned.1.call-done), channel_id=1, source_target_pairs={{0,1},{1,0},{2,3},{3,2},{4,5},{5,4},{6,7},{7,6},{8,9},{9,8},{10,11... | collective-permute-start | bytes 1493000 | tf_op jit(solution)/shard_map/ppermute | solution.py:233
  868.8 12.6 %collective-permute-start.20 = (bf16[144,1728]{1,0:T(8,128)(2,1)S(1)}, bf16[144,1728]{1,0:T(8,128)(2,1)S(1)}, u32[]{:S(2)}, u32[]{:S(2)}) collective-permute-start(bf16[144,1728]{1,0:T(8,128)(2,1)S(1)} %add_convert_fusion.2), channel_id=1, source_target_pairs={{0,2},{1,3},{2,0},{3,1},{4,6},{5,7},{6,4},{7,5},{8,10},{9,11},{10,... | collective-permute-start | bytes 1493000 | tf_op jit(solution)/shard_map/ppermute | solution.py:241
  (49 other events, 290.7 us)
Sparse Core Ops, SparseCore 0:
  9.6 45.5 all-gather.8
  57.4 45.6 all-gather.6
  104.8 99.2 all-gather.10
  205.6 98.7 all-gather.12
  476.5 36.2 reduce-scatter.8
  515.0 109.6 reduce-scatter.4
  627.0 109.0 reduce-scatter.10
  738.4 47.7 reduce-scatter.6

commit v3 on v2

--- a/solution.py
+++ b/solution.py
@@ -373,6 +373,7 @@
     grad_branch_one = (grad_residual * gate_one).astype(half).reshape(flat_rows, width)
     grad_attended = dot(proj_full, grad_branch_one, 1, 1).astype(half)
 
+    grad_attended, late_branch_one = lax.optimization_barrier((grad_attended, grad_branch_one))
     first, second = grad_attended[:, :tokens_here], grad_attended[:, tokens_here:]
     received = ex.across(ex.other(first, second))
     own = ex.mine(first, second)
@@ -381,19 +382,20 @@
         jnp.concatenate([grad_gate_one, grad_shift_two, grad_scale_two, grad_gate_two], axis=1)
     )
     own_moved = [ex.shift(own[by * span : (by + 1) * span], by) for by in range(1, groups)]
-    received, term_fc2 = lax.optimization_barrier((received, term_fc2))
     grad_fc2 = scatter_rows(term_fc2)
     received_moved = [ex.shift(received[by * span : (by + 1) * span], by) for by in range(1, groups)]
     term_fc1 = dot(normed_two, grad_pre, 0, 0).astype(half)
-    term_proj = dot(attended, grad_branch_one, 1, 0).astype(half)
+    grad_fc1 = scatter_rows(term_fc1)
+    term_proj = dot(attended, late_branch_one, 1, 0).astype(half)
     term_proj = ex.place(
         term_proj.reshape(groups, span, width), [(by - ex.group) % groups for by in range(groups)]
     ).reshape(width, width)
     early = gather_rows(early)
-    received_moved, own_moved, term_fc1, term_proj, early = lax.optimization_barrier(
-        (received_moved, own_moved, term_fc1, term_proj, early)
-    )
-    grad_fc1 = scatter_rows(term_fc1)
+    received_moved, own_moved, term_proj, early, grad_fc2 = lax.optimization_barrier(
+        (received_moved, own_moved, term_proj, early, grad_fc2)
+    )
+    grad_proj = scatter_rows(term_proj)
+    grad_fc2 = ex.over_sides(grad_fc2.astype(full)).astype(half)
     blocks = [own[:span], received[:span]]
     for by in range(1, groups):
         blocks += [own_moved[by - 1], received_moved[by - 1]]
@@ -401,12 +403,20 @@
 
     grad_packed = None
     for which in range(chunks):
+        if which:
+            grad_packed, grad_fc2, grad_fc1 = lax.optimization_barrier(
+                (grad_packed, grad_fc2, grad_fc1)
+            )
+            grad_fc2 = ex.over_groups(grad_fc2.astype(full))
+            grad_fc1 = ex.over_sides(grad_fc1.astype(full)).astype(half)
         grad_packed = attend_back(
             packed, grad_heads, log_totals[which], chunk_heads, which, grad_packed
         )
     grad_packed = grad_packed.reshape(3 * span, length)
-    grad_packed, grad_fc2 = lax.optimization_barrier((grad_packed, grad_fc2))
-    grad_fc2 = ex.total(grad_fc2)
+    grad_packed, grad_fc2, grad_fc1, grad_proj = lax.optimization_barrier(
+        (grad_packed, grad_fc2, grad_fc1, grad_proj)
+    )
+    grad_fc1 = ex.over_groups(grad_fc1.astype(full))
 
     def term_of(at):
         return dot(grad_packed[:, at * tokens_here : (at + 1) * tokens_here], qkv_full, 0, 1)
@@ -421,8 +431,7 @@
     grad_normed_one = jnp.stack([ex.mine(kept, received), ex.other(kept, received)])
 
     grad_qkv = scatter_rows(dot(normed_image, grad_packed, 0, 1).astype(half))
-    grad_proj = ex.total(scatter_rows(term_proj))
-    grad_fc1 = ex.total(grad_fc1)
+    grad_proj = ex.total(grad_proj)
     grad_qkv = ex.over_sides(grad_qkv.astype(full)).astype(half)
     grad_qkv = jnp.stack([grad_qkv] + [ex.shift(grad_qkv, by) for by in range(1, groups)])
     grad_qkv = ex.place(grad_qkv, [(ex.group - at) % groups for at in range(groups)])

time: 899 us -> 762 us (0.85)
  waiting for transfers between devices: 307 us -> 176 us
    reduce_scatter x4, waiting for transfers between devices: 102 us -> 1.57 us  [scatter_rows(): return lax.psum_scatter(term, 'dp', scatter_dimension=0, tiled=True)]
    ppermute x13, waiting for transfers between devices: 81.9 us -> 29.2 us  [across(): return lax.ppermute(value, 'seq', [(at, at ^ 1) for at in range(self.size)])]
    ppermute x14, waiting for transfers between devices: 72.1 us -> 96.7 us  [shift(): return lax.ppermute(value, 'seq', pairs)]
    unnamed x165 -> x167, local copies, waits for them, and re-layouts: 20.4 us -> 19.6 us
  transfers between devices with their start and end apart: 37 -> 37, of which waited for: 20 -> 16; matrix products, arithmetic and copies ran while one was open for 23% -> 39% of each run, Pallas kernels for 18% -> 21%
where the time goes in v3:
time: 762 us; the launch traced here: 759 us
  matrix products  208 us (27%)
  waiting for transfers between devices  176 us (23%)
  Pallas kernels  159 us (21%)
  other arithmetic  75.5 us (10%)
  blocking collectives  43 us (6%)
  starting transfers between devices  42.3 us (6%)
  local copies, waits for them, and re-layouts  39.1 us (5%)
  between operations  15.8 us (2%)
    dot_general x20, matrix products, dot(): lax.dot_general(former, latter, (((former_dim,), (latter_dim,)), ((), ())...  204 us
    pallas_call x2, Pallas kernels, attend_back(): pl.pallas_call(functools.partial(backward_kernel, rows, chunk), grid=(hea...  107 us
    ppermute x14, waiting for transfers between devices, shift(): return lax.ppermute(value, 'seq', pairs)  96.7 us
    pallas_call x2, Pallas kernels, attend(): pl.pallas_call(functools.partial(forward_kernel, rows, chunk), grid=(head...  51.8 us
    all_gather x4, waiting for transfers between devices, gather_rows(): return lax.all_gather(shard, 'dp', axis=0, tiled=True)  36.9 us
    all_gather x2, blocking collectives, gather_rows(): return lax.all_gather(shard, 'dp', axis=0, tiled=True)  32.6 us
    ppermute x13, waiting for transfers between devices, across(): return lax.ppermute(value, 'seq', [(at, at ^ 1) for at in range(self.size)])  29.2 us
    unnamed x167, local copies, waits for them, and re-layouts  19.6 us
  transfers between devices with their start and end apart: 37, of which 16 were waited for; matrix products, arithmetic and copies ran while one was open for 39% of the time, Pallas kernels for 21%

profile of v3, /device:TPU:0, one launch (start us, length us, event | category | flops | bytes accessed | tf_op | source)
XLA Modules:
  0.0 758.6 jit_solution(18371665048509506705)
XLA Ops:
  12.7 3.0 collective-permute-start
  15.9 10.4 %all_to_all.20 = bf16[8,2,144]{2,1,0:T(2,128)(2,1)S(1)} all-to-all(bf16[8,2,144]{2,1,0:T(2,128)(2,1)S(1)} %copy.140), channel_id=1, replica_groups=mesh['dp'=8,'seq'=4] {'dp'}, dimensions={0} | all-to-all | bytes 9216 | tf_op jit(solution)/shard_map/all_to_all | solution.py:295
  26.9 1.9 fusion.32
  29.8 4.1 all-to-all-start.1
  35.5 6.5 collective-permute-done
  44.6 10.3 %all-to-all-done.1 = f32[8,2,6912]{2,1,0:T(2,128)} async-done(((f32[8,2,6912]{2,1,0:T(2,128)}), f32[8,2,6912]{2,1,0:T(2,128)}, u32[]{:S(2)}, u32[]{:S(2)}) %all-to-all-start.1) | async-done | bytes 442400 | tf_op jit(solution)/shard_map/all_to_all | solution.py:298
  54.8 1.8 reduce_sum.153
  59.4 3.6 collective-permute-done.1
  63.0 24.6 %collective-permute-done.2 = bf16[512,1152]{1,0:T(8,128)(2,1)} collective-permute-done((bf16[512,1152]{1,0:T(8,128)(2,1)}, bf16[512,1152]{1,0:T(8,128)(2,1)}, u32[]{:S(2)}, u32[]{:S(2)}) %collective-permute-start.2) | collective-permute-done | bytes 1179680 | tf_op jit(solution)/shard_map/ppermute | solution.py:241
  87.6 3.2 convert_reduce_fusion
  91.4 4.1 fusion.11
  96.1 3.4 constant_dynamic-slice_fusion.3
  99.6 3.6 all-gather.7.cloned.1.call-done
  103.2 14.4 %convolution_convert_fusion.3 = bf16[1728,2048]{1,0:T(8,128)(2,1)S(1)} fusion(bf16[1152,1728]{1,0:T(8,128)(2,1)} %all-gather.7.cloned.1.call-done, f32[1152]{0:T(1024)} %get-tuple-element.52, f32[1152]{0:T(1024)} %get-tuple-element.51, f32[2048]{0:T(1024)} %add_rsqrt_fusion, f32[2048]{0:T(1024)} %copy-done.57, ...), kind=kOutput, calls=%fused_computation.23 | convolution fusion | flops 8187936768 | bytes 15803392 | tf_op jit(solution)/shard_map/dot_general | solution.py:36
  117.6 25.7 %attend.2 = (bf16[2,4,72,1024]{3,2,1,0:T(8,128)(2,1)S(1)}, f32[4,1,2048]{2,1,0:T(1,128)S(1)}) custom-call(bf16[24,72,2048]{2,1,0:T(8,128)(2,1)S(1)} %bitcast.115, bf16[24,72,2048]{2,1,0:T(8,128)(2,1)S(1)} %bitcast.116, bf16[24,72,2048]{2,1,0:T(8,128)(2,1)S(1)} %bitcast.117), custom_call_target="tpu_custom_call" | custom-call | flops 16911433728 | bytes 4718592 | tf_op jit(solution)/shard_map/attend/pallas_call | solution.py:100
  146.4 26.2 %attend.3 = (bf16[2,4,72,1024]{3,2,1,0:T(8,128)(2,1)S(1)}, f32[4,1,2048]{2,1,0:T(1,128)S(1)}) custom-call(bf16[24,72,2048]{2,1,0:T(8,128)(2,1)S(1)} %bitcast.118, bf16[24,72,2048]{2,1,0:T(8,128)(2,1)S(1)} %bitcast.119, bf16[24,72,2048]{2,1,0:T(8,128)(2,1)S(1)} %bitcast.120), custom_call_target="tpu_custom_call" | custom-call | flops 16911433728 | bytes 4718592 | tf_op jit(solution)/shard_map/attend/pallas_call | solution.py:100
  177.3 10.7 %collective-permute-done.7 = bf16[288,1024]{1,0:T(8,128)(2,1)S(1)} collective-permute-done((bf16[288,1024]{1,0:T(8,128)(2,1)S(1)}, bf16[288,1024]{1,0:T(8,128)(2,1)S(1)}, u32[]{:S(2)}, u32[]{:S(2)}) %collective-permute-start.7) | collective-permute-done | bytes 589856 | tf_op jit(solution)/shard_map/ppermute | solution.py:241
  189.6 5.9 collective-permute-done.8
  196.4 14.8 %fusion.76 = bf16[1024,1152]{0,1:T(8,128)(2,1)} fusion(bf16[288,512]{1,0:T(8,128)(2,1)S(1)} %get-tuple-element.105, bf16[288,512]{1,0:T(8,128)(2,1)S(1)} %get-tuple-element.104, bf16[288,512]{1,0:T(8,128)(2,1)S(1)} %get-tuple-element.103, bf16[288,512]{1,0:T(8,128)(2,1)S(1)} %get-tuple-element.102, bf16[288,512]{1,0:T(8,128)(2,1)S(1)} %get-tuple-element.101, ...), kind=kLoop, calls=%fused_computation.179 | loop fusion | flops 18874368 | bytes 4718592 | tf_op jit(solution)/shard_map/dot_general | solution.py:36
  211.2 4.6 copy.143
  215.8 9.2 %fusion.80 = (f32[2,512]{1,0:T(2,128)S(1)}, f32[2,512,1152]{2,1,0:T(8,128)S(1)}, f32[2,512]{1,0:T(2,128)}, f32[2,512,1152]{2,1,0:T(8,128)}) fusion(f32[2,1152]{1,0:T(2,128)S(1)} %copy-done.55, bf16[2,512,1152]{2,1,0:T(8,128)(2,1)S(1)} %copy-done.6, f32[2,512]{1,0:T(2,128)S(1)} %broadcast_multiply_fusion.3, bf16[2,512,1152]{2,1,0:T(8,128)(2,1)} %bitcast.154, ...), kind=kOutput, calls=%fused_computation.181 | convolution fusion | flops 2726164480 | bytes 16831488 | tf_op jit(solution)/shard_map/dot_general | solution.py:36
  228.4 2.4 fusion.26
  230.8 19.0 %fusion.88 = f32[1024,4608]{1,0:T(8,128)} fusion(bf16[1024,1152]{1,0:T(8,128)(2,1)S(1)} %bitcast.150, bf16[1152,4608]{1,0:T(8,128)(2,1)} %all-gather.11.cloned.1.call-done), kind=kOutput, calls=%fused_computation.187 | convolution fusion | flops 10871635968 | bytes 31850496 | tf_op jit(solution)/shard_map/dot_general | solution.py:36
  249.8 21.2 %convolution_convert_fusion.1 = bf16[4608,1152]{1,0:T(8,128)(2,1)} fusion(bf16[1024,1152]{1,0:T(8,128)(2,1)S(1)} %bitcast.153, f32[1024,4608]{1,0:T(8,128)} %fusion.88), kind=kOutput, calls=%fused_computation.3 | convolution fusion | flops 10919411712 | bytes 31850496 | tf_op jit(solution)/shard_map/dot_general | solution.py:36
  271.1 33.3 %all-gather.13.cloned.1.call-done = bf16[4608,1152]{1,0:T(8,128)(2,1)} async-done(((bf16[576,1152]{1,0:T(8,128)(2,1)}), bf16[4608,1152]{1,0:T(8,128)(2,1)}) %all-gather.13.cloned.1.call-update) | async-done | bytes 10616848 | tf_op jit(solution)/shard_map/all_gather | solution.py:269
  304.4 25.8 %fusion.8 = bf16[1024,4608]{1,0:T(8,128)(2,1)S(1)} fusion(f32[1024,4608]{1,0:T(8,128)} %fusion.88, bf16[1024,1152]{1,0:T(8,128)(2,1)} %bitcast.152, bf16[4608,1152]{1,0:T(8,128)(2,1)} %all-gather.13.cloned.1.call-done), kind=kOutput, calls=%fused_computation.12 | convolution fusion | flops 10961289216 | bytes 41287680 | tf_op jit(solution)/shard_map/dot_general | solution.py:36
  330.2 3.6 copy-done.66
  333.8 13.5 %convolution_convert_fusion = bf16[1152,4608]{1,0:T(8,128)(2,1)} fusion(bf16[1024,1152]{1,0:T(8,128)(2,1)S(1)} %bitcast.151, bf16[1024,4608]{1,0:T(8,128)(2,1)S(1)} %fusion.8), kind=kOutput, calls=%fused_computation.2 | convolution fusion | flops 10876944384 | bytes 22413312 | tf_op jit(solution)/shard_map/dot_general | solution.py:36
  348.6 19.8 %fusion.28 = (f32[1024]{0:T(1024)S(1)}, f32[1024,1152]{1,0:T(8,128)}) fusion(f32[2,1152]{1,0:T(2,128)S(1)} %copy-done.41, bf16[1024,4608]{1,0:T(8,128)(2,1)} %copy-done.66, bf16[1152,4608]{1,0:T(8,128)(2,1)} %all-gather.11.cloned.1.call-done), kind=kOutput, calls=%fused_computation.47 | convolution fusion | flops 10873994240 | bytes 24785920 | tf_op jit(solution)/shard_map/dot_general | solution.py:36
  368.4 6.8 fusion.29
  375.3 24.3 %fusion.79 = f32[1024,1152]{1,0:T(8,128)} fusion(bf16[4608,1152]{1,0:T(8,128)(2,1)} %all-gather.13.cloned.1.call-done, f32[1024,4608]{1,0:T(8,128)} %fusion.88), kind=kOutput, calls=%fused_computation.180 | convolution fusion | flops 10914103296 | bytes 34209792 | tf_op jit(solution)/shard_map/dot_general | solution.py:36
  399.7 6.4 multiply_reduce_fusion
  409.6 3.7 convolution_convert_fusion.5
  417.5 19.0 %convolution_convert_fusion.2 = bf16[1152,1152]{1,0:T(8,128)(2,1)S(1)} fusion(bf16[1024,1152]{1,0:T(8,128)(2,1)S(1)} %bitcast.149, bf16[288,512]{1,0:T(8,128)(2,1)S(1)} %copy-done.37, bf16[288,512]{1,0:T(8,128)(2,1)S(1)} %copy-done.35, bf16[288,512]{1,0:T(8,128)(2,1)S(1)} %copy-done.33, bf16[288,512]{1,0:T(8,128)(2,1)S(1)} %copy-done.31, ...), kind=kOutput, calls=%fused_computation.22 | convolution fusion | flops 2738110464 | bytes 7372800 | tf_op jit(solution)/shard_map/dot_general | solution.py:36
  439.2 2.5 collective-permute-done.9
  444.1 15.8 %all-gather = f32[8,2,4608]{2,1,0:T(2,128)S(1)} all-gather(f32[1,2,4608]{2,1,0:T(2,128)S(1)} %add_bitcast_fusion), channel_id=1, replica_groups=mesh['dp'=8,'seq'=4] {'dp'}, dimensions={0}, use_global_device_ids=true | all-gather | bytes 331776 | tf_op jit(solution)/shard_map/all_gather | solution.py:269
  461.7 1.9 pad_maximum_fusion.5
  463.6 53.7 %attend_back.2.refs_0_ = bf16[6,4,72,2048]{3,2,1,0:T(8,128)(2,1)S(1)} custom-call(bf16[24,72,2048]{2,1,0:T(8,128)(2,1)} %bitcast.121, bf16[24,72,2048]{2,1,0:T(8,128)(2,1)} %bitcast.122, bf16[24,72,2048]{2,1,0:T(8,128)(2,1)} %bitcast.123, bf16[8,72,2048]{2,1,0:T(8,128)(2,1)S(1)} %bitcast.113, f32[4,1,2048]{2,1,0:T(1,128)S(1)} %get-tuple-element.33.l_ref), custom_call_target="tpu_custom_call" | custom-call | flops 33822867456 | bytes 9437184 | tf_op jit(solution)/shard_map/attend_back/pallas_call | solution.py:199
  517.2 2.9 copy-done.1
  520.2 1.9 fusion.45
  522.0 2.8 fusion.90
  524.8 2.8 add_convert_fusion.2
  532.1 3.0 copy-done.2
  535.1 53.5 %attend_back.3 = bf16[6,4,72,2048]{3,2,1,0:T(8,128)(2,1)S(1)} custom-call(bf16[24,72,2048]{2,1,0:T(8,128)(2,1)} %bitcast.124, bf16[24,72,2048]{2,1,0:T(8,128)(2,1)} %bitcast.125, bf16[24,72,2048]{2,1,0:T(8,128)(2,1)} %bitcast.126, bf16[8,72,2048]{2,1,0:T(8,128)(2,1)S(1)} %bitcast.114, ...), custom_call_target="tpu_custom_call", output_to_operand_aliasing={{}: (5, {})} | custom-call | flops 33822867456 | bytes 9437184 | tf_op jit(solution)/shard_map/attend_back/pallas_call | solution.py:199
  588.6 2.8 copy-done.3
  595.7 15.9 %convolution_convert_fusion.4 = bf16[1152,1728]{1,0:T(8,128)(2,1)} fusion(bf16[1728,2048]{1,0:T(8,128)(2,1)} %bitcast.127, f32[1152]{0:T(1024)S(1)} %copy-done.62, f32[1152]{0:T(1024)S(1)} %copy-done.61, f32[2048]{0:T(1024)S(1)} %copy-done.63, f32[2048]{0:T(1024)S(1)} %copy-done.58, bf16[512,1152]{1,0:T(8,128)(2,1)} %collective-permute-done.2, ...), kind=kOutput, calls=%fused_computation.24 | convolution fusion | flops 8186388480 | bytes 15803392 | tf_op jit(solution)/shard_map/dot_general | solution.py:36
  611.7 5.7 convolution_convert_fusion.6
  619.7 2.6 convolution_convert_fusion.7
  623.9 35.3 %collective-permute-done.25 = bf16[144,1152]{1,0:T(8,128)(2,1)S(1)} collective-permute-done((bf16[144,1152]{1,0:T(8,128)(2,1)S(1)}, bf16[144,1152]{1,0:T(8,128)(2,1)S(1)}, u32[]{:S(2)}, u32[]{:S(2)}) %collective-permute-start.25) | collective-permute-done | bytes 331808 | tf_op jit(solution)/shard_map/ppermute | solution.py:241
  660.2 2.7 add_convert_fusion.3
  663.5 3.7 convert_add_fusion.2
  667.2 13.7 %collective-permute-done.17 = bf16[512,1152]{1,0:T(8,128)(2,1)S(1)} collective-permute-done((bf16[512,1152]{1,0:T(8,128)(2,1)S(1)}, bf16[512,1152]{1,0:T(8,128)(2,1)S(1)}, u32[]{:S(2)}, u32[]{:S(2)}) %collective-permute-start.17) | collective-permute-done | bytes 1179680 | tf_op jit(solution)/shard_map/ppermute | solution.py:241
  680.9 2.9 collective-permute-done.19
  683.8 2.7 fusion.30
  686.6 2.2 fusion.24
  689.5 3.1 collective-permute-done.20
  693.8 3.4 fusion.23
  697.2 16.8 %all-gather.1 = f32[8,2,2304]{2,1,0:T(2,128)S(1)} all-gather(f32[1,2,2304]{2,1,0:T(2,128)S(1)} %add_bitcast_fusion.1), channel_id=1, replica_groups=mesh['dp'=8,'seq'=4] {'dp'}, dimensions={0}, use_global_device_ids=true | all-gather | bytes 165888 | tf_op jit(solution)/shard_map/all_gather | solution.py:269
  716.5 3.7 all-to-all-start.2
  720.9 8.2 %collective-permute-done.22 = bf16[144,1728]{1,0:T(8,128)(2,1)} collective-permute-done((bf16[144,1728]{1,0:T(8,128)(2,1)}, bf16[144,1728]{1,0:T(8,128)(2,1)}, u32[]{:S(2)}, u32[]{:S(2)}) %collective-permute-start.22) | collective-permute-done | bytes 497696 | tf_op jit(solution)/shard_map/ppermute | solution.py:233
  731.9 2.2 pad_maximum_fusion.2
  734.8 8.9 %collective-permute-done.23 = bf16[144,1728]{1,0:T(8,128)(2,1)} collective-permute-done((bf16[144,1728]{1,0:T(8,128)(2,1)S(1)}, bf16[144,1728]{1,0:T(8,128)(2,1)}, u32[]{:S(2)}, u32[]{:S(2)}) %collective-permute-start.23) | collective-permute-done | bytes 497696 | tf_op jit(solution)/shard_map/ppermute | solution.py:241
  745.3 1.8 reshape.186
  747.1 1.9 fusion.81
  (296 shorter events, 71.2 us)
Async XLA Ops:
  7.2 88.9 %all-gather.9.cloned.1.call-start = ((), (), s32[]{:S(2)}) async-start(), calls=%async_computation.8 | async-start | bytes 2985984 | tf_op jit(solution)/shard_map/all_gather | solution.py:269
  7.9 95.2 %all-gather.7.cloned.1.call-start = ((), (), s32[]{:S(2)}) async-start(), calls=%async_computation.7 | async-start | bytes 4644864 | tf_op jit(solution)/shard_map/all_gather | solution.py:269
  10.8 220.0 %all-gather.11.cloned.1.call-start = ((), (), s32[]{:S(2)}) async-start(), calls=%async_computation.9 | async-start | bytes 11943936 | tf_op jit(solution)/shard_map/all_gather | solution.py:269
  12.7 90.4 %copy-start.9 = (bf16[512,1152]{1,0:T(8,128)(2,1)}, bf16[512,1152]{1,0:T(8,128)(2,1)S(1)}, u32[]{:S(2)}) copy-start(bf16[512,1152]{1,0:T(8,128)(2,1)S(1)} %get-tuple-element.68) | copy-start | bytes 3538948
  12.7 29.2 %collective-permute-start = (bf16[512,1152]{1,0:T(8,128)(2,1)}, bf16[512,1152]{1,0:T(8,128)(2,1)}, u32[]{:S(2)}, u32[]{:S(2)}) collective-permute-start(bf16[512,1152]{1,0:T(8,128)(2,1)} %get-tuple-element.69), channel_id=1, source_target_pairs={{0,1},{1,0},{2,3},{3,2},{4,5},{5,4},{6,7},{7,6},{8,9},{9,8},{10,11... | collective-permute-start | bytes 3538952 | tf_op jit(solution)/shard_map/ppermute | solution.py:233
  29.8 25.0 %all-to-all-start.1 = ((f32[8,2,6912]{2,1,0:T(2,128)}), f32[8,2,6912]{2,1,0:T(2,128)}, u32[]{:S(2)}, u32[]{:S(2)}) async-start(f32[8,2,6912]{2,1,0:T(2,128)} %copy.142), calls=%async_computation.1 | async-start | bytes 884736 | tf_op jit(solution)/shard_map/all_to_all | solution.py:298
  33.9 270.5 %all-gather.13.cloned.1.call-start = ((), (), s32[]{:S(2)}) async-start(), calls=%async_computation.10 | async-start | bytes 11943936 | tf_op jit(solution)/shard_map/all_gather | solution.py:269
  34.0 29.0 %collective-permute-start.1 = (bf16[512,1152]{1,0:T(8,128)(2,1)S(1)}, bf16[512,1152]{1,0:T(8,128)(2,1)}, u32[]{:S(2)}, u32[]{:S(2)}) collective-permute-start(bf16[512,1152]{1,0:T(8,128)(2,1)S(1)} %get-tuple-element.68), channel_id=1, source_target_pairs={{0,2},{1,3},{2,0},{3,1},{4,6},{5,7},{6,4},{7,5},{8,10},{9,11},{10,... | collective-permute-start | bytes 3538952 | tf_op jit(solution)/shard_map/ppermute | solution.py:241
  42.0 45.6 %collective-permute-start.2 = (bf16[512,1152]{1,0:T(8,128)(2,1)}, bf16[512,1152]{1,0:T(8,128)(2,1)}, u32[]{:S(2)}, u32[]{:S(2)}) collective-permute-start(bf16[512,1152]{1,0:T(8,128)(2,1)} %collective-permute-done), channel_id=1, source_target_pairs={{0,2},{1,3},{2,0},{3,1},{4,6},{5,7},{6,4},{7,5},{8,10},{9,11},{10,... | collective-permute-start | bytes 3538952 | tf_op jit(solution)/shard_map/ppermute | solution.py:241
  43.8 416.4 %reduce-scatter.5.cloned.1.call-start = ((), (), s32[]{:S(2)}) async-start(), calls=%async_computation.11 | async-start | bytes 11943936 | tf_op jit(solution)/shard_map/reduce_scatter | solution.py:273
  44.5 171.3 %copy-start.51 = (f32[2,512]{1,0:T(2,128)}, f32[2,512]{1,0:T(2,128)S(1)}, u32[]{:S(2)}) copy-start(f32[2,512]{1,0:T(2,128)S(1)} %broadcast_multiply_fusion.3) | copy-start | bytes 12292
  59.4 166.3 %copy-start.40 = (f32[2,1152]{1,0:T(2,128)}, f32[2,1152]{1,0:T(2,128)S(1)}, u32[]{:S(2)}) copy-start(f32[2,1152]{1,0:T(2,128)S(1)} %get-tuple-element.108) | copy-start | bytes 27652
  117.6 28.8 %copy-start = (bf16[1728,2048]{1,0:T(8,128)(2,1)}, bf16[1728,2048]{1,0:T(8,128)(2,1)S(1)}, u32[]{:S(2)}) copy-start(bf16[1728,2048]{1,0:T(8,128)(2,1)S(1)} %convolution_convert_fusion.3) | copy-start | bytes 21233668
  143.4 33.8 %collective-permute-start.3 = (bf16[288,512]{1,0:T(8,128)(2,1)S(1)}, bf16[288,512]{1,0:T(8,128)(2,1)S(1)}, u32[]{:S(2)}, u32[]{:S(2)}) collective-permute-start(bf16[288,512]{1,0:T(8,128)(2,1)S(1)} %slice.187), channel_id=1, source_target_pairs={{0,1},{1,0},{2,3},{3,2},{4,5},{5,4},{6,7},{7,6},{8,9},{9,8},{10,11... | collective-permute-start | bytes 884744 | tf_op jit(solution)/shard_map/ppermute | solution.py:233
  144.9 28.9 %copy-start.14 = (bf16[1,576,1152]{2,1,0:T(8,128)(2,1)S(1)}, bf16[1,576,1152]{2,1,0:T(8,128)(2,1)}, u32[]{:S(2)}) copy-start(bf16[1,576,1152]{2,1,0:T(8,128)(2,1)} %get-tuple-element.62) | copy-start | bytes 3981316
  144.9 28.9 %copy-start.15 = (bf16[1,576,1152]{2,1,0:T(8,128)(2,1)S(1)}, bf16[1,576,1152]{2,1,0:T(8,128)(2,1)}, u32[]{:S(2)}) copy-start(bf16[1,576,1152]{2,1,0:T(8,128)(2,1)} %get-tuple-element.63) | copy-start | bytes 3981316
  144.9 30.7 %collective-permute-start.5 = (bf16[288,1024]{1,0:T(8,128)(2,1)S(1)}, bf16[288,1024]{1,0:T(8,128)(2,1)S(1)}, u32[]{:S(2)}, u32[]{:S(2)}) collective-permute-start(bf16[288,1024]{1,0:T(8,128)(2,1)S(1)} %bitcast.161), channel_id=1, source_target_pairs={{0,2},{1,3},{2,0},{3,1},{4,6},{5,7},{6,4},{7,5},{8,10},{9,11},{10,... | collective-permute-start | bytes 1769480 | tf_op jit(solution)/shard_map/ppermute | solution.py:241
  172.7 16.8 %collective-permute-start.4 = (bf16[288,512]{1,0:T(8,128)(2,1)S(1)}, bf16[288,512]{1,0:T(8,128)(2,1)S(1)}, u32[]{:S(2)}, u32[]{:S(2)}) collective-permute-start(bf16[288,512]{1,0:T(8,128)(2,1)S(1)} %slice.189), channel_id=1, source_target_pairs={{0,1},{1,0},{2,3},{3,2},{4,5},{5,4},{6,7},{7,6},{8,9},{9,8},{10,11... | collective-permute-start | bytes 884744 | tf_op jit(solution)/shard_map/ppermute | solution.py:233
  173.3 14.6 %collective-permute-start.7 = (bf16[288,1024]{1,0:T(8,128)(2,1)S(1)}, bf16[288,1024]{1,0:T(8,128)(2,1)S(1)}, u32[]{:S(2)}, u32[]{:S(2)}) collective-permute-start(bf16[288,1024]{1,0:T(8,128)(2,1)S(1)} %bitcast.160), channel_id=1, source_target_pairs={{0,2},{1,3},{2,0},{3,1},{4,6},{5,7},{6,4},{7,5},{8,10},{9,11},{10,... | collective-permute-start | bytes 1769480 | tf_op jit(solution)/shard_map/ppermute | solution.py:241
  175.6 13.9 %collective-permute-start.6 = (bf16[288,512]{1,0:T(8,128)(2,1)S(1)}, bf16[288,512]{1,0:T(8,128)(2,1)S(1)}, u32[]{:S(2)}, u32[]{:S(2)}) collective-permute-start(bf16[288,512]{1,0:T(8,128)(2,1)S(1)} %slice.191), channel_id=1, source_target_pairs={{0,1},{1,0},{2,3},{3,2},{4,5},{5,4},{6,7},{7,6},{8,9},{9,8},{10,11... | collective-permute-start | bytes 884744 | tf_op jit(solution)/shard_map/ppermute | solution.py:233
  177.2 18.4 %copy-start.22 = (bf16[288,512]{1,0:T(8,128)(2,1)}, bf16[288,512]{1,0:T(8,128)(2,1)S(1)}, u32[]{:S(2)}) copy-start(bf16[288,512]{1,0:T(8,128)(2,1)S(1)} %get-tuple-element.98) | copy-start | bytes 884740
  187.9 7.6 %collective-permute-start.8 = (bf16[288,512]{1,0:T(8,128)(2,1)S(1)}, bf16[288,512]{1,0:T(8,128)(2,1)S(1)}, u32[]{:S(2)}, u32[]{:S(2)}) collective-permute-start(bf16[288,512]{1,0:T(8,128)(2,1)S(1)} %slice.193), channel_id=1, source_target_pairs={{0,1},{1,0},{2,3},{3,2},{4,5},{5,4},{6,7},{7,6},{8,9},{9,8},{10,11... | collective-permute-start | bytes 884744 | tf_op jit(solution)/shard_map/ppermute | solution.py:233
  196.4 19.4 %copy-start.55 = (f32[2,1152]{1,0:T(2,128)S(1)}, f32[2,1152]{1,0:T(2,128)}, u32[]{:S(2)}) copy-start(f32[2,1152]{1,0:T(2,128)} %get-tuple-element.110) | copy-start | bytes 27652
  230.8 19.0 %copy-start.18 = (bf16[2,512,1152]{2,1,0:T(8,128)(2,1)S(1)}, bf16[2,512,1152]{2,1,0:T(8,128)(2,1)}, u32[]{:S(2)}) copy-start(bf16[2,512,1152]{2,1,0:T(8,128)(2,1)} %get-tuple-element.114) | copy-start | bytes 7077892
  271.0 258.1 %reduce-scatter.7.cloned.1.call-start = ((), (), s32[]{:S(2)}) async-start(), calls=%async_computation.12 | async-start | bytes 11943936 | tf_op jit(solution)/shard_map/reduce_scatter | solution.py:273
  347.3 247.3 %reduce-scatter.9.cloned.1.call-start = ((), (), s32[]{:S(2)}) async-start(), calls=%async_computation.13 | async-start | bytes 2985984 | tf_op jit(solution)/shard_map/reduce_scatter | solution.py:273
  348.6 19.8 %copy-start.43 = (f32[2,512]{1,0:T(2,128)S(1)}, f32[2,512]{1,0:T(2,128)}, u32[]{:S(2)}) copy-start(f32[2,512]{1,0:T(2,128)} %copy-done.42) | copy-start | bytes 12292
  348.6 19.8 %copy-start.50 = (f32[2,512]{1,0:T(2,128)S(1)}, f32[2,512]{1,0:T(2,128)}, u32[]{:S(2)}) copy-start(f32[2,512]{1,0:T(2,128)} %copy-done.49) | copy-start | bytes 12292
  368.4 31.2 %slice-start.2 = ((s8[4718592]{0:T(1024)(128)(4,1)}), s8[4194304]{0:T(1024)(128)(4,1)S(1)}, s32[]{:S(2)}) async-start(s8[4718592]{0:T(1024)(128)(4,1)} %bitcast.134), calls=%async_computation.17 | async-start | bytes 8388608
  368.4 31.2 %slice-start.6 = ((s8[4718592]{0:T(1024)(128)(4,1)}), s8[4194304]{0:T(1024)(128)(4,1)S(1)}, s32[]{:S(2)}) async-start(s8[4718592]{0:T(1024)(128)(4,1)} %bitcast.139), calls=%async_computation.21 | async-start | bytes 8388608
  368.4 31.2 %slice-start.8 = ((s8[4718592]{0:T(1024)(128)(4,1)}), s8[4194304]{0:T(1024)(128)(4,1)S(1)}, s32[]{:S(2)}) async-start(s8[4718592]{0:T(1024)(128)(4,1)} %bitcast.142), calls=%async_computation.23 | async-start | bytes 8388608
  375.2 24.4 %slice-start.3 = ((s8[4718592]{0:T(1024)(128)(4,1)}), s8[524288]{0:T(1024)(128)(4,1)S(1)}, s32[]{:S(2)}) async-start(s8[4718592]{0:T(1024)(128)(4,1)} %bitcast.134), calls=%async_computation.18 | async-start | bytes 1048576
  375.2 24.4 %slice-start.7 = ((s8[4718592]{0:T(1024)(128)(4,1)}), s8[524288]{0:T(1024)(128)(4,1)S(1)}, s32[]{:S(2)}) async-start(s8[4718592]{0:T(1024)(128)(4,1)} %bitcast.139), calls=%async_computation.22 | async-start | bytes 1048576
  375.2 24.4 %copy-start.13 = (bf16[2,512,1152]{2,1,0:T(8,128)(2,1)S(1)}, bf16[2,512,1152]{2,1,0:T(8,128)(2,1)}, u32[]{:S(2)}) copy-start(bf16[2,512,1152]{2,1,0:T(8,128)(2,1)} %param.15) | copy-start | bytes 7077892
  375.3 24.4 %slice-start.9 = ((s8[4718592]{0:T(1024)(128)(4,1)}), s8[524288]{0:T(1024)(128)(4,1)S(1)}, s32[]{:S(2)}) async-start(s8[4718592]{0:T(1024)(128)(4,1)} %bitcast.142), calls=%async_computation.24 | async-start | bytes 1048576
  375.3 24.4 %copy-start.46 = (f32[2,1152]{1,0:T(2,128)S(1)}, f32[2,1152]{1,0:T(2,128)}, u32[]{:S(2)}) copy-start(f32[2,1152]{1,0:T(2,128)} %get-tuple-element.107) | copy-start | bytes 27652
  406.2 32.4 %collective-permute-start.12 = (f32[2,4608]{1,0:T(2,128)S(1)}, f32[2,4608]{1,0:T(2,128)S(1)}, u32[]{:S(2)}, u32[]{:S(2)}) collective-permute-start(f32[2,4608]{1,0:T(2,128)S(1)} %pad_maximum_fusion.7), channel_id=1, source_target_pairs={{0,1},{1,0},{2,3},{3,2},{4,5},{5,4},{6,7},{7,6},{8,9},{9,8},{10,11... | collective-permute-start | bytes 110600 | tf_op jit(solution)/shard_map/ppermute | solution.py:233
  413.6 28.1 %collective-permute-start.9 = (bf16[1152,512]{1,0:T(8,128)(2,1)S(1)}, bf16[1152,512]{1,0:T(8,128)(2,1)S(1)}, u32[]{:S(2)}, u32[]{:S(2)}) collective-permute-start(bf16[1152,512]{1,0:T(8,128)(2,1)S(1)} %get-tuple-element.66), channel_id=1, source_target_pairs={{0,1},{1,0},{2,3},{3,2},{4,5},{5,4},{6,7},{7,6},{8,9},{9,8},{10,11... | collective-permute-start | bytes 3538952 | tf_op jit(solution)/shard_map/ppermute | solution.py:233
  416.0 44.1 %collective-permute-start.11 = (bf16[576,512]{1,0:T(8,128)(2,1)S(1)}, bf16[576,512]{1,0:T(8,128)(2,1)S(1)}, u32[]{:S(2)}, u32[]{:S(2)}) collective-permute-start(bf16[576,512]{1,0:T(8,128)(2,1)S(1)} %get-tuple-element.83), channel_id=1, source_target_pairs={{0,2},{1,3},{2,0},{3,1},{4,6},{5,7},{6,4},{7,5},{8,10},{9,11},{10,... | collective-permute-start | bytes 1769480 | tf_op jit(solution)/shard_map/ppermute | solution.py:241
  438.6 5.5 collective-permute-start.13
  442.6 17.5 %collective-permute-start.10 = (bf16[576,512]{1,0:T(8,128)(2,1)S(1)}, bf16[576,512]{1,0:T(8,128)(2,1)S(1)}, u32[]{:S(2)}, u32[]{:S(2)}) collective-permute-start(bf16[576,512]{1,0:T(8,128)(2,1)S(1)} %get-tuple-element.85), channel_id=1, source_target_pairs={{0,2},{1,3},{2,0},{3,1},{4,6},{5,7},{6,4},{7,5},{8,10},{9,11},{10,... | collective-permute-start | bytes 1769480 | tf_op jit(solution)/shard_map/ppermute | solution.py:241
  460.2 64.6 %collective-permute-start.14 = (bf16[576,1152]{1,0:T(8,128)(2,1)}, bf16[576,1152]{1,0:T(8,128)(2,1)}, u32[]{:S(2)}, u32[]{:S(2)}) collective-permute-start(bf16[576,1152]{1,0:T(8,128)(2,1)} %reduce-scatter.5.cloned.1.call-done), channel_id=1, source_target_pairs={{0,1},{1,0},{2,3},{3,2},{4,5},{5,4},{6,7},{7,6},{8,9},{9,8},{10,11... | collective-permute-start | bytes 3981320 | tf_op jit(solution)/shard_map/ppermute | solution.py:233
  520.1 194.6 %reduce-scatter.11.cloned.1.call-start = ((), (), s32[]{:S(2)}) async-start(), calls=%async_computation.14 | async-start | bytes 4644864 | tf_op jit(solution)/shard_map/reduce_scatter | solution.py:273
  529.1 64.1 %collective-permute-start.16 = (bf16[144,4608]{1,0:T(8,128)(2,1)}, bf16[144,4608]{1,0:T(8,128)(2,1)S(1)}, u32[]{:S(2)}, u32[]{:S(2)}) collective-permute-start(bf16[144,4608]{1,0:T(8,128)(2,1)} %reduce-scatter.7.cloned.1.call-done), channel_id=1, source_target_pairs={{0,1},{1,0},{2,3},{3,2},{4,5},{5,4},{6,7},{7,6},{8,9},{9,8},{10,11... | collective-permute-start | bytes 3981320 | tf_op jit(solution)/shard_map/ppermute | solution.py:233
  530.6 60.9 %collective-permute-start.15 = (bf16[576,1152]{1,0:T(8,128)(2,1)}, bf16[576,1152]{1,0:T(8,128)(2,1)S(1)}, u32[]{:S(2)}, u32[]{:S(2)}) collective-permute-start(bf16[576,1152]{1,0:T(8,128)(2,1)} %add_convert_fusion.2), channel_id=1, source_target_pairs={{0,2},{1,3},{2,0},{3,1},{4,6},{5,7},{6,4},{7,5},{8,10},{9,11},{10,... | collective-permute-start | bytes 3981320 | tf_op jit(solution)/shard_map/ppermute | solution.py:241
  535.1 56.4 %copy-start.16 = (bf16[576,1152]{1,0:T(8,128)(2,1)S(1)}, bf16[576,1152]{1,0:T(8,128)(2,1)}, u32[]{:S(2)}) copy-start(bf16[576,1152]{1,0:T(8,128)(2,1)} %add_convert_fusion.2) | copy-start | bytes 3981316
  594.6 68.9 %collective-permute-start.26 = (bf16[144,4608]{1,0:T(8,128)(2,1)}, bf16[144,4608]{1,0:T(8,128)(2,1)}, u32[]{:S(2)}, u32[]{:S(2)}) collective-permute-start(bf16[144,4608]{1,0:T(8,128)(2,1)} %add_convert_fusion.1), channel_id=1, source_target_pairs={{0,2},{1,3},{2,0},{3,1},{4,6},{5,7},{6,4},{7,5},{8,10},{9,11},{10,... | collective-permute-start | bytes 3981320 | tf_op jit(solution)/shard_map/ppermute | solution.py:241
  595.1 23.8 %collective-permute-start.24 = (bf16[144,1152]{1,0:T(8,128)(2,1)}, bf16[144,1152]{1,0:T(8,128)(2,1)S(1)}, u32[]{:S(2)}, u32[]{:S(2)}) collective-permute-start(bf16[144,1152]{1,0:T(8,128)(2,1)} %reduce-scatter.9.cloned.1.call-done), channel_id=1, source_target_pairs={{0,1},{1,0},{2,3},{3,2},{4,5},{5,4},{6,7},{7,6},{8,9},{9,8},{10,11... | collective-permute-start | bytes 995336 | tf_op jit(solution)/shard_map/ppermute | solution.py:233
  617.4 42.8 %collective-permute-start.18 = (bf16[512,1152]{1,0:T(8,128)(2,1)S(1)}, bf16[512,1152]{1,0:T(8,128)(2,1)S(1)}, u32[]{:S(2)}, u32[]{:S(2)}) collective-permute-start(bf16[512,1152]{1,0:T(8,128)(2,1)S(1)} %convolution_convert_fusion.6), channel_id=1, source_target_pairs={{0,2},{1,3},{2,0},{3,1},{4,6},{5,7},{6,4},{7,5},{8,10},{9,11},{10,... | collective-permute-start | bytes 3538952 | tf_op jit(solution)/shard_map/ppermute | solution.py:241
  619.0 40.1 %collective-permute-start.25 = (bf16[144,1152]{1,0:T(8,128)(2,1)S(1)}, bf16[144,1152]{1,0:T(8,128)(2,1)S(1)}, u32[]{:S(2)}, u32[]{:S(2)}) collective-permute-start(bf16[144,1152]{1,0:T(8,128)(2,1)S(1)} %fusion.55), channel_id=1, source_target_pairs={{0,2},{1,3},{2,0},{3,1},{4,6},{5,7},{6,4},{7,5},{8,10},{9,11},{10,... | collective-permute-start | bytes 995336 | tf_op jit(solution)/shard_map/ppermute | solution.py:241
  622.3 58.6 %collective-permute-start.17 = (bf16[512,1152]{1,0:T(8,128)(2,1)S(1)}, bf16[512,1152]{1,0:T(8,128)(2,1)S(1)}, u32[]{:S(2)}, u32[]{:S(2)}) collective-permute-start(bf16[512,1152]{1,0:T(8,128)(2,1)S(1)} %convolution_convert_fusion.7), channel_id=1, source_target_pairs={{0,2},{1,3},{2,0},{3,1},{4,6},{5,7},{6,4},{7,5},{8,10},{9,11},{10,... | collective-permute-start | bytes 3538952 | tf_op jit(solution)/shard_map/ppermute | solution.py:241
  662.8 21.0 %collective-permute-start.19 = (bf16[512,1152]{1,0:T(8,128)(2,1)S(1)}, bf16[512,1152]{1,0:T(8,128)(2,1)S(1)}, u32[]{:S(2)}, u32[]{:S(2)}) collective-permute-start(bf16[512,1152]{1,0:T(8,128)(2,1)S(1)} %add_convert_fusion.3), channel_id=1, source_target_pairs={{0,1},{1,0},{2,3},{3,2},{4,5},{5,4},{6,7},{7,6},{8,9},{9,8},{10,11... | collective-permute-start | bytes 3538952 | tf_op jit(solution)/shard_map/ppermute | solution.py:233
  663.5 30.3 %slice-start.4 = ((s8[4718592]{0:T(1024)(128)(4,1)}), s8[4194304]{0:T(1024)(128)(4,1)S(1)}, s32[]{:S(2)}) async-start(s8[4718592]{0:T(1024)(128)(4,1)} %bitcast.136), calls=%async_computation.19 | async-start | bytes 8388608
  667.2 19.4 %copy-start.7 = (bf16[2,512,1152]{2,1,0:T(8,128)(2,1)S(1)}, bf16[2,512,1152]{2,1,0:T(8,128)(2,1)}, u32[]{:S(2)}) copy-start(bf16[2,512,1152]{2,1,0:T(8,128)(2,1)} %param.8) | copy-start | bytes 7077892
  667.2 19.4 %copy-start.44 = (f32[2,1152]{1,0:T(2,128)S(1)}, f32[2,1152]{1,0:T(2,128)}, u32[]{:S(2)}) copy-start(f32[2,1152]{1,0:T(2,128)} %get-tuple-element.106) | copy-start | bytes 27652
  667.2 19.4 %copy-start.52 = (f32[2,512]{1,0:T(2,128)S(1)}, f32[2,512]{1,0:T(2,128)}, u32[]{:S(2)}) copy-start(f32[2,512]{1,0:T(2,128)} %copy-done.51) | copy-start | bytes 12292
  667.2 19.4 %copy-start.53 = (f32[2,512]{1,0:T(2,128)S(1)}, f32[2,512]{1,0:T(2,128)}, u32[]{:S(2)}) copy-start(f32[2,512]{1,0:T(2,128)} %add_rsqrt_fusion.1) | copy-start | bytes 12292
  667.2 26.6 %slice-start.5 = ((s8[4718592]{0:T(1024)(128)(4,1)}), s8[524288]{0:T(1024)(128)(4,1)S(1)}, s32[]{:S(2)}) async-start(s8[4718592]{0:T(1024)(128)(4,1)} %bitcast.136), calls=%async_computation.20 | async-start | bytes 1048576
  688.8 3.8 collective-permute-start.20
  692.7 21.5 %copy-start.8 = (bf16[144,6912]{1,0:T(8,128)(2,1)S(1)}, bf16[144,6912]{1,0:T(8,128)(2,1)}, u32[]{:S(2)}) copy-start(bf16[144,6912]{1,0:T(8,128)(2,1)} %param.10) | copy-start | bytes 5971972
  692.7 4.5 collective-permute-start.21
  714.7 14.4 %collective-permute-start.22 = (bf16[144,1728]{1,0:T(8,128)(2,1)}, bf16[144,1728]{1,0:T(8,128)(2,1)}, u32[]{:S(2)}, u32[]{:S(2)}) collective-permute-start(bf16[144,1728]{1,0:T(8,128)(2,1)} %reduce-scatter.11.cloned.1.call-done), channel_id=1, source_target_pairs={{0,1},{1,0},{2,3},{3,2},{4,5},{5,4},{6,7},{7,6},{8,9},{9,8},{10,11... | collective-permute-start | bytes 1493000 | tf_op jit(solution)/shard_map/ppermute | solution.py:233
  716.5 17.6 %all-to-all-start.2 = ((f32[8,2,144]{2,1,0:T(2,128)}), f32[8,2,144]{2,1,0:T(2,128)S(1)}, u32[]{:S(2)}, u32[]{:S(2)}) async-start(f32[8,2,144]{2,1,0:T(2,128)} %all_to_all.15), calls=%async_computation.5 | async-start | bytes 32768 | tf_op jit(solution)/shard_map/all_to_all | solution.py:473
  730.4 13.3 %collective-permute-start.23 = (bf16[144,1728]{1,0:T(8,128)(2,1)S(1)}, bf16[144,1728]{1,0:T(8,128)(2,1)}, u32[]{:S(2)}, u32[]{:S(2)}) collective-permute-start(bf16[144,1728]{1,0:T(8,128)(2,1)S(1)} %add_convert_fusion.4), channel_id=1, source_target_pairs={{0,2},{1,3},{2,0},{3,1},{4,6},{5,7},{6,4},{7,5},{8,10},{9,11},{10,... | collective-permute-start | bytes 1493000 | tf_op jit(solution)/shard_map/ppermute | solution.py:241
  (50 other events, 240.3 us)
Sparse Core Ops, SparseCore 0:
  9.6 45.5 all-gather.8
  57.4 45.6 all-gather.6
  104.8 99.2 all-gather.10
  205.6 98.7 all-gather.12
  306.6 108.8 reduce-scatter.4
  417.7 111.4 reduce-scatter.6
  532.0 36.4 reduce-scatter.8
  611.8 47.7 reduce-scatter.10
